TPU v7x, 256 devices: a whole 4x4x8 slice. The times are simulated.
256 devices in a mesh: px: 16 (over z, core), py: 16 (over x, y).
Axes of the slice: x: 4, y: 4, z: 8, core: 2. Of those that a mesh axis runs over, the one named last changes fastest.
Arguments:
- right_side: float32 [64, 128, 1024], P('px', 'py'), may hold values from -40 to 40
- diagonal: float32 [64, 128, 1024], P('px', 'py'), may hold values from 0.05 to 3
- aggregate_id: int32 [64, 128, 1024], P('px', 'py'), may hold values from 0 to 511, as said below
- coarse_diag: float32 [32, 32, 128], P('px', 'py'), may hold values from 150 to 230
- coarse_link: float32 [3, 32, 32, 128], P(None, 'px', 'py'), may hold values from 0.75 to 1.25
Outputs:
- solution_field: float32 [64, 128, 1024], P('px', 'py')
- residual: float32 [64, 128, 1024], P('px', 'py')
Inputs may be any that keep to these rules, and one draw needn't show every extreme that they name: `aggregate_id`: the cell (x, y, z) names the aggregate ((x % 4) // 2) * 2 * 128 + ((y % 8) // 4) * 128 + k of its own partition, where k differs from z // 8 by at most one; every aggregate of every partition holds cells.
All inputs are finite; a program needn't handle non-finite values.
Results may differ from a plain program's by a relative error of at most 0.0003.
Values sent between devices are 32-bit elements; how exact they have to be, the bound alone decides.
No kernel may reach another device: no remote copies, remote signals or barrier semaphores. Data moves between devices by JAX's collectives and lax.ppermute only.
A program may use at most 64 MiB of HBM per device.

v0:
```python
import jax
import jax.numpy as jnp
from jax import lax
from jax.sharding import Mesh
from jax.sharding import PartitionSpec as P

ITERS = 4
PX_PY = ("px_0", "px_1", "py_0", "py_1")
PX = ("px_0", "px_1")
PY = ("py_0", "py_1")


OMEGA = 2.0 / 3.0
FACES = (32.0, 16.0, 8.0)


def padded_2(value, sides, width):
    edges = {}
    for axis, dim in sides:
        peers, length = (lax.axis_size(axis), value.shape[dim])
        up = [(i, (i + 1) % peers) for i in range(peers - 1)]
        last = lax.slice_in_dim(value, length - width, length, axis=dim)
        first = lax.slice_in_dim(value, 0, width, axis=dim)
        edges[dim] = (
            lax.ppermute(last, axis, up),
            lax.ppermute(first, axis, [(b, a) for a, b in up]),
        )
    done = []
    for _, dim in sides:
        low, high = edges[dim]
        around = [(width, width) if d in done else (0, 0) for d in range(value.ndim)]
        value = jnp.concatenate([jnp.pad(low, around), value, jnp.pad(high, around)], axis=dim)
        done.append(dim)
    return value


def with_halo(cells, sides, width):
    for axis, dim in sides:
        count = lax.axis_size(axis)
        ends = count - 1
        head = lax.slice_in_dim(cells, 0, width, axis=dim)
        tail = lax.slice_in_dim(cells, cells.shape[dim] - width, cells.shape[dim], axis=dim)
        cells = jnp.concatenate(
            [
                lax.ppermute(tail, axis, [(i, (i + 1) % count) for i in range(ends)]),
                cells,
                lax.ppermute(head, axis, [((i + 1) % count, i) for i in range(ends)]),
            ],
            axis=dim,
        )
    return cells


def by_axis(value, axes):
    for axis in axes:
        value = lax.psum(value, axis)
    return value


def beside_sum(padded):
    padded = jnp.pad(padded, ((0, 0), (0, 0), (1, 1)))
    beside = padded[2:, 1:-1, 1:-1] + padded[:-2, 1:-1, 1:-1]
    beside = beside + padded[1:-1, 2:, 1:-1] + padded[1:-1, :-2, 1:-1]
    beside = beside + padded[1:-1, 1:-1, 2:] + padded[1:-1, 1:-1, :-2]
    return beside


def apply_fine(values, diagonal):
    widened = padded_2(values, ((PX, 0), (PY, 1)), 1)
    return (6.0 + diagonal) * values - beside_sum(widened)


def coarse_apply(coarse, coarse_diag, weights):
    weighted = weights * coarse[None]
    stacked = jnp.stack((coarse, weighted[0], weighted[1]), axis=0)
    widened = padded_2(stacked, ((PX, 1), (PY, 2)), 1)
    near = weights[0] * widened[0, 2:, 1:-1] + widened[1, :-2, 1:-1]
    near = near + weights[1] * widened[0, 1:-1, 2:] + widened[2, 1:-1, :-2]
    deep_c = jnp.pad(coarse, ((0, 0), (0, 0), (1, 1)))
    deep_w = jnp.pad(weighted[2], ((0, 0), (0, 0), (1, 1)))
    near = near + weights[2] * deep_c[:, :, 2:] + deep_w[:, :, :-2]
    return coarse_diag * coarse - near


def coarse_solve(coarse_rhs, coarse_diag, weights):
    estimate = coarse_rhs / coarse_diag
    for sweep_index in range(2):
        estimate = (
            estimate + (coarse_rhs - coarse_apply(estimate, coarse_diag, weights)) / coarse_diag
        )
    return estimate


def local(right_side, diagonal, aggregate_id, coarse_diag, coarse_link):
    rows_here = right_side.shape[0]
    cols_here = right_side.shape[1]
    depth_here = right_side.shape[2]
    rows_agg = coarse_diag.shape[0]
    cols_agg = coarse_diag.shape[1]
    depth_agg = coarse_diag.shape[2]
    scaling = 6.0 + diagonal
    faces = jnp.array(FACES, dtype=jnp.float32)
    weights = coarse_link * faces[:, None, None, None]
    home = lax.iota(jnp.int32, depth_here) // 8
    offset = aggregate_id % depth_agg - home[None, None, :]
    go_up = offset == 1
    go_down = offset == -1

    def box_sum(values):
        return values.reshape(rows_agg, 2, cols_agg, 4, depth_agg, 8).sum(axis=(1, 3, 5))

    def expand(coarse):
        wide = jnp.broadcast_to(
            coarse[:, None, :, None, :, None], (rows_agg, 2, cols_agg, 4, depth_agg, 8)
        )
        return wide.reshape(rows_here, cols_here, depth_here)

    def restrict(values):
        middle = box_sum(jnp.where(offset == 0, values, 0.0))
        upper = box_sum(jnp.where(go_up, values, 0.0))
        lower = box_sum(jnp.where(go_down, values, 0.0))
        middle = middle + jnp.pad(upper[:, :, :-1], ((0, 0), (0, 0), (1, 0)))
        return middle + jnp.pad(lower[:, :, 1:], ((0, 0), (0, 0), (0, 1)))

    def lift(coarse):
        above = jnp.pad(coarse[:, :, 1:], ((0, 0), (0, 0), (0, 1)))
        below = jnp.pad(coarse[:, :, :-1], ((0, 0), (0, 0), (1, 0)))
        return jnp.where(go_up, expand(above), jnp.where(go_down, expand(below), expand(coarse)))

    diag_wide = with_halo(diagonal, ((PX, 0), (PY, 1)), 2)
    scale_wide = 6.0 + diag_wide
    scale_mid = scale_wide[1:-1, 1:-1]
    row_global = lax.axis_index(PX) * rows_here + lax.iota(jnp.int32, rows_here + 2) - 1
    col_global = lax.axis_index(PY) * cols_here + lax.iota(jnp.int32, cols_here + 2) - 1
    row_inside = (row_global >= 0) & (row_global < rows_here * lax.axis_size(PX))
    col_inside = (col_global >= 0) & (col_global < cols_here * lax.axis_size(PY))
    inside = row_inside[:, None, None] & col_inside[None, :, None]

    def smooth_restrict(vector):
        widened = with_halo(vector, ((PX, 0), (PY, 1)), 2)
        smoothed_wide = OMEGA * widened / scale_wide
        middle = widened[1:-1, 1:-1] - (
            scale_mid * smoothed_wide[1:-1, 1:-1] - beside_sum(smoothed_wide)
        )
        middle = jnp.where(inside, middle, 0.0)
        shrunk = middle / scale_mid
        smoothed = smoothed_wide[2:-2, 2:-2]
        remainder = middle[1:-1, 1:-1]
        reduced = remainder - OMEGA * ((6.0 + diagonal) * shrunk[1:-1, 1:-1] - beside_sum(shrunk))
        return (smoothed, remainder, reduced)

    def precondition(vector):
        smoothed, remainder, reduced = smooth_restrict(vector)
        coarse_rhs = restrict(reduced)
        correction = coarse_solve(coarse_rhs, coarse_diag, weights)
        lifted = lift(correction)
        spread = lifted - OMEGA * apply_fine(lifted, diagonal) / scaling
        leftover = remainder - apply_fine(spread, diagonal)
        return smoothed + spread + OMEGA * leftover / scaling

    solution = jnp.zeros_like(right_side)
    residual = right_side
    shaped = precondition(residual)
    operated = apply_fine(shaped, diagonal)
    for iteration in range(ITERS):
        gamma_now, delta_now = (
            by_axis(jnp.sum(residual * shaped), PX_PY),
            by_axis(jnp.sum(operated * shaped), PX_PY),
        )
        further = iteration + 1 < ITERS
        if further:
            shaped_next = precondition(operated)
            applied_next = apply_fine(shaped_next, diagonal)
        if iteration == 0:
            alpha_now = gamma_now / delta_now
            direction = shaped
            along_dir = operated
            search_pre = shaped_next
            search_img = applied_next
        else:
            beta_now = gamma_now / gamma_old
            alpha_now = gamma_now / (delta_now - beta_now * gamma_now / alpha_old)
            direction = shaped + beta_now * direction
            along_dir = operated + beta_now * along_dir
            if further:
                search_pre = shaped_next + beta_now * search_pre
                search_img = applied_next + beta_now * search_img
        solution = solution + alpha_now * direction
        residual = residual - alpha_now * along_dir
        if further:
            shaped = shaped - alpha_now * search_pre
            operated = operated - alpha_now * search_img
        gamma_old = gamma_now
        alpha_old = alpha_now
    return (solution, residual)


def solution(mesh):
    finer = Mesh(mesh.devices.reshape(8, 2, 4, 4), ("px_0", "px_1", "py_0", "py_1"))
    in_specs = (
        P(PX, PY, None),
        P(PX, PY, None),
        P(PX, PY, None),
        P(PX, PY, None),
        P(None, PX, PY, None),
    )
    out_specs = (P(PX, PY, None), P(PX, PY, None))
    return jax.shard_map(local, mesh=finer, in_specs=in_specs, out_specs=out_specs, check_vma=False)
```

profile of v0, /device:TPU:8, one launch (start us, length us, event | category | flops | bytes accessed | tf_op | source)
XLA Modules:
  0.0 671.8 jit_solution(10432730826388933379)
XLA Ops:
  8.0 4.1 collective-permute-start.4
  53.3 5.5 collective-permute-done.8
  60.8 6.0 collective-permute-start.15
  66.9 4.0 collective-permute-start.13
  81.7 4.1 collective-permute-start.17
  87.1 6.0 collective-permute-start.19
  95.1 5.8 collective-permute-done.18
  116.0 4.3 collective-permute-start.25
  132.4 4.3 collective-permute-start.28
  138.2 5.9 collective-permute-done.29
  144.1 3.9 collective-permute-start.30
  150.3 4.1 collective-permute-done.31
  167.3 3.9 collective-permute-start.35
  175.7 4.6 collective-permute-done.32
  182.4 4.0 collective-permute-start.39
  186.4 4.0 collective-permute-start.37
  203.2 4.6 collective-permute-start.41
  209.1 6.0 collective-permute-start.43
  217.1 5.5 collective-permute-done.42
  223.1 4.4 collective-permute-start.45
  240.1 5.9 collective-permute-start.49
  253.2 26.3 %all-reduce.95 = (f32[]{:T(128)}, f32[]{:T(128)}) all-reduce(f32[]{:T(128)} %get-tuple-element.9, f32[]{:T(128)} %get-tuple-element.8), channel_id=1, replica_groups=mesh['px_0'=8,'px_1'=2,'py_0'=4,'py_1'=4] {'px_0'}, use_global_device_ids=true, to_apply=%region_4.5 | all-reduce | flops 2 | bytes 16 | tf_op jit(solution)/shard_map/psum | solution.py:56
  282.6 9.8 %all-reduce.103 = (f32[]{:T(128)}, f32[]{:T(128)}) all-reduce(f32[]{:T(128)} %get-tuple-element.40, f32[]{:T(128)} %get-tuple-element.41), channel_id=1, replica_groups=mesh['px_0'=8,'px_1'=2,'py_0'=4,'py_1'=4] {'py_0'}, use_global_device_ids=true, to_apply=%region_6.7 | all-reduce | flops 2 | bytes 16 | tf_op jit(solution)/shard_map/psum | solution.py:56
  292.4 12.4 %all-reduce.99 = (f32[]{:T(128)}, f32[]{:T(128)}) all-reduce(f32[]{:T(128)} %get-tuple-element.32, f32[]{:T(128)} %get-tuple-element.33), channel_id=1, replica_groups=mesh['px_0'=8,'px_1'=2,'py_0'=4,'py_1'=4] {'py_1'}, use_global_device_ids=true, to_apply=%region_7.8 | all-reduce | flops 2 | bytes 16 | tf_op jit(solution)/shard_map/psum | solution.py:56
  310.6 4.1 collective-permute-done.53
  316.7 4.1 collective-permute-start.55
  333.9 3.9 collective-permute-start.58
  355.2 4.0 collective-permute-start.61
  371.3 4.1 collective-permute-start.65
  376.7 6.0 collective-permute-start.67
  384.7 5.8 collective-permute-done.66
  416.5 25.0 %all-reduce.94 = (f32[]{:T(128)}, f32[]{:T(128)}) all-reduce(f32[]{:T(128)} %get-tuple-element.7, f32[]{:T(128)} %get-tuple-element.6), channel_id=1, replica_groups=mesh['px_0'=8,'px_1'=2,'py_0'=4,'py_1'=4] {'px_0'}, use_global_device_ids=true, to_apply=%region_17.18 | all-reduce | flops 2 | bytes 16 | tf_op jit(solution)/shard_map/psum | solution.py:56
  444.6 8.6 %all-reduce.102 = (f32[]{:T(128)}, f32[]{:T(128)}) all-reduce(f32[]{:T(128)} %get-tuple-element.38, f32[]{:T(128)} %get-tuple-element.39), channel_id=1, replica_groups=mesh['px_0'=8,'px_1'=2,'py_0'=4,'py_1'=4] {'py_0'}, use_global_device_ids=true, to_apply=%region_19.20 | all-reduce | flops 2 | bytes 16 | tf_op jit(solution)/shard_map/psum | solution.py:56
  453.3 12.3 %all-reduce.98 = (f32[]{:T(128)}, f32[]{:T(128)}) all-reduce(f32[]{:T(128)} %get-tuple-element.30, f32[]{:T(128)} %get-tuple-element.31), channel_id=1, replica_groups=mesh['px_0'=8,'px_1'=2,'py_0'=4,'py_1'=4] {'py_1'}, use_global_device_ids=true, to_apply=%region_20.21 | all-reduce | flops 2 | bytes 16 | tf_op jit(solution)/shard_map/psum | solution.py:56
  474.5 4.1 collective-permute-done.77
  480.6 4.2 collective-permute-start.79
  492.5 3.9 collective-permute-start.82
  510.4 4.6 collective-permute-start.87
  515.0 4.0 collective-permute-start.85
  526.9 4.1 collective-permute-start.89
  532.3 6.0 collective-permute-start.91
  540.3 5.8 collective-permute-done.90
  572.1 25.0 %all-reduce.93 = (f32[]{:T(128)}, f32[]{:T(128)}) all-reduce(f32[]{:T(128)} %get-tuple-element.5, f32[]{:T(128)} %get-tuple-element.4), channel_id=1, replica_groups=mesh['px_0'=8,'px_1'=2,'py_0'=4,'py_1'=4] {'px_0'}, use_global_device_ids=true, to_apply=%region_30.31 | all-reduce | flops 2 | bytes 16 | tf_op jit(solution)/shard_map/psum | solution.py:56
  600.2 8.3 %all-reduce.101 = (f32[]{:T(128)}, f32[]{:T(128)}) all-reduce(f32[]{:T(128)} %get-tuple-element.36, f32[]{:T(128)} %get-tuple-element.37), channel_id=1, replica_groups=mesh['px_0'=8,'px_1'=2,'py_0'=4,'py_1'=4] {'py_0'}, use_global_device_ids=true, to_apply=%region_32.33 | all-reduce | flops 2 | bytes 16 | tf_op jit(solution)/shard_map/psum | solution.py:56
  608.5 12.6 %all-reduce.97 = (f32[]{:T(128)}, f32[]{:T(128)}) all-reduce(f32[]{:T(128)} %get-tuple-element.28, f32[]{:T(128)} %get-tuple-element.29), channel_id=1, replica_groups=mesh['px_0'=8,'px_1'=2,'py_0'=4,'py_1'=4] {'py_1'}, use_global_device_ids=true, to_apply=%region_33.34 | all-reduce | flops 2 | bytes 16 | tf_op jit(solution)/shard_map/psum | solution.py:56
  626.2 18.0 %all-reduce.92 = (f32[]{:T(128)}, f32[]{:T(128)}) all-reduce(f32[]{:T(128)} %get-tuple-element.3, f32[]{:T(128)} %get-tuple-element.2), channel_id=1, replica_groups=mesh['px_0'=8,'px_1'=2,'py_0'=4,'py_1'=4] {'px_0'}, use_global_device_ids=true, to_apply=%region_43.44 | all-reduce | flops 2 | bytes 16 | tf_op jit(solution)/shard_map/psum | solution.py:56
  647.3 8.3 %all-reduce.100 = (f32[]{:T(128)}, f32[]{:T(128)}) all-reduce(f32[]{:T(128)} %get-tuple-element.34, f32[]{:T(128)} %get-tuple-element.35), channel_id=1, replica_groups=mesh['px_0'=8,'px_1'=2,'py_0'=4,'py_1'=4] {'py_0'}, use_global_device_ids=true, to_apply=%region_45.46 | all-reduce | flops 2 | bytes 16 | tf_op jit(solution)/shard_map/psum | solution.py:56
  655.7 10.9 %all-reduce.96 = (f32[]{:T(128)}, f32[]{:T(128)}) all-reduce(f32[]{:T(128)} %get-tuple-element.26, f32[]{:T(128)} %get-tuple-element.27), channel_id=1, replica_groups=mesh['px_0'=8,'px_1'=2,'py_0'=4,'py_1'=4] {'py_1'}, use_global_device_ids=true, to_apply=%region_46.47 | all-reduce | flops 2 | bytes 16 | tf_op jit(solution)/shard_map/psum | solution.py:56
  (499 shorter events, 307.2 us)
Async XLA Ops:
  1.5 19.3 %collective-permute-start.1 = (f32[2,8,1024]{2,1,0:T(8,128)S(1)}, f32[2,8,1024]{2,1,0:T(8,128)S(1)}, u32[]{:S(2)}, u32[]{:S(2)}) collective-permute-start(f32[2,8,1024]{2,1,0:T(8,128)S(1)} %get-tuple-element.165), channel_id=1, source_target_pairs={{16,0},{32,16},{48,32},{64,48},{80,64},{96,80},{112,96},{128,112},... | collective-permute-start | bytes 196616 | tf_op jit(solution)/shard_map/ppermute | solution.py:47
  2.8 17.1 %collective-permute-start = (f32[2,8,1024]{2,1,0:T(8,128)S(1)}, f32[2,8,1024]{2,1,0:T(8,128)S(1)}, u32[]{:S(2)}, u32[]{:S(2)}) collective-permute-start(f32[2,8,1024]{2,1,0:T(8,128)S(1)} %get-tuple-element.166), channel_id=1, source_target_pairs={{0,16},{16,32},{32,48},{48,64},{64,80},{80,96},{96,112},{112,128},... | collective-permute-start | bytes 196616 | tf_op jit(solution)/shard_map/ppermute | solution.py:45
  14.0 12.7 %collective-permute-start.6 = (f32[8,2,1024]{2,1,0:T(2,128)S(1)}, f32[8,2,1024]{2,1,0:T(2,128)S(1)}, u32[]{:S(2)}, u32[]{:S(2)}) collective-permute-start(f32[8,2,1024]{2,1,0:T(2,128)S(1)} %get-tuple-element.103), channel_id=1, source_target_pairs={{0,1},{1,2},{2,3},{3,4},{4,5},{5,6},{6,7},{7,8},{8,9},{9,10},{10,1... | collective-permute-start | bytes 196616 | tf_op jit(solution)/shard_map/ppermute | solution.py:45
  17.5 9.3 %collective-permute-start.7 = (f32[8,2,1024]{2,1,0:T(2,128)S(1)}, f32[8,2,1024]{2,1,0:T(2,128)S(1)}, u32[]{:S(2)}, u32[]{:S(2)}) collective-permute-start(f32[8,2,1024]{2,1,0:T(2,128)S(1)} %get-tuple-element.104), channel_id=1, source_target_pairs={{1,0},{2,1},{3,2},{4,3},{5,4},{6,5},{7,6},{8,7},{9,8},{10,9},{11,1... | collective-permute-start | bytes 196616 | tf_op jit(solution)/shard_map/ppermute | solution.py:47
  43.8 9.5 %collective-permute-start.10 = (f32[3,2,1,128]{3,2,1,0:T(1,128)S(1)}, f32[3,2,1,128]{3,2,1,0:T(1,128)S(1)}, u32[]{:S(2)}, u32[]{:S(2)}) collective-permute-start(f32[3,2,1,128]{3,2,1,0:T(1,128)S(1)} %get-tuple-element.197), channel_id=1, source_target_pairs={{1,0},{2,1},{3,2},{4,3},{5,4},{6,5},{7,6},{8,7},{9,8},{10,9},{11,1... | collective-permute-start | bytes 9224 | tf_op jit(solution)/shard_map/ppermute | solution.py:26
  58.9 13.3 %collective-permute-start.14 = (f32[3,2,1,128]{3,2,1,0:T(1,128)S(1)}, f32[3,2,1,128]{3,2,1,0:T(1,128)S(1)}, u32[]{:S(2)}, u32[]{:S(2)}) collective-permute-start(f32[3,2,1,128]{3,2,1,0:T(1,128)S(1)} %get-tuple-element.193), channel_id=1, source_target_pairs={{1,0},{2,1},{3,2},{4,3},{5,4},{6,5},{7,6},{8,7},{9,8},{10,9},{11,1... | collective-permute-start | bytes 9224 | tf_op jit(solution)/shard_map/ppermute | solution.py:26
  60.8 11.3 %collective-permute-start.15 = (f32[3,2,1,128]{3,2,1,0:T(1,128)S(1)}, f32[3,2,1,128]{3,2,1,0:T(1,128)S(1)}, u32[]{:S(2)}, u32[]{:S(2)}) collective-permute-start(f32[3,2,1,128]{3,2,1,0:T(1,128)S(1)} %get-tuple-element.194), channel_id=1, source_target_pairs={{0,1},{1,2},{2,3},{3,4},{4,5},{5,6},{6,7},{7,8},{8,9},{9,10},{10,1... | collective-permute-start | bytes 9224 | tf_op jit(solution)/shard_map/ppermute | solution.py:25
  81.7 19.3 %collective-permute-start.17 = (f32[1,8,1024]{2,1,0:T(8,128)S(1)}, f32[1,8,1024]{2,1,0:T(8,128)S(1)}, u32[]{:S(2)}, u32[]{:S(2)}) collective-permute-start(f32[1,8,1024]{2,1,0:T(8,128)S(1)} %get-tuple-element.161), channel_id=1, source_target_pairs={{0,16},{16,32},{32,48},{48,64},{64,80},{80,96},{96,112},{112,128},... | collective-permute-start | bytes 98312 | tf_op jit(solution)/shard_map/ppermute | solution.py:25
  85.8 15.2 %collective-permute-start.16 = (f32[1,8,1024]{2,1,0:T(8,128)S(1)}, f32[1,8,1024]{2,1,0:T(8,128)S(1)}, u32[]{:S(2)}, u32[]{:S(2)}) collective-permute-start(f32[1,8,1024]{2,1,0:T(8,128)S(1)} %get-tuple-element.162), channel_id=1, source_target_pairs={{16,0},{32,16},{48,32},{64,48},{80,64},{96,80},{112,96},{128,112},... | collective-permute-start | bytes 98312 | tf_op jit(solution)/shard_map/ppermute | solution.py:26
  101.4 13.1 %collective-permute-start.21 = (f32[1,8,1024]{2,1,0:T(8,128)S(1)}, f32[1,8,1024]{2,1,0:T(8,128)S(1)}, u32[]{:S(2)}, u32[]{:S(2)}) collective-permute-start(f32[1,8,1024]{2,1,0:T(8,128)S(1)} %get-tuple-element.157), channel_id=1, source_target_pairs={{0,16},{16,32},{32,48},{48,64},{64,80},{80,96},{96,112},{112,128},... | collective-permute-start | bytes 98312 | tf_op jit(solution)/shard_map/ppermute | solution.py:25
  103.5 11.1 %collective-permute-start.20 = (f32[1,8,1024]{2,1,0:T(8,128)S(1)}, f32[1,8,1024]{2,1,0:T(8,128)S(1)}, u32[]{:S(2)}, u32[]{:S(2)}) collective-permute-start(f32[1,8,1024]{2,1,0:T(8,128)S(1)} %get-tuple-element.158), channel_id=1, source_target_pairs={{16,0},{32,16},{48,32},{64,48},{80,64},{96,80},{112,96},{128,112},... | collective-permute-start | bytes 98312 | tf_op jit(solution)/shard_map/ppermute | solution.py:26
  116.0 15.3 %collective-permute-start.25 = (f32[1,8,1024]{2,1,0:T(8,128)S(1)}, f32[1,8,1024]{2,1,0:T(8,128)S(1)}, u32[]{:S(2)}, u32[]{:S(2)}) collective-permute-start(f32[1,8,1024]{2,1,0:T(8,128)S(1)} %get-tuple-element.153), channel_id=1, source_target_pairs={{0,16},{16,32},{32,48},{48,64},{64,80},{80,96},{96,112},{112,128},... | collective-permute-start | bytes 98312 | tf_op jit(solution)/shard_map/ppermute | solution.py:25
  120.3 11.0 %collective-permute-start.24 = (f32[1,8,1024]{2,1,0:T(8,128)S(1)}, f32[1,8,1024]{2,1,0:T(8,128)S(1)}, u32[]{:S(2)}, u32[]{:S(2)}) collective-permute-start(f32[1,8,1024]{2,1,0:T(8,128)S(1)} %get-tuple-element.154), channel_id=1, source_target_pairs={{16,0},{32,16},{48,32},{64,48},{80,64},{96,80},{112,96},{128,112},... | collective-permute-start | bytes 98312 | tf_op jit(solution)/shard_map/ppermute | solution.py:26
  165.4 10.3 %collective-permute-start.34 = (f32[3,2,1,128]{3,2,1,0:T(1,128)S(1)}, f32[3,2,1,128]{3,2,1,0:T(1,128)S(1)}, u32[]{:S(2)}, u32[]{:S(2)}) collective-permute-start(f32[3,2,1,128]{3,2,1,0:T(1,128)S(1)} %get-tuple-element.189), channel_id=1, source_target_pairs={{1,0},{2,1},{3,2},{4,3},{5,4},{6,5},{7,6},{8,7},{9,8},{10,9},{11,1... | collective-permute-start | bytes 9224 | tf_op jit(solution)/shard_map/ppermute | solution.py:26
  167.3 8.4 %collective-permute-start.35 = (f32[3,2,1,128]{3,2,1,0:T(1,128)S(1)}, f32[3,2,1,128]{3,2,1,0:T(1,128)S(1)}, u32[]{:S(2)}, u32[]{:S(2)}) collective-permute-start(f32[3,2,1,128]{3,2,1,0:T(1,128)S(1)} %get-tuple-element.190), channel_id=1, source_target_pairs={{0,1},{1,2},{2,3},{3,4},{4,5},{5,6},{6,7},{7,8},{8,9},{9,10},{10,1... | collective-permute-start | bytes 9224 | tf_op jit(solution)/shard_map/ppermute | solution.py:25
  180.5 11.3 %collective-permute-start.38 = (f32[3,2,1,128]{3,2,1,0:T(1,128)S(1)}, f32[3,2,1,128]{3,2,1,0:T(1,128)S(1)}, u32[]{:S(2)}, u32[]{:S(2)}) collective-permute-start(f32[3,2,1,128]{3,2,1,0:T(1,128)S(1)} %get-tuple-element.185), channel_id=1, source_target_pairs={{1,0},{2,1},{3,2},{4,3},{5,4},{6,5},{7,6},{8,7},{9,8},{10,9},{11,1... | collective-permute-start | bytes 9224 | tf_op jit(solution)/shard_map/ppermute | solution.py:26
  182.4 9.3 %collective-permute-start.39 = (f32[3,2,1,128]{3,2,1,0:T(1,128)S(1)}, f32[3,2,1,128]{3,2,1,0:T(1,128)S(1)}, u32[]{:S(2)}, u32[]{:S(2)}) collective-permute-start(f32[3,2,1,128]{3,2,1,0:T(1,128)S(1)} %get-tuple-element.186), channel_id=1, source_target_pairs={{0,1},{1,2},{2,3},{3,4},{4,5},{5,6},{6,7},{7,8},{8,9},{9,10},{10,1... | collective-permute-start | bytes 9224 | tf_op jit(solution)/shard_map/ppermute | solution.py:25
  203.2 19.5 %collective-permute-start.41 = (f32[1,8,1024]{2,1,0:T(8,128)S(1)}, f32[1,8,1024]{2,1,0:T(8,128)S(1)}, u32[]{:S(2)}, u32[]{:S(2)}) collective-permute-start(f32[1,8,1024]{2,1,0:T(8,128)S(1)} %get-tuple-element.145), channel_id=1, source_target_pairs={{0,16},{16,32},{32,48},{48,64},{64,80},{80,96},{96,112},{112,128},... | collective-permute-start | bytes 98312 | tf_op jit(solution)/shard_map/ppermute | solution.py:25
  207.8 14.9 %collective-permute-start.40 = (f32[1,8,1024]{2,1,0:T(8,128)S(1)}, f32[1,8,1024]{2,1,0:T(8,128)S(1)}, u32[]{:S(2)}, u32[]{:S(2)}) collective-permute-start(f32[1,8,1024]{2,1,0:T(8,128)S(1)} %get-tuple-element.146), channel_id=1, source_target_pairs={{16,0},{32,16},{48,32},{64,48},{80,64},{96,80},{112,96},{128,112},... | collective-permute-start | bytes 98312 | tf_op jit(solution)/shard_map/ppermute | solution.py:26
  209.1 8.0 %collective-permute-start.43 = (f32[4,1,1024]{2,1,0:T(1,128)S(1)}, f32[4,1,1024]{2,1,0:T(1,128)S(1)}, u32[]{:S(2)}, u32[]{:S(2)}) collective-permute-start(f32[4,1,1024]{2,1,0:T(1,128)S(1)} %get-tuple-element.147), channel_id=1, source_target_pairs={{0,1},{1,2},{2,3},{3,4},{4,5},{5,6},{6,7},{7,8},{8,9},{9,10},{10,1... | collective-permute-start | bytes 49160 | tf_op jit(solution)/shard_map/ppermute | solution.py:25
  223.1 15.4 %collective-permute-start.45 = (f32[1,8,1024]{2,1,0:T(8,128)S(1)}, f32[1,8,1024]{2,1,0:T(8,128)S(1)}, u32[]{:S(2)}, u32[]{:S(2)}) collective-permute-start(f32[1,8,1024]{2,1,0:T(8,128)S(1)} %get-tuple-element.141), channel_id=1, source_target_pairs={{0,16},{16,32},{32,48},{48,64},{64,80},{80,96},{96,112},{112,128},... | collective-permute-start | bytes 98312 | tf_op jit(solution)/shard_map/ppermute | solution.py:25
  227.5 11.0 %collective-permute-start.44 = (f32[1,8,1024]{2,1,0:T(8,128)S(1)}, f32[1,8,1024]{2,1,0:T(8,128)S(1)}, u32[]{:S(2)}, u32[]{:S(2)}) collective-permute-start(f32[1,8,1024]{2,1,0:T(8,128)S(1)} %get-tuple-element.142), channel_id=1, source_target_pairs={{16,0},{32,16},{48,32},{64,48},{80,64},{96,80},{112,96},{128,112},... | collective-permute-start | bytes 98312 | tf_op jit(solution)/shard_map/ppermute | solution.py:26
  240.1 66.1 %collective-permute-start.49 = (f32[1,8,1024]{2,1,0:T(8,128)S(1)}, f32[1,8,1024]{2,1,0:T(8,128)S(1)}, u32[]{:S(2)}, u32[]{:S(2)}) collective-permute-start(f32[1,8,1024]{2,1,0:T(8,128)S(1)} %get-tuple-element.137), channel_id=1, source_target_pairs={{0,16},{16,32},{32,48},{48,64},{64,80},{80,96},{96,112},{112,128},... | collective-permute-start | bytes 98312 | tf_op jit(solution)/shard_map/ppermute | solution.py:25
  246.0 60.1 %collective-permute-start.48 = (f32[1,8,1024]{2,1,0:T(8,128)S(1)}, f32[1,8,1024]{2,1,0:T(8,128)S(1)}, u32[]{:S(2)}, u32[]{:S(2)}) collective-permute-start(f32[1,8,1024]{2,1,0:T(8,128)S(1)} %get-tuple-element.138), channel_id=1, source_target_pairs={{16,0},{32,16},{48,32},{64,48},{80,64},{96,80},{112,96},{128,112},... | collective-permute-start | bytes 98312 | tf_op jit(solution)/shard_map/ppermute | solution.py:26
  247.4 58.7 %collective-permute-start.51 = (f32[4,1,1024]{2,1,0:T(1,128)S(1)}, f32[4,1,1024]{2,1,0:T(1,128)S(1)}, u32[]{:S(2)}, u32[]{:S(2)}) collective-permute-start(f32[4,1,1024]{2,1,0:T(1,128)S(1)} %get-tuple-element.139), channel_id=1, source_target_pairs={{0,1},{1,2},{2,3},{3,4},{4,5},{5,6},{6,7},{7,8},{8,9},{9,10},{10,1... | collective-permute-start | bytes 49160 | tf_op jit(solution)/shard_map/ppermute | solution.py:25
  251.0 55.1 %collective-permute-start.50 = (f32[4,1,1024]{2,1,0:T(1,128)S(1)}, f32[4,1,1024]{2,1,0:T(1,128)S(1)}, u32[]{:S(2)}, u32[]{:S(2)}) collective-permute-start(f32[4,1,1024]{2,1,0:T(1,128)S(1)} %get-tuple-element.140), channel_id=1, source_target_pairs={{1,0},{2,1},{3,2},{4,3},{5,4},{6,5},{7,6},{8,7},{9,8},{10,9},{11,1... | collective-permute-start | bytes 49160 | tf_op jit(solution)/shard_map/ppermute | solution.py:26
  333.9 10.3 %collective-permute-start.58 = (f32[3,2,1,128]{3,2,1,0:T(1,128)S(1)}, f32[3,2,1,128]{3,2,1,0:T(1,128)S(1)}, u32[]{:S(2)}, u32[]{:S(2)}) collective-permute-start(f32[3,2,1,128]{3,2,1,0:T(1,128)S(1)} %get-tuple-element.181), channel_id=1, source_target_pairs={{1,0},{2,1},{3,2},{4,3},{5,4},{6,5},{7,6},{8,7},{9,8},{10,9},{11,1... | collective-permute-start | bytes 9224 | tf_op jit(solution)/shard_map/ppermute | solution.py:26
  347.9 12.7 %collective-permute-start.62 = (f32[3,2,1,128]{3,2,1,0:T(1,128)S(1)}, f32[3,2,1,128]{3,2,1,0:T(1,128)S(1)}, u32[]{:S(2)}, u32[]{:S(2)}) collective-permute-start(f32[3,2,1,128]{3,2,1,0:T(1,128)S(1)} %get-tuple-element.177), channel_id=1, source_target_pairs={{1,0},{2,1},{3,2},{4,3},{5,4},{6,5},{7,6},{8,7},{9,8},{10,9},{11,1... | collective-permute-start | bytes 9224 | tf_op jit(solution)/shard_map/ppermute | solution.py:26
  351.8 8.8 %collective-permute-start.63 = (f32[3,2,1,128]{3,2,1,0:T(1,128)S(1)}, f32[3,2,1,128]{3,2,1,0:T(1,128)S(1)}, u32[]{:S(2)}, u32[]{:S(2)}) collective-permute-start(f32[3,2,1,128]{3,2,1,0:T(1,128)S(1)} %get-tuple-element.178), channel_id=1, source_target_pairs={{0,1},{1,2},{2,3},{3,4},{4,5},{5,6},{6,7},{7,8},{8,9},{9,10},{10,1... | collective-permute-start | bytes 9224 | tf_op jit(solution)/shard_map/ppermute | solution.py:25
  371.3 19.3 %collective-permute-start.65 = (f32[1,8,1024]{2,1,0:T(8,128)S(1)}, f32[1,8,1024]{2,1,0:T(8,128)S(1)}, u32[]{:S(2)}, u32[]{:S(2)}) collective-permute-start(f32[1,8,1024]{2,1,0:T(8,128)S(1)} %get-tuple-element.129), channel_id=1, source_target_pairs={{0,16},{16,32},{32,48},{48,64},{64,80},{80,96},{96,112},{112,128},... | collective-permute-start | bytes 98312 | tf_op jit(solution)/shard_map/ppermute | solution.py:25
  375.4 15.2 %collective-permute-start.64 = (f32[1,8,1024]{2,1,0:T(8,128)S(1)}, f32[1,8,1024]{2,1,0:T(8,128)S(1)}, u32[]{:S(2)}, u32[]{:S(2)}) collective-permute-start(f32[1,8,1024]{2,1,0:T(8,128)S(1)} %get-tuple-element.130), channel_id=1, source_target_pairs={{16,0},{32,16},{48,32},{64,48},{80,64},{96,80},{112,96},{128,112},... | collective-permute-start | bytes 98312 | tf_op jit(solution)/shard_map/ppermute | solution.py:26
  391.1 13.1 %collective-permute-start.69 = (f32[1,8,1024]{2,1,0:T(8,128)S(1)}, f32[1,8,1024]{2,1,0:T(8,128)S(1)}, u32[]{:S(2)}, u32[]{:S(2)}) collective-permute-start(f32[1,8,1024]{2,1,0:T(8,128)S(1)} %get-tuple-element.125), channel_id=1, source_target_pairs={{0,16},{16,32},{32,48},{48,64},{64,80},{80,96},{96,112},{112,128},... | collective-permute-start | bytes 98312 | tf_op jit(solution)/shard_map/ppermute | solution.py:25
  393.1 11.0 %collective-permute-start.68 = (f32[1,8,1024]{2,1,0:T(8,128)S(1)}, f32[1,8,1024]{2,1,0:T(8,128)S(1)}, u32[]{:S(2)}, u32[]{:S(2)}) collective-permute-start(f32[1,8,1024]{2,1,0:T(8,128)S(1)} %get-tuple-element.126), channel_id=1, source_target_pairs={{16,0},{32,16},{48,32},{64,48},{80,64},{96,80},{112,96},{128,112},... | collective-permute-start | bytes 98312 | tf_op jit(solution)/shard_map/ppermute | solution.py:26
  405.7 64.3 %collective-permute-start.73 = (f32[1,8,1024]{2,1,0:T(8,128)S(1)}, f32[1,8,1024]{2,1,0:T(8,128)S(1)}, u32[]{:S(2)}, u32[]{:S(2)}) collective-permute-start(f32[1,8,1024]{2,1,0:T(8,128)S(1)} %get-tuple-element.121), channel_id=1, source_target_pairs={{0,16},{16,32},{32,48},{48,64},{64,80},{80,96},{96,112},{112,128},... | collective-permute-start | bytes 98312 | tf_op jit(solution)/shard_map/ppermute | solution.py:25
  409.3 60.6 %collective-permute-start.72 = (f32[1,8,1024]{2,1,0:T(8,128)S(1)}, f32[1,8,1024]{2,1,0:T(8,128)S(1)}, u32[]{:S(2)}, u32[]{:S(2)}) collective-permute-start(f32[1,8,1024]{2,1,0:T(8,128)S(1)} %get-tuple-element.122), channel_id=1, source_target_pairs={{16,0},{32,16},{48,32},{64,48},{80,64},{96,80},{112,96},{128,112},... | collective-permute-start | bytes 98312 | tf_op jit(solution)/shard_map/ppermute | solution.py:26
  410.7 59.2 %collective-permute-start.75 = (f32[4,1,1024]{2,1,0:T(1,128)S(1)}, f32[4,1,1024]{2,1,0:T(1,128)S(1)}, u32[]{:S(2)}, u32[]{:S(2)}) collective-permute-start(f32[4,1,1024]{2,1,0:T(1,128)S(1)} %get-tuple-element.123), channel_id=1, source_target_pairs={{0,1},{1,2},{2,3},{3,4},{4,5},{5,6},{6,7},{7,8},{8,9},{9,10},{10,1... | collective-permute-start | bytes 49160 | tf_op jit(solution)/shard_map/ppermute | solution.py:25
  414.3 55.6 %collective-permute-start.74 = (f32[4,1,1024]{2,1,0:T(1,128)S(1)}, f32[4,1,1024]{2,1,0:T(1,128)S(1)}, u32[]{:S(2)}, u32[]{:S(2)}) collective-permute-start(f32[4,1,1024]{2,1,0:T(1,128)S(1)} %get-tuple-element.124), channel_id=1, source_target_pairs={{1,0},{2,1},{3,2},{4,3},{5,4},{6,5},{7,6},{8,7},{9,8},{10,9},{11,1... | collective-permute-start | bytes 49160 | tf_op jit(solution)/shard_map/ppermute | solution.py:26
  492.5 11.2 %collective-permute-start.82 = (f32[3,2,1,128]{3,2,1,0:T(1,128)S(1)}, f32[3,2,1,128]{3,2,1,0:T(1,128)S(1)}, u32[]{:S(2)}, u32[]{:S(2)}) collective-permute-start(f32[3,2,1,128]{3,2,1,0:T(1,128)S(1)} %get-tuple-element.173), channel_id=1, source_target_pairs={{1,0},{2,1},{3,2},{4,3},{5,4},{6,5},{7,6},{8,7},{9,8},{10,9},{11,1... | collective-permute-start | bytes 9224 | tf_op jit(solution)/shard_map/ppermute | solution.py:26
  507.1 13.3 %collective-permute-start.86 = (f32[3,2,1,128]{3,2,1,0:T(1,128)S(1)}, f32[3,2,1,128]{3,2,1,0:T(1,128)S(1)}, u32[]{:S(2)}, u32[]{:S(2)}) collective-permute-start(f32[3,2,1,128]{3,2,1,0:T(1,128)S(1)} %get-tuple-element.169), channel_id=1, source_target_pairs={{1,0},{2,1},{3,2},{4,3},{5,4},{6,5},{7,6},{8,7},{9,8},{10,9},{11,1... | collective-permute-start | bytes 9224 | tf_op jit(solution)/shard_map/ppermute | solution.py:26
  510.4 10.0 %collective-permute-start.87 = (f32[3,2,1,128]{3,2,1,0:T(1,128)S(1)}, f32[3,2,1,128]{3,2,1,0:T(1,128)S(1)}, u32[]{:S(2)}, u32[]{:S(2)}) collective-permute-start(f32[3,2,1,128]{3,2,1,0:T(1,128)S(1)} %get-tuple-element.170), channel_id=1, source_target_pairs={{0,1},{1,2},{2,3},{3,4},{4,5},{5,6},{6,7},{7,8},{8,9},{9,10},{10,1... | collective-permute-start | bytes 9224 | tf_op jit(solution)/shard_map/ppermute | solution.py:25
  526.9 19.3 %collective-permute-start.89 = (f32[1,8,1024]{2,1,0:T(8,128)S(1)}, f32[1,8,1024]{2,1,0:T(8,128)S(1)}, u32[]{:S(2)}, u32[]{:S(2)}) collective-permute-start(f32[1,8,1024]{2,1,0:T(8,128)S(1)} %get-tuple-element.113), channel_id=1, source_target_pairs={{0,16},{16,32},{32,48},{48,64},{64,80},{80,96},{96,112},{112,128},... | collective-permute-start | bytes 98312 | tf_op jit(solution)/shard_map/ppermute | solution.py:25
  531.0 15.2 %collective-permute-start.88 = (f32[1,8,1024]{2,1,0:T(8,128)S(1)}, f32[1,8,1024]{2,1,0:T(8,128)S(1)}, u32[]{:S(2)}, u32[]{:S(2)}) collective-permute-start(f32[1,8,1024]{2,1,0:T(8,128)S(1)} %get-tuple-element.114), channel_id=1, source_target_pairs={{16,0},{32,16},{48,32},{64,48},{80,64},{96,80},{112,96},{128,112},... | collective-permute-start | bytes 98312 | tf_op jit(solution)/shard_map/ppermute | solution.py:26
  546.7 13.1 %collective-permute-start.93 = (f32[1,8,1024]{2,1,0:T(8,128)S(1)}, f32[1,8,1024]{2,1,0:T(8,128)S(1)}, u32[]{:S(2)}, u32[]{:S(2)}) collective-permute-start(f32[1,8,1024]{2,1,0:T(8,128)S(1)} %get-tuple-element.109), channel_id=1, source_target_pairs={{0,16},{16,32},{32,48},{48,64},{64,80},{80,96},{96,112},{112,128},... | collective-permute-start | bytes 98312 | tf_op jit(solution)/shard_map/ppermute | solution.py:25
  548.7 11.0 %collective-permute-start.92 = (f32[1,8,1024]{2,1,0:T(8,128)S(1)}, f32[1,8,1024]{2,1,0:T(8,128)S(1)}, u32[]{:S(2)}, u32[]{:S(2)}) collective-permute-start(f32[1,8,1024]{2,1,0:T(8,128)S(1)} %get-tuple-element.110), channel_id=1, source_target_pairs={{16,0},{32,16},{48,32},{64,48},{80,64},{96,80},{112,96},{128,112},... | collective-permute-start | bytes 98312 | tf_op jit(solution)/shard_map/ppermute | solution.py:26
  561.2 63.8 %collective-permute-start.97 = (f32[1,8,1024]{2,1,0:T(8,128)S(1)}, f32[1,8,1024]{2,1,0:T(8,128)S(1)}, u32[]{:S(2)}, u32[]{:S(2)}) collective-permute-start(f32[1,8,1024]{2,1,0:T(8,128)S(1)} %get-tuple-element.105), channel_id=1, source_target_pairs={{0,16},{16,32},{32,48},{48,64},{64,80},{80,96},{96,112},{112,128},... | collective-permute-start | bytes 98312 | tf_op jit(solution)/shard_map/ppermute | solution.py:25
  564.9 60.1 %collective-permute-start.96 = (f32[1,8,1024]{2,1,0:T(8,128)S(1)}, f32[1,8,1024]{2,1,0:T(8,128)S(1)}, u32[]{:S(2)}, u32[]{:S(2)}) collective-permute-start(f32[1,8,1024]{2,1,0:T(8,128)S(1)} %get-tuple-element.106), channel_id=1, source_target_pairs={{16,0},{32,16},{48,32},{64,48},{80,64},{96,80},{112,96},{128,112},... | collective-permute-start | bytes 98312 | tf_op jit(solution)/shard_map/ppermute | solution.py:26
  566.2 58.7 %collective-permute-start.99 = (f32[4,1,1024]{2,1,0:T(1,128)S(1)}, f32[4,1,1024]{2,1,0:T(1,128)S(1)}, u32[]{:S(2)}, u32[]{:S(2)}) collective-permute-start(f32[4,1,1024]{2,1,0:T(1,128)S(1)} %get-tuple-element.107), channel_id=1, source_target_pairs={{0,1},{1,2},{2,3},{3,4},{4,5},{5,6},{6,7},{7,8},{8,9},{9,10},{10,1... | collective-permute-start | bytes 49160 | tf_op jit(solution)/shard_map/ppermute | solution.py:25
  569.9 55.1 %collective-permute-start.98 = (f32[4,1,1024]{2,1,0:T(1,128)S(1)}, f32[4,1,1024]{2,1,0:T(1,128)S(1)}, u32[]{:S(2)}, u32[]{:S(2)}) collective-permute-start(f32[4,1,1024]{2,1,0:T(1,128)S(1)} %get-tuple-element.108), channel_id=1, source_target_pairs={{1,0},{2,1},{3,2},{4,3},{5,4},{6,5},{7,6},{8,7},{9,8},{10,9},{11,1... | collective-permute-start | bytes 49160 | tf_op jit(solution)/shard_map/ppermute | solution.py:26
  (103 other events, 3319.8 us)
where the time goes:
time: 684 us; the launch traced here: 672 us
  starting transfers between devices  281 us (41%)
  blocking collectives  190 us (28%)
  waiting for transfers between devices  93.5 us (14%)
  local copies, waits for them, and re-layouts  55.5 us (8%)
  other arithmetic  34.7 us (5%)
  between operations  17.5 us (3%)
    psum x16, blocking collectives, by_axis(): value = lax.psum(value, axis)  190 us
    ppermute x40, starting transfers between devices, padded_2(): lax.ppermute(last, axis, up)  157 us
    ppermute x40, starting transfers between devices, padded_2(): lax.ppermute(first, axis, [(b, a) for a, b in up])  73.7 us
    ppermute x40, waiting for transfers between devices, padded_2(): lax.ppermute(first, axis, [(b, a) for a, b in up])  66.1 us
    ppermute x10, starting transfers between devices, with_halo(): lax.ppermute(tail, axis, [(i, (i + 1) % count) for i in range(ends)])  28.7 us
    ppermute x10, waiting for transfers between devices, with_halo(): lax.ppermute(head, axis, [((i + 1) % count, i) for i in range(ends)])  25.8 us
    reshape x12, local copies, waits for them, and re-layouts, box_sum(): values.reshape(rows_agg, 2, cols_agg, 4, depth_agg, 8).sum(axis=(1, 3, 5))  22.2 us
    ppermute x10, starting transfers between devices, with_halo(): lax.ppermute(head, axis, [((i + 1) % count, i) for i in range(ends)])  21.6 us
  transfers between devices with their start and end apart: 100, of which 28 were waited for; matrix products, arithmetic and copies ran while one was open for 1% of the time, Pallas kernels for 0%

commit v1 on v0

v1 whole, which is shorter than its diff:
```python
import jax
import jax.numpy as jnp
from jax import lax
from jax.experimental import pallas as pl
from jax.experimental.pallas import tpu as pltpu
from jax.sharding import PartitionSpec as P

ITERS = 4
OMEGA = 2.0 / 3.0
REST = 1.0 - OMEGA
FACES = (32.0, 16.0, 8.0)
F32 = jnp.float32


def call(body, outs, *args, scalars=1, scratch=(), flops=2_000_000):
    smem = pl.BlockSpec(memory_space=pltpu.SMEM)
    vmem = pl.BlockSpec(memory_space=pltpu.VMEM)
    specs = [smem] * scalars + [vmem] * (len(args) - scalars)
    return pl.pallas_call(
        body,
        out_shape=[jax.ShapeDtypeStruct(shape, F32) for shape in outs],
        in_specs=specs,
        out_specs=[vmem] * len(outs),
        scratch_shapes=list(scratch),
        compiler_params=pltpu.CompilerParams(vmem_limit_bytes=20 * 1024 * 1024),
        cost_estimate=pl.CostEstimate(flops=flops, bytes_accessed=1_000_000, transcendentals=0),
    )(*args)


def along_z(value):
    lane = lax.broadcasted_iota(jnp.int32, value.shape, value.ndim - 1)
    sub = lax.broadcasted_iota(jnp.int32, value.shape, value.ndim - 2)
    after = pltpu.roll(value, 127, value.ndim - 1)
    before = pltpu.roll(value, 1, value.ndim - 1)
    after_row = jnp.where(sub == 7, 0.0, pltpu.roll(after, 7, value.ndim - 2))
    before_row = jnp.where(sub == 0, 0.0, pltpu.roll(before, 1, value.ndim - 2))
    return jnp.where(lane == 127, after_row, after) + jnp.where(lane == 0, before_row, before)


def by_eight(value, ahead):
    lane = lax.broadcasted_iota(jnp.int32, value.shape, value.ndim - 1)
    if ahead:
        moved = pltpu.roll(value, 120, value.ndim - 1)
        return jnp.where(lane >= 120, pltpu.roll(moved, 7, value.ndim - 2), moved)
    moved = pltpu.roll(value, 8, value.ndim - 1)
    return jnp.where(lane < 8, pltpu.roll(moved, 1, value.ndim - 2), moved)


def beside(below, here, above):
    count = here.shape[0]
    inner = here[1 : count - 1]
    return below + above + here[0 : count - 2] + here[2:count] + along_z(inner)


def enter_body(b_ref, d_ref, a_ref, low_ref, high_ref, olow_ref, ohigh_ref):
    lane = lax.broadcasted_iota(jnp.int32, (8, 128), 1)
    for x in range(4):
        for s in range(8):
            part = slice(s * 128, (s + 1) * 128)
            b = b_ref[x, :, part]
            d = d_ref[x, :, part]
            home = (lane + s * 128) // 8
            o = ((a_ref[x, :, part] & 127) - home).astype(F32)
            ref = low_ref if x < 2 else high_ref
            at = (x % 2) * 64 + s
            ref[pl.ds(at, 8, stride=8), :] = b
            ref[pl.ds(128 + at, 8, stride=8), :] = d
            if x < 3:
                olow_ref[pl.ds(x * 64 + s, 8, stride=8), :] = o
            if x > 0:
                ohigh_ref[pl.ds((x - 1) * 64 + s, 8, stride=8), :] = o


def pack_first_body(low_ref, high_ref, xlow_ref, xhigh_ref, olow_ref, ohigh_ref, oxlow_ref, oxhigh_ref,
                    first_ref, last_ref, ofirst_ref, olast_ref):
    for f in range(2):
        for r, ref in enumerate((xlow_ref, low_ref, high_ref, xhigh_ref)):
            for k in range(2):
                first_ref[f, 2 * r + k] = ref[f, k, 0:2]
                last_ref[f, 2 * r + k] = ref[f, k, 6:8]
    rows = [oxlow_ref.at[0], oxlow_ref.at[1], oxlow_ref.at[2], olow_ref.at[0], olow_ref.at[1], olow_ref.at[2],
            ohigh_ref.at[2], oxhigh_ref.at[0], oxhigh_ref.at[1], oxhigh_ref.at[2]]
    for r, ref in enumerate(rows):
        ofirst_ref[r] = ref[0:3]
        olast_ref[r] = ref[5:8]


def setup_body(me_ref, low_ref, high_ref, xlow_ref, xhigh_ref, ylow_ref, yhigh_ref, olow_ref, ohigh_ref,
               oxlow_ref, oxhigh_ref, oylow_ref, oyhigh_ref, inverse_ref, scale_ref, offset_ref):
    px, py, last_x, last_y = me_ref[0], me_ref[1], me_ref[2], me_ref[3]
    below = jnp.where(px > 0, 1.0, 0.0).astype(F32)
    above = jnp.where(px < last_x, 1.0, 0.0).astype(F32)
    left = jnp.where(py > 0, 1.0, 0.0).astype(F32)
    right = jnp.where(py < last_y, 1.0, 0.0).astype(F32)
    for r, (ref, seen) in enumerate(((xlow_ref, below), (low_ref, None), (high_ref, None), (xhigh_ref, above))):
        for k in range(2):
            x = 2 * r + k
            s_mid = 6.0 + ref[1, k]
            s_left = 6.0 + ylow_ref[1, x]
            s_right = 6.0 + yhigh_ref[1, x]
            i_mid, i_left, i_right = 1.0 / s_mid, left / s_left, right / s_right
            if seen is not None:
                i_mid, i_left, i_right = i_mid * seen, i_left * seen, i_right * seen
            inverse_ref[x, 0:2] = i_left
            inverse_ref[x, 2:10] = i_mid
            inverse_ref[x, 10:12] = i_right
            if 1 <= x <= 6:
                scale_ref[x - 1, 0:1] = s_left[1:2]
                scale_ref[x - 1, 1:9] = s_mid
                scale_ref[x - 1, 9:10] = s_right[0:1]
    rows = [oxlow_ref.at[0], oxlow_ref.at[1], oxlow_ref.at[2], olow_ref.at[0], olow_ref.at[1], olow_ref.at[2],
            ohigh_ref.at[2], oxhigh_ref.at[0], oxhigh_ref.at[1], oxhigh_ref.at[2]]
    for r, ref in enumerate(rows):
        offset_ref[r, 0:3] = oylow_ref[r]
        offset_ref[r, 3:11] = ref[...]
        offset_ref[r, 11:14] = oyhigh_ref[r]


def pack_body(low_ref, high_ref, xlow_ref, xhigh_ref, first_ref, last_ref):
    for r, ref in enumerate((xlow_ref, low_ref, high_ref, xhigh_ref)):
        for k in range(2):
            first_ref[2 * r + k] = ref[k, 0:2]
            last_ref[2 * r + k] = ref[k, 6:8]


def restrict_body(first, *refs):
    if first:
        (low, high, xlow, xhigh, ylow, yhigh, inverse_ref, offset_ref, cdiag_ref, link_ref,
         smooth_ref, remain_ref, send_ref) = refs
        low, high, xlow, xhigh, ylow, yhigh = (r.at[0] for r in (low, high, xlow, xhigh, ylow, yhigh))
    else:
        (low, high, xlow, xhigh, ylow, yhigh, inverse_ref, offset_ref, dots_ref,
         smooth_ref, remain_ref, send_ref) = refs
    mids = [ref.at[k] for ref in (xlow, low, high, xhigh) for k in range(2)]

    def vector(x):
        return jnp.concatenate([ylow[x], mids[x][...], yhigh[x]], axis=0)

    smooth = [OMEGA * vector(x) * inverse_ref[x] for x in range(8)]
    shrunk = []
    remains = []
    for x in range(1, 7):
        near = beside(smooth[x - 1][1:11], smooth[x], smooth[x + 1][1:11])
        remain = REST * vector(x)[1:11] + near
        smooth_ref[x - 1] = smooth[x][1:11]
        remain_ref[x - 1] = remain
        remains.append(remain[1:9])
        shrunk.append(remain * inverse_ref[x, 1:11])
    sums = []
    for big_x in range(2):
        parts = []
        for x in (2 * big_x, 2 * big_x + 1):
            near = beside(shrunk[x][1:9], shrunk[x + 1], shrunk[x + 2][1:9])
            reduced = REST * remains[x + 1] + OMEGA * near
            offset = offset_ref[x + 3, 3:11]
            parts.append((
                jnp.where(jnp.abs(offset) < 0.5, reduced, 0.0),
                jnp.where(offset > 0.5, reduced, 0.0),
                jnp.where(offset < -0.5, reduced, 0.0),
            ))
        for big_y in range(2):
            cols = slice(4 * big_y, 4 * big_y + 4)
            here, up, down = (
                jnp.sum(parts[0][k][cols], axis=0) + jnp.sum(parts[1][k][cols], axis=0) for k in range(3)
            )
            sums.append(here + by_eight(up, False) + by_eight(down, True))
    stacked = jnp.concatenate(sums, axis=0)
    row = lax.broadcasted_iota(jnp.int32, (128, 128), 0)
    col = lax.broadcasted_iota(jnp.int32, (128, 128), 1)
    group = jnp.where(row // 8 == col % 16, 1.0, 0.0).astype(F32)
    grouped = jnp.dot(stacked, group, preferred_element_type=F32, precision=lax.Precision.HIGHEST)
    sub = lax.broadcasted_iota(jnp.int32, (8, 128), 0)
    lane = lax.broadcasted_iota(jnp.int32, (8, 128), 1)
    rows = [
        jnp.sum(jnp.where(lane // 16 == sub, grouped[8 * c : 8 * c + 8], 0.0), axis=0, keepdims=True)
        for c in range(4)
    ]
    zero = jnp.zeros((1, 128), F32)
    rows = rows + ([zero] if first else [dots_ref[...]]) + [zero] * 3
    tile = jnp.concatenate(rows, axis=0)
    for j in range(send_ref.shape[0]):
        send_ref[j, 0:8] = tile
    if first:
        more = [cdiag_ref[c // 2, c % 2 : c % 2 + 1, :] for c in range(4)]
        for f in range(3):
            more = more + [FACES[f] * link_ref[f, c // 2, c % 2 : c % 2 + 1, :] for c in range(4)]
        tile = jnp.concatenate(more, axis=0)
        for j in range(send_ref.shape[0]):
            send_ref[j, 8:24] = tile


def window_body(first, me_ref, got_ref, send_ref):
    px, last_x = me_ref[0], me_ref[2]
    count = got_ref.shape[0]
    total = got_ref[0, 4:5, :]
    for j in range(1, count):
        total = total + got_ref[j, 4:5, :]
    zero = jnp.zeros((1, 128), F32)
    at = [jnp.clip(px + d, 0, last_x) for d in range(-2, 3)]
    rows = []
    for big_y in range(2):
        for d in range(5):
            for big_x in range(2):
                rows.append(got_ref[at[d], 2 * big_x + big_y : 2 * big_x + big_y + 1, :])
        rows = rows + [total] + [zero] * 5
    tile = jnp.concatenate(rows, axis=0)
    for j in range(send_ref.shape[0]):
        send_ref[j, 0:32] = tile
    if first:
        rows = []
        for f in range(4):
            for big_y in range(2):
                for d in range(5):
                    for big_x in range(2):
                        r = 8 + 4 * f + 2 * big_x + big_y
                        rows.append(got_ref[at[d], r : r + 1, :])
        tile = jnp.concatenate(rows, axis=0)
        for j in range(send_ref.shape[0]):
            send_ref[j, 32:112] = tile


SPOTS = ((-2, 1), (-1, 0), (-1, 1), (0, 0), (0, 1), (1, 0), (1, 1), (2, 0))


def shift_x(value, ahead):
    return pltpu.roll(value, 15 if ahead else 1, 0)


def shift_k(value, ahead):
    return pltpu.roll(value, 127 if ahead else 1, 1)


def coarse_setup_body(me_ref, got_ref, coef_ref):
    px, py, last_x, last_y = me_ref[0], me_ref[1], me_ref[2], me_ref[3]
    row = lax.broadcasted_iota(jnp.int32, (16, 128), 0)
    lane = lax.broadcasted_iota(jnp.int32, (16, 128), 1)
    pad = jnp.zeros((6, 128), F32)
    where_x = 2 * px - 4 + row
    inside_x = (where_x >= 0) & (where_x < 2 * (last_x + 1)) & (row < 10)

    def take(y, f):
        d, big_y = SPOTS[y]
        at = jnp.clip(py + d, 0, last_y)
        start = 32 + 20 * f + 10 * big_y
        return jnp.concatenate([got_ref[at, start : start + 10, :], pad], axis=0)

    links = [[take(y, f) for y in range(8)] for f in range(1, 4)]
    for y in range(8):
        where_y = 2 * py - 3 + y
        seen = jnp.where((where_y >= 0) & (where_y < 2 * (last_y + 1)), 1.0, 0.0).astype(F32)
        diag = jnp.where(inside_x, take(y, 0), 1.0)
        inverse = jnp.where(inside_x, seen / diag, 0.0)
        coef_ref[0, y] = inverse
        if 1 <= y <= 6:
            coef_ref[1, y] = links[0][y] * inverse
            coef_ref[2, y] = shift_x(links[0][y], False) * inverse
            coef_ref[3, y] = links[1][y] * inverse
            coef_ref[4, y] = links[1][y - 1] * inverse
            coef_ref[5, y] = jnp.where(lane < 127, links[2][y] * inverse, 0.0)
            coef_ref[6, y] = jnp.where(lane > 0, shift_k(links[2][y], False) * inverse, 0.0)
        else:
            for f in range(1, 7):
                coef_ref[f, y] = jnp.zeros((16, 128), F32)


def dots_of(pairs):
    lane = lax.broadcasted_iota(jnp.int32, (1, 128), 1)
    out = jnp.zeros((1, 128), F32)
    for k, value in enumerate(pairs):
        out = jnp.where(lane == k, jnp.sum(value), out)
    return out


def correct_rows(me_ref, got_ref, coef_ref, smooth_ref, remain_ref, inverse_ref, scale_ref, offset_ref):
    py, last_y = me_ref[1], me_ref[3]
    start = []
    for y, (d, big_y) in enumerate(SPOTS):
        at = jnp.clip(py + d, 0, last_y)
        start.append(got_ref[at, 16 * big_y : 16 * big_y + 16, :] * coef_ref[0, y])

    def sweep(now, y):
        here = now[y]
        total = start[y] + coef_ref[1, y] * shift_x(here, True) + coef_ref[2, y] * shift_x(here, False)
        total = total + coef_ref[3, y] * now[y + 1] + coef_ref[4, y] * now[y - 1]
        return total + coef_ref[5, y] * shift_k(here, True) + coef_ref[6, y] * shift_k(here, False)

    second = [None] + [sweep(start, y) for y in range(1, 7)] + [None]
    third = [None, None] + [sweep(second, y) for y in range(2, 6)]
    sub = lax.broadcasted_iota(jnp.int32, (8, 128), 0)
    lane = lax.broadcasted_iota(jnp.int32, (8, 128), 1)
    index = sub * 16 + lane // 8

    def spread_out(tile, x):
        wide = jnp.broadcast_to(tile[x + 4 : x + 5, :], (8, 128))
        return jnp.take_along_axis(wide, index, axis=1)

    tables = [[], [], []]
    for y in range(2, 6):
        for k, tile in enumerate((third[y], shift_k(third[y], True), shift_k(third[y], False))):
            tables[k].append([spread_out(tile, x) for x in range(-2, 4)])
    counts = (3, 4, 4, 3)

    def lifted(x):
        big_x = x // 2
        here, up, down = (
            jnp.concatenate(
                [jnp.broadcast_to(tables[k][y][big_x + 2][None], (counts[y], 8, 128)) for y in range(4)], axis=0
            )
            for k in range(3)
        )
        offset = offset_ref[x + 3]
        return jnp.where(offset > 0.5, up, jnp.where(offset < -0.5, down, here))

    lifts = [lifted(x) for x in range(-3, 7)]
    spreads = []
    for x in range(8):
        near = beside(lifts[x][1:13], lifts[x + 1], lifts[x + 2][1:13])
        spreads.append(REST * lifts[x + 1][1:13] + OMEGA * (inverse_ref[x] * near))
    shaped = []
    for x in range(6):
        near = beside(spreads[x][1:11], spreads[x + 1], spreads[x + 2][1:11])
        spread = spreads[x + 1][1:11]
        left = remain_ref[x] - (scale_ref[x] * spread - near)
        shaped.append(smooth_ref[x] + spread + OMEGA * (inverse_ref[x + 1, 1:11] * left))
    for x in range(4):
        near = beside(shaped[x][1:9], shaped[x + 1], shaped[x + 2][1:9])
        own = shaped[x + 1][1:9]
        yield x, own, scale_ref[x + 1, 1:9] * own - near


def put(low_ref, high_ref, x, value):
    (low_ref if x < 2 else high_ref)[x % 2] = value


def begin_body(me_ref, got_ref, coef_ref, smooth_ref, remain_ref, inverse_ref, scale_ref, offset_ref,
               low_ref, high_ref, z_ref, wlow_ref, whigh_ref, dots_ref):
    gamma = jnp.zeros((8, 128), F32)
    delta = jnp.zeros((8, 128), F32)
    for x, z, w in correct_rows(me_ref, got_ref, coef_ref, smooth_ref, remain_ref, inverse_ref, scale_ref, offset_ref):
        z_ref[x] = z
        put(wlow_ref, whigh_ref, x, w)
        r = (low_ref if x < 2 else high_ref)[0, x % 2]
        gamma = gamma + jnp.sum(r * z, axis=0)
        delta = delta + jnp.sum(w * z, axis=0)
    dots_ref[...] = dots_of((gamma, delta))


def scalars_of(total, old):
    gamma, delta = total[:, 0:1], total[:, 1:2]
    if old is None:
        return gamma, gamma / delta, None
    gamma_old, alpha_old = old[:, 0:1], old[:, 1:2]
    beta = gamma / gamma_old
    return gamma, gamma / (delta - beta * gamma / alpha_old), beta


def as_row(gamma, alpha):
    lane = lax.broadcasted_iota(jnp.int32, (1, 128), 1)
    return jnp.where(lane == 0, gamma, jnp.where(lane == 1, alpha, 0.0))


def total_of(got_ref, row):
    total = got_ref[0, row : row + 1, :]
    for j in range(1, got_ref.shape[0]):
        total = total + got_ref[j, row : row + 1, :]
    return total


def step_body(first, me_ref, got_ref, coef_ref, smooth_ref, remain_ref, inverse_ref, scale_ref, offset_ref,
              z_ref, wlow_ref, whigh_ref, *refs):
    if first:
        low_ref, high_ref = refs[:2]
        refs = refs[2:]
        old = None
    else:
        x_ref, r_ref, p_ref, s_ref, q_ref, t_ref, old_ref = refs[:7]
        refs = refs[7:]
        old = old_ref[...]
    zo_ref, wolow_ref, wohigh_ref, xo_ref, ro_ref, po_ref, so_ref, qo_ref, to_ref, dots_ref, keep_ref = refs
    gamma, alpha, beta = scalars_of(total_of(got_ref, 10), old)
    keep_ref[...] = as_row(gamma, alpha)
    alpha3 = jnp.broadcast_to(alpha, (8, 128))[None]
    beta3 = None if first else jnp.broadcast_to(beta, (8, 128))[None]
    gamma_sum = jnp.zeros((8, 128), F32)
    delta_sum = jnp.zeros((8, 128), F32)
    for x, m, n in correct_rows(me_ref, got_ref, coef_ref, smooth_ref, remain_ref, inverse_ref, scale_ref, offset_ref):
        z = z_ref[x]
        w = (wlow_ref if x < 2 else whigh_ref)[x % 2]
        if first:
            p, s, q, t = z, w, m, n
            r = (low_ref if x < 2 else high_ref)[0, x % 2]
            xo_ref[x] = alpha3 * p
        else:
            p, s, q, t = z + beta3 * p_ref[x], w + beta3 * s_ref[x], m + beta3 * q_ref[x], n + beta3 * t_ref[x]
            r = r_ref[x]
            xo_ref[x] = x_ref[x] + alpha3 * p
        r = r - alpha3 * s
        z = z - alpha3 * q
        w = w - alpha3 * t
        po_ref[x], so_ref[x], qo_ref[x], to_ref[x] = p, s, q, t
        ro_ref[x], zo_ref[x] = r, z
        put(wolow_ref, wohigh_ref, x, w)
        gamma_sum = gamma_sum + jnp.sum(r * z, axis=0)
        delta_sum = delta_sum + jnp.sum(w * z, axis=0)
    dots_ref[...] = dots_of((gamma_sum, delta_sum))


def spread_dots_body(dots_ref, send_ref):
    tile = jnp.broadcast_to(dots_ref[...], (8, 128))
    for j in range(send_ref.shape[0]):
        send_ref[j] = tile


def sum_dots_body(got_ref, send_ref):
    total = got_ref[0]
    for j in range(1, got_ref.shape[0]):
        total = total + got_ref[j]
    for j in range(send_ref.shape[0]):
        send_ref[j] = total


def finish_body(got_ref, z_ref, wlow_ref, whigh_ref, x_ref, r_ref, p_ref, s_ref, old_ref, xo_ref, ro_ref,
                xs_ref, rs_ref):
    gamma, alpha, beta = scalars_of(total_of(got_ref, 0), old_ref[...])
    alpha3 = jnp.broadcast_to(alpha, (8, 128))[None]
    beta3 = jnp.broadcast_to(beta, (8, 128))[None]
    for x in range(4):
        w = (wlow_ref if x < 2 else whigh_ref)[x % 2]
        p = z_ref[x] + beta3 * p_ref[x]
        s = w + beta3 * s_ref[x]
        xs_ref[pl.ds(64 * x, 64), :] = (x_ref[x] + alpha3 * p).reshape(64, 128)
        rs_ref[pl.ds(64 * x, 64), :] = (r_ref[x] - alpha3 * s).reshape(64, 128)
    for x in range(4):
        for s in range(8):
            part = slice(s * 128, (s + 1) * 128)
            xo_ref[x, :, part] = xs_ref[pl.ds(64 * x + s, 8, stride=8), :]
            ro_ref[x, :, part] = rs_ref[pl.ds(64 * x + s, 8, stride=8), :]


def bodied(body, first):
    def run(*refs):
        body(first, *refs)

    return run


def local(right_side, diagonal, aggregate_id, coarse_diag, coarse_link):
    count_x, count_y = lax.axis_size("px"), lax.axis_size("py")
    me = jnp.stack([lax.axis_index("px"), lax.axis_index("py"), count_x - 1, count_y - 1]).astype(jnp.int32)

    def both_ways(low, high, axis):
        count = lax.axis_size(axis)
        up = [(i, (i + 1) % count) for i in range(count)]
        down = [(b, a) for a, b in up]
        return lax.ppermute(high, axis, up), lax.ppermute(low, axis, down)

    def gather(value, axis):
        return lax.all_to_all(value, axis, 0, 0)

    two, field = (2, 8, 8, 128), (4, 8, 8, 128)
    low, high, olow, ohigh = call(
        enter_body, [(256, 128)] * 2 + [(192, 128)] * 2, right_side, diagonal, aggregate_id, scalars=0
    )
    low, high = low.reshape((2,) + two), high.reshape((2,) + two)
    olow, ohigh = olow.reshape(3, 8, 8, 128), ohigh.reshape(3, 8, 8, 128)
    xlow, xhigh = both_ways(low, high, "px")
    oxlow, oxhigh = both_ways(olow, ohigh, "px")
    first, last, ofirst, olast = call(
        pack_first_body, [(2, 8, 2, 8, 128)] * 2 + [(10, 3, 8, 128)] * 2,
        low, high, xlow, xhigh, olow, ohigh, oxlow, oxhigh, scalars=0,
    )
    ylow, yhigh = both_ways(first, last, "py")
    oylow, oyhigh = both_ways(ofirst, olast, "py")
    inverse, scale, offset = call(
        setup_body, [(8, 12, 8, 128), (6, 10, 8, 128), (10, 14, 8, 128)],
        me, low, high, xlow, xhigh, ylow, yhigh, olow, ohigh, oxlow, oxhigh, oylow, oyhigh,
    )
    mid = (6, 10, 8, 128)
    smooth, remain, send = call(
        bodied(restrict_body, True), [mid, mid, (count_x, 24, 128)],
        low, high, xlow, xhigh, ylow, yhigh, inverse, offset, coarse_diag, coarse_link, scalars=0,
    )
    send, = call(bodied(window_body, True), [(count_y, 112, 128)], me, gather(send, "px"))
    got = gather(send, "py")
    coef, = call(coarse_setup_body, [(7, 8, 16, 128)], me, got)
    fixed = (inverse, scale, offset)
    z, wlow, whigh, dots = call(
        begin_body, [field, two, two, (1, 128)], me, got, coef, smooth, remain, *fixed, low, high
    )
    state = None
    for iteration in range(ITERS - 1):
        xlow, xhigh = both_ways(wlow, whigh, "px")
        first, last = call(pack_body, [(8, 2, 8, 128)] * 2, wlow, whigh, xlow, xhigh, scalars=0)
        ylow, yhigh = both_ways(first, last, "py")
        smooth, remain, send = call(
            bodied(restrict_body, False), [mid, mid, (count_x, 8, 128)],
            wlow, whigh, xlow, xhigh, ylow, yhigh, inverse, offset, dots, scalars=0,
        )
        send, = call(bodied(window_body, False), [(count_y, 32, 128)], me, gather(send, "px"))
        got = gather(send, "py")
        more = (low, high) if state is None else state
        z, wlow, whigh, x, r, p, s, q, t, dots, keep = call(
            bodied(step_body, state is None), [field, two, two] + [field] * 6 + [(1, 128)] * 2,
            me, got, coef, smooth, remain, *fixed, z, wlow, whigh, *more,
        )
        state = (x, r, p, s, q, t, keep)
    send, = call(spread_dots_body, [(count_x, 8, 128)], dots, scalars=0)
    send, = call(sum_dots_body, [(count_y, 8, 128)], gather(send, "px"), scalars=0)
    got = gather(send, "py")
    return tuple(call(
        finish_body, [right_side.shape] * 2, got, z, wlow, whigh, x, r, p, s, keep,
        scalars=0, scratch=[pltpu.VMEM((256, 128), F32)] * 2,
    ))


def solution(mesh):
    cells = P("px", "py", None)
    in_specs = (cells, cells, cells, cells, P(None, "px", "py", None))
    return jax.shard_map(local, mesh=mesh, in_specs=in_specs, out_specs=(cells, cells), check_vma=False)
```

time: 684 us -> 219 us (0.32); the launches traced: 672 us -> 217 us
  starting transfers between devices: 281 us -> 19.9 us
  waiting for transfers between devices: 93.5 us -> 30.9 us
  local copies, waits for them, and re-layouts: 55.5 us -> 3.39 us
  blocking collectives: 190 us -> 149 us
  other arithmetic: 34.7 us -> 0.08 us
  between operations: 17.5 us -> 0.83 us
  Pallas kernels: 0 us -> 13.3 us
    ppermute x100 -> x20, starting transfers between devices: 281 us -> 19.9 us  [both_ways(): return (lax.ppermute(high, axis, up), lax.ppermute(low, axis, down))]
    psum x16 -> x0, blocking collectives: 190 us -> none  [by_axis(): value = lax.psum(value, axis)]
    all_to_all x0 -> x10, blocking collectives: none -> 149 us  [gather(): return lax.all_to_all(value, axis, 0, 0)]
    ppermute x100 -> x20, waiting for transfers between devices: 93.5 us -> 30.9 us  [both_ways(): return (lax.ppermute(high, axis, up), lax.ppermute(low, axis, down))]
    reshape x24 -> x0, local copies, waits for them, and re-layouts: 42.4 us -> none  [the longest x12 22.2 us: box_sum(): values.reshape(rows_agg, 2, cols_agg, 4, depth_agg, 8).sum(axis=(1, 3, 5))]
    pallas_call x0 -> x22, Pallas kernels: none -> 13.3 us  [call(): pl.pallas_call(body, out_shape=[jax.ShapeDtypeStruct(shape, F32) for shap...]
    reduce_sum x16 -> x0, other arithmetic: 11.8 us -> none  [the longest x12 7.07 us: box_sum(): values.reshape(rows_agg, 2, cols_agg, 4, depth_agg, 8).sum(axis=(1, 3, 5))]
    select_n x13 -> x0, other arithmetic: 8.09 us -> none  [the longest x4 3.24 us: lift(): jnp.where(go_up, expand(above), jnp.where(go_down, expand(below), expand(...]
  transfers between devices with their start and end apart: 100 -> 20, of which waited for: 28 -> 15; matrix products, arithmetic and copies ran while one was open for 1% -> 0% of each run, Pallas kernels for 0% -> 0%
where the time goes in v1:
time: 219 us; the launch traced here: 217 us
  blocking collectives  149 us (68%)
  waiting for transfers between devices  30.9 us (14%)
  starting transfers between devices  19.9 us (9%)
  Pallas kernels  13.3 us (6%)
  local copies, waits for them, and re-layouts  3.39 us (2%)
    all_to_all x10, blocking collectives, gather(): return lax.all_to_all(value, axis, 0, 0)  149 us
    ppermute x20, waiting for transfers between devices, both_ways(): return (lax.ppermute(high, axis, up), lax.ppermute(low, axis, down))  30.9 us
    ppermute x20, starting transfers between devices, both_ways(): return (lax.ppermute(high, axis, up), lax.ppermute(low, axis, down))  19.9 us
    pallas_call x22, Pallas kernels, call(): pl.pallas_call(body, out_shape=[jax.ShapeDtypeStruct(shape, F32) for shap...  13.3 us
  transfers between devices with their start and end apart: 20, of which 15 were waited for; matrix products, arithmetic and copies ran while one was open for 0% of the time, Pallas kernels for 0%

profile of v1, /device:TPU:8, one launch (start us, length us, event | category | flops | bytes accessed | tf_op | source)
XLA Modules:
  0.0 217.1 jit_solution(8913474975328774106)
XLA Ops:
  0.6 0.9 copy-done
  1.5 0.9 copy-done.1
  2.4 0.9 copy-done.2
  3.4 5.3 %collective-permute-start.1 = (f32[2,2,8,8,128]{4,3,2,1,0:T(8,128)S(1)}, f32[2,2,8,8,128]{4,3,2,1,0:T(8,128)S(1)}, u32[]{:S(2)}, u32[]{:S(2)}) collective-permute-start(f32[2,2,8,8,128]{4,3,2,1,0:T(8,128)S(1)} %bitcast.6), channel_id=1, source_target_pairs={{16,0},{32,16},{48,32},{64,48},{80,64},{96,80},{112,96},{128,112},... | collective-permute-start | bytes 393224 | tf_op jit(solution)/shard_map/ppermute | solution.py:455
  8.8 0.7 collective-permute-start.3
  9.4 2.9 %collective-permute-done.3.oxhigh_ref = f32[3,8,8,128]{3,2,1,0:T(8,128)S(1)} collective-permute-done((f32[3,8,8,128]{3,2,1,0:T(8,128)S(1)}, f32[3,8,8,128]{3,2,1,0:T(8,128)S(1)}, u32[]{:S(2)}, u32[]{:S(2)}) %collective-permute-start.3) | collective-permute-done | bytes 98336 | tf_op jit(solution)/shard_map/ppermute | solution.py:455
  12.3 2.4 %collective-permute-done.2.oxlow_ref = f32[3,8,8,128]{3,2,1,0:T(8,128)S(1)} collective-permute-done((f32[3,8,8,128]{3,2,1,0:T(8,128)S(1)}, f32[3,8,8,128]{3,2,1,0:T(8,128)S(1)}, u32[]{:S(2)}, u32[]{:S(2)}) %collective-permute-start.2) | collective-permute-done | bytes 98336 | tf_op jit(solution)/shard_map/ppermute | solution.py:455
  14.7 1.7 collective-permute-start.4
  16.8 1.6 collective-permute-start.6
  18.4 2.2 %collective-permute-start.7 = (f32[10,3,8,128]{3,2,1,0:T(8,128)S(1)}, f32[10,3,8,128]{3,2,1,0:T(8,128)S(1)}, u32[]{:S(2)}, u32[]{:S(2)}) collective-permute-start(f32[10,3,8,128]{3,2,1,0:T(8,128)S(1)} %get-tuple-element.73), channel_id=1, source_target_pairs={{1,0},{2,1},{3,2},{4,3},{5,4},{6,5},{7,6},{8,7},{9,8},{10,9},{11,1... | collective-permute-start | bytes 368648 | tf_op jit(solution)/shard_map/ppermute | solution.py:455
  20.7 2.8 %collective-permute-done.6.oylow_ref = f32[10,3,8,128]{3,2,1,0:T(8,128)S(1)} collective-permute-done((f32[10,3,8,128]{3,2,1,0:T(8,128)S(1)}, f32[10,3,8,128]{3,2,1,0:T(8,128)S(1)}, u32[]{:S(2)}, u32[]{:S(2)}) %collective-permute-start.6) | collective-permute-done | bytes 122912 | tf_op jit(solution)/shard_map/ppermute | solution.py:455
  23.5 0.6 shard_map.70
  24.2 0.6 copy-done.4
  25.3 15.2 %all_to_all.50.refs_1_ = f32[16,24,128]{2,1,0:T(8,128)S(1)} all-to-all(f32[16,24,128]{2,1,0:T(8,128)S(1)} %get-tuple-element.76), channel_id=1, replica_groups=mesh['px'=16,'py'=16] {'px'}, dimensions={0} | all-to-all | bytes 393216 | tf_op jit(solution)/shard_map/all_to_all | solution.py:458
  40.6 0.6 shard_map.72
  41.2 26.7 %all_to_all.51.got_ref = f32[16,112,128]{2,1,0:T(8,128)S(1)} all-to-all(f32[16,112,128]{2,1,0:T(8,128)S(1)} %shard_map.72), channel_id=1, replica_groups=mesh['px'=16,'py'=16] {'py'}, dimensions={0} | all-to-all | bytes 1835008 | tf_op jit(solution)/shard_map/all_to_all | solution.py:458
  67.9 0.6 shard_map.73.coef_ref.refs_2_
  68.5 1.4 shard_map.74
  70.5 1.4 collective-permute-done.9.xhigh_ref.refs_3_
  71.9 3.0 %collective-permute-done.8.xlow_ref.refs_2_ = f32[2,8,8,128]{3,2,1,0:T(8,128)S(1)} collective-permute-done((f32[2,8,8,128]{3,2,1,0:T(8,128)S(1)}, f32[2,8,8,128]{3,2,1,0:T(8,128)S(1)}, u32[]{:S(2)}, u32[]{:S(2)}) %collective-permute-start.8) | collective-permute-done | bytes 65568 | tf_op jit(solution)/shard_map/ppermute | solution.py:455
  75.0 1.0 collective-permute-start.10
  75.9 1.1 collective-permute-start.11
  77.1 2.2 %collective-permute-done.10.refs_4_ = f32[8,2,8,128]{3,2,1,0:T(8,128)S(1)} collective-permute-done((f32[8,2,8,128]{3,2,1,0:T(8,128)S(1)}, f32[8,2,8,128]{3,2,1,0:T(8,128)S(1)}, u32[]{:S(2)}, u32[]{:S(2)}) %collective-permute-start.10) | collective-permute-done | bytes 65568 | tf_op jit(solution)/shard_map/ppermute | solution.py:455
  79.3 0.9 collective-permute-done.11.refs_5_
  80.7 11.1 %all_to_all.52.refs_1_ = f32[16,8,128]{2,1,0:T(8,128)S(1)} all-to-all(f32[16,8,128]{2,1,0:T(8,128)S(1)} %get-tuple-element.85), channel_id=1, replica_groups=mesh['px'=16,'py'=16] {'px'}, dimensions={0} | all-to-all | bytes 131072 | tf_op jit(solution)/shard_map/all_to_all | solution.py:458
  92.4 17.4 %all_to_all.53.refs_1_ = f32[16,32,128]{2,1,0:T(8,128)S(1)} all-to-all(f32[16,32,128]{2,1,0:T(8,128)S(1)} %shard_map.77), channel_id=1, replica_groups=mesh['px'=16,'py'=16] {'py'}, dimensions={0} | all-to-all | bytes 524288 | tf_op jit(solution)/shard_map/all_to_all | solution.py:458
  109.8 1.5 shard_map.78
  111.8 1.4 collective-permute-done.13.xhigh_ref.refs_3_
  113.2 3.0 %collective-permute-done.12.xlow_ref.refs_2_ = f32[2,8,8,128]{3,2,1,0:T(8,128)S(1)} collective-permute-done((f32[2,8,8,128]{3,2,1,0:T(8,128)S(1)}, f32[2,8,8,128]{3,2,1,0:T(8,128)S(1)}, u32[]{:S(2)}, u32[]{:S(2)}) %collective-permute-start.12) | collective-permute-done | bytes 65568 | tf_op jit(solution)/shard_map/ppermute | solution.py:455
  116.2 1.1 collective-permute-start.14
  117.3 1.0 collective-permute-start.15
  118.3 2.2 %collective-permute-done.14.refs_4_ = f32[8,2,8,128]{3,2,1,0:T(8,128)S(1)} collective-permute-done((f32[8,2,8,128]{3,2,1,0:T(8,128)S(1)}, f32[8,2,8,128]{3,2,1,0:T(8,128)S(1)}, u32[]{:S(2)}, u32[]{:S(2)}) %collective-permute-start.14) | collective-permute-done | bytes 65568 | tf_op jit(solution)/shard_map/ppermute | solution.py:455
  120.5 1.0 collective-permute-done.15.refs_5_
  122.1 10.6 %all_to_all.54.refs_1_ = f32[16,8,128]{2,1,0:T(8,128)S(1)} all-to-all(f32[16,8,128]{2,1,0:T(8,128)S(1)} %get-tuple-element.94), channel_id=1, replica_groups=mesh['px'=16,'py'=16] {'px'}, dimensions={0} | all-to-all | bytes 131072 | tf_op jit(solution)/shard_map/all_to_all | solution.py:458
  133.3 17.7 %all_to_all.55.refs_1_ = f32[16,32,128]{2,1,0:T(8,128)S(1)} all-to-all(f32[16,32,128]{2,1,0:T(8,128)S(1)} %shard_map.81), channel_id=1, replica_groups=mesh['px'=16,'py'=16] {'py'}, dimensions={0} | all-to-all | bytes 524288 | tf_op jit(solution)/shard_map/all_to_all | solution.py:458
  151.0 1.5 shard_map.82
  153.0 1.4 collective-permute-done.17.xhigh_ref.refs_3_
  154.4 3.0 %collective-permute-done.16.xlow_ref.refs_2_ = f32[2,8,8,128]{3,2,1,0:T(8,128)S(1)} collective-permute-done((f32[2,8,8,128]{3,2,1,0:T(8,128)S(1)}, f32[2,8,8,128]{3,2,1,0:T(8,128)S(1)}, u32[]{:S(2)}, u32[]{:S(2)}) %collective-permute-start.16) | collective-permute-done | bytes 65568 | tf_op jit(solution)/shard_map/ppermute | solution.py:455
  157.4 1.3 collective-permute-start.18
  158.7 1.0 collective-permute-start.19
  159.7 2.2 %collective-permute-done.18.refs_4_ = f32[8,2,8,128]{3,2,1,0:T(8,128)S(1)} collective-permute-done((f32[8,2,8,128]{3,2,1,0:T(8,128)S(1)}, f32[8,2,8,128]{3,2,1,0:T(8,128)S(1)}, u32[]{:S(2)}, u32[]{:S(2)}) %collective-permute-start.18) | collective-permute-done | bytes 65568 | tf_op jit(solution)/shard_map/ppermute | solution.py:455
  161.9 1.0 collective-permute-done.19.refs_5_
  163.5 10.6 %all_to_all.56.refs_1_ = f32[16,8,128]{2,1,0:T(8,128)S(1)} all-to-all(f32[16,8,128]{2,1,0:T(8,128)S(1)} %get-tuple-element.110), channel_id=1, replica_groups=mesh['px'=16,'py'=16] {'px'}, dimensions={0} | all-to-all | bytes 131072 | tf_op jit(solution)/shard_map/all_to_all | solution.py:458
  174.7 17.7 %all_to_all.57.refs_1_ = f32[16,32,128]{2,1,0:T(8,128)S(1)} all-to-all(f32[16,32,128]{2,1,0:T(8,128)S(1)} %shard_map.85), channel_id=1, replica_groups=mesh['px'=16,'py'=16] {'py'}, dimensions={0} | all-to-all | bytes 524288 | tf_op jit(solution)/shard_map/all_to_all | solution.py:458
  192.4 2.1 shard_map.86
  194.5 10.4 %all_to_all.58.got_ref = f32[16,8,128]{2,1,0:T(8,128)S(1)} all-to-all(f32[16,8,128]{2,1,0:T(8,128)S(1)} %shard_map.87), channel_id=1, replica_groups=mesh['px'=16,'py'=16] {'px'}, dimensions={0} | all-to-all | bytes 131072 | tf_op jit(solution)/shard_map/all_to_all | solution.py:458
  204.9 11.3 %all_to_all.59.got_ref = f32[16,8,128]{2,1,0:T(8,128)S(1)} all-to-all(f32[16,8,128]{2,1,0:T(8,128)S(1)} %shard_map.88), channel_id=1, replica_groups=mesh['px'=16,'py'=16] {'py'}, dimensions={0} | all-to-all | bytes 131072 | tf_op jit(solution)/shard_map/all_to_all | solution.py:458
  216.1 1.0 shard_map.89
  (36 shorter events, 6.1 us)
Async XLA Ops:
  0.6 0.9 copy-start
  1.5 0.9 copy-start.1
  2.4 0.9 copy-start.2
  3.4 11.3 %collective-permute-start = (f32[2,2,8,8,128]{4,3,2,1,0:T(8,128)S(1)}, f32[2,2,8,8,128]{4,3,2,1,0:T(8,128)S(1)}, u32[]{:S(2)}, u32[]{:S(2)}) collective-permute-start(f32[2,2,8,8,128]{4,3,2,1,0:T(8,128)S(1)} %bitcast.12), channel_id=1, source_target_pairs={{0,16},{16,32},{32,48},{48,64},{64,80},{80,96},{96,112},{112,128},... | collective-permute-start | bytes 393224 | tf_op jit(solution)/shard_map/ppermute | solution.py:455
  3.4 11.2 %collective-permute-start.1 = (f32[2,2,8,8,128]{4,3,2,1,0:T(8,128)S(1)}, f32[2,2,8,8,128]{4,3,2,1,0:T(8,128)S(1)}, u32[]{:S(2)}, u32[]{:S(2)}) collective-permute-start(f32[2,2,8,8,128]{4,3,2,1,0:T(8,128)S(1)} %bitcast.6), channel_id=1, source_target_pairs={{16,0},{32,16},{48,32},{64,48},{80,64},{96,80},{112,96},{128,112},... | collective-permute-start | bytes 393224 | tf_op jit(solution)/shard_map/ppermute | solution.py:455
  8.8 3.5 %collective-permute-start.3 = (f32[3,8,8,128]{3,2,1,0:T(8,128)S(1)}, f32[3,8,8,128]{3,2,1,0:T(8,128)S(1)}, u32[]{:S(2)}, u32[]{:S(2)}) collective-permute-start(f32[3,8,8,128]{3,2,1,0:T(8,128)S(1)} %bitcast.18), channel_id=1, source_target_pairs={{16,0},{32,16},{48,32},{64,48},{80,64},{96,80},{112,96},{128,112},... | collective-permute-start | bytes 294920 | tf_op jit(solution)/shard_map/ppermute | solution.py:455
  9.4 5.3 %collective-permute-start.2 = (f32[3,8,8,128]{3,2,1,0:T(8,128)S(1)}, f32[3,8,8,128]{3,2,1,0:T(8,128)S(1)}, u32[]{:S(2)}, u32[]{:S(2)}) collective-permute-start(f32[3,8,8,128]{3,2,1,0:T(8,128)S(1)} %bitcast.21), channel_id=1, source_target_pairs={{0,16},{16,32},{32,48},{48,64},{64,80},{80,96},{96,112},{112,128},... | collective-permute-start | bytes 294920 | tf_op jit(solution)/shard_map/ppermute | solution.py:455
  14.7 8.7 %collective-permute-start.4 = (f32[2,8,2,8,128]{4,3,2,1,0:T(8,128)S(1)}, f32[2,8,2,8,128]{4,3,2,1,0:T(8,128)S(1)}, u32[]{:S(2)}, u32[]{:S(2)}) collective-permute-start(f32[2,8,2,8,128]{4,3,2,1,0:T(8,128)S(1)} %get-tuple-element.70), channel_id=1, source_target_pairs={{0,1},{1,2},{2,3},{3,4},{4,5},{5,6},{6,7},{7,8},{8,9},{9,10},{10,1... | collective-permute-start | bytes 393224 | tf_op jit(solution)/shard_map/ppermute | solution.py:455
  16.4 7.1 %collective-permute-start.5 = (f32[2,8,2,8,128]{4,3,2,1,0:T(8,128)S(1)}, f32[2,8,2,8,128]{4,3,2,1,0:T(8,128)S(1)}, u32[]{:S(2)}, u32[]{:S(2)}) collective-permute-start(f32[2,8,2,8,128]{4,3,2,1,0:T(8,128)S(1)} %get-tuple-element.71), channel_id=1, source_target_pairs={{1,0},{2,1},{3,2},{4,3},{5,4},{6,5},{7,6},{8,7},{9,8},{10,9},{11,1... | collective-permute-start | bytes 393224 | tf_op jit(solution)/shard_map/ppermute | solution.py:455
  16.8 6.6 %collective-permute-start.6 = (f32[10,3,8,128]{3,2,1,0:T(8,128)S(1)}, f32[10,3,8,128]{3,2,1,0:T(8,128)S(1)}, u32[]{:S(2)}, u32[]{:S(2)}) collective-permute-start(f32[10,3,8,128]{3,2,1,0:T(8,128)S(1)} %get-tuple-element.72), channel_id=1, source_target_pairs={{0,1},{1,2},{2,3},{3,4},{4,5},{5,6},{6,7},{7,8},{8,9},{9,10},{10,1... | collective-permute-start | bytes 368648 | tf_op jit(solution)/shard_map/ppermute | solution.py:455
  18.4 5.1 %collective-permute-start.7 = (f32[10,3,8,128]{3,2,1,0:T(8,128)S(1)}, f32[10,3,8,128]{3,2,1,0:T(8,128)S(1)}, u32[]{:S(2)}, u32[]{:S(2)}) collective-permute-start(f32[10,3,8,128]{3,2,1,0:T(8,128)S(1)} %get-tuple-element.73), channel_id=1, source_target_pairs={{1,0},{2,1},{3,2},{4,3},{5,4},{6,5},{7,6},{8,7},{9,8},{10,9},{11,1... | collective-permute-start | bytes 368648 | tf_op jit(solution)/shard_map/ppermute | solution.py:455
  23.5 0.7 copy-start.3
  24.1 0.7 copy-start.4
  70.0 1.9 collective-permute-start.9
  70.0 4.9 %collective-permute-start.8 = (f32[2,8,8,128]{3,2,1,0:T(8,128)S(1)}, f32[2,8,8,128]{3,2,1,0:T(8,128)S(1)}, u32[]{:S(2)}, u32[]{:S(2)}) collective-permute-start(f32[2,8,8,128]{3,2,1,0:T(8,128)S(1)} %get-tuple-element.81.high_ref.refs_1_.refs_10_), channel_id=1, source_target_pairs={{0,16},{16,32},{32,48},{48,64},{64,80},{80,96},{96,112},{112,128},... | collective-permute-start | bytes 196616 | tf_op jit(solution)/shard_map/ppermute | solution.py:455
  75.0 4.3 %collective-permute-start.10 = (f32[8,2,8,128]{3,2,1,0:T(8,128)S(1)}, f32[8,2,8,128]{3,2,1,0:T(8,128)S(1)}, u32[]{:S(2)}, u32[]{:S(2)}) collective-permute-start(f32[8,2,8,128]{3,2,1,0:T(8,128)S(1)} %get-tuple-element.82), channel_id=1, source_target_pairs={{0,1},{1,2},{2,3},{3,4},{4,5},{5,6},{6,7},{7,8},{8,9},{9,10},{10,1... | collective-permute-start | bytes 196616 | tf_op jit(solution)/shard_map/ppermute | solution.py:455
  75.9 4.3 %collective-permute-start.11 = (f32[8,2,8,128]{3,2,1,0:T(8,128)S(1)}, f32[8,2,8,128]{3,2,1,0:T(8,128)S(1)}, u32[]{:S(2)}, u32[]{:S(2)}) collective-permute-start(f32[8,2,8,128]{3,2,1,0:T(8,128)S(1)} %get-tuple-element.83), channel_id=1, source_target_pairs={{1,0},{2,1},{3,2},{4,3},{5,4},{6,5},{7,6},{8,7},{9,8},{10,9},{11,1... | collective-permute-start | bytes 196616 | tf_op jit(solution)/shard_map/ppermute | solution.py:455
  111.2 1.9 collective-permute-start.13
  111.3 4.9 %collective-permute-start.12 = (f32[2,8,8,128]{3,2,1,0:T(8,128)S(1)}, f32[2,8,8,128]{3,2,1,0:T(8,128)S(1)}, u32[]{:S(2)}, u32[]{:S(2)}) collective-permute-start(f32[2,8,8,128]{3,2,1,0:T(8,128)S(1)} %get-tuple-element.90.high_ref.refs_1_.refs_10_), channel_id=1, source_target_pairs={{0,16},{16,32},{32,48},{48,64},{64,80},{80,96},{96,112},{112,128},... | collective-permute-start | bytes 196616 | tf_op jit(solution)/shard_map/ppermute | solution.py:455
  116.2 4.3 %collective-permute-start.14 = (f32[8,2,8,128]{3,2,1,0:T(8,128)S(1)}, f32[8,2,8,128]{3,2,1,0:T(8,128)S(1)}, u32[]{:S(2)}, u32[]{:S(2)}) collective-permute-start(f32[8,2,8,128]{3,2,1,0:T(8,128)S(1)} %get-tuple-element.91), channel_id=1, source_target_pairs={{0,1},{1,2},{2,3},{3,4},{4,5},{5,6},{6,7},{7,8},{8,9},{9,10},{10,1... | collective-permute-start | bytes 196616 | tf_op jit(solution)/shard_map/ppermute | solution.py:455
  117.3 4.3 %collective-permute-start.15 = (f32[8,2,8,128]{3,2,1,0:T(8,128)S(1)}, f32[8,2,8,128]{3,2,1,0:T(8,128)S(1)}, u32[]{:S(2)}, u32[]{:S(2)}) collective-permute-start(f32[8,2,8,128]{3,2,1,0:T(8,128)S(1)} %get-tuple-element.92), channel_id=1, source_target_pairs={{1,0},{2,1},{3,2},{4,3},{5,4},{6,5},{7,6},{8,7},{9,8},{10,9},{11,1... | collective-permute-start | bytes 196616 | tf_op jit(solution)/shard_map/ppermute | solution.py:455
  152.5 1.9 collective-permute-start.17
  152.5 4.9 %collective-permute-start.16 = (f32[2,8,8,128]{3,2,1,0:T(8,128)S(1)}, f32[2,8,8,128]{3,2,1,0:T(8,128)S(1)}, u32[]{:S(2)}, u32[]{:S(2)}) collective-permute-start(f32[2,8,8,128]{3,2,1,0:T(8,128)S(1)} %get-tuple-element.106.high_ref.refs_1_.refs_10_), channel_id=1, source_target_pairs={{0,16},{16,32},{32,48},{48,64},{64,80},{80,96},{96,112},{112,128},... | collective-permute-start | bytes 196616 | tf_op jit(solution)/shard_map/ppermute | solution.py:455
  157.4 4.5 %collective-permute-start.18 = (f32[8,2,8,128]{3,2,1,0:T(8,128)S(1)}, f32[8,2,8,128]{3,2,1,0:T(8,128)S(1)}, u32[]{:S(2)}, u32[]{:S(2)}) collective-permute-start(f32[8,2,8,128]{3,2,1,0:T(8,128)S(1)} %get-tuple-element.107), channel_id=1, source_target_pairs={{0,1},{1,2},{2,3},{3,4},{4,5},{5,6},{6,7},{7,8},{8,9},{9,10},{10,1... | collective-permute-start | bytes 196616 | tf_op jit(solution)/shard_map/ppermute | solution.py:455
  158.7 4.3 %collective-permute-start.19 = (f32[8,2,8,128]{3,2,1,0:T(8,128)S(1)}, f32[8,2,8,128]{3,2,1,0:T(8,128)S(1)}, u32[]{:S(2)}, u32[]{:S(2)}) collective-permute-start(f32[8,2,8,128]{3,2,1,0:T(8,128)S(1)} %get-tuple-element.108), channel_id=1, source_target_pairs={{1,0},{2,1},{3,2},{4,3},{5,4},{6,5},{7,6},{8,7},{9,8},{10,9},{11,1... | collective-permute-start | bytes 196616 | tf_op jit(solution)/shard_map/ppermute | solution.py:455

commit v2 on v1

--- a/solution.py
+++ b/solution.py
@@ -52,7 +52,7 @@
     return below + above + here[0 : count - 2] + here[2:count] + along_z(inner)
 
 
-def enter_body(b_ref, d_ref, a_ref, low_ref, high_ref, olow_ref, ohigh_ref):
+def enter_body(b_ref, d_ref, a_ref, low_ref, high_ref):
     lane = lax.broadcasted_iota(jnp.int32, (8, 128), 1)
     for x in range(4):
         for s in range(8):
@@ -66,54 +66,58 @@
             ref[pl.ds(at, 8, stride=8), :] = b
             ref[pl.ds(128 + at, 8, stride=8), :] = d
             if x < 3:
-                olow_ref[pl.ds(x * 64 + s, 8, stride=8), :] = o
+                low_ref[pl.ds(256 + x * 64 + s, 8, stride=8), :] = o
             if x > 0:
-                ohigh_ref[pl.ds((x - 1) * 64 + s, 8, stride=8), :] = o
-
-
-def pack_first_body(low_ref, high_ref, xlow_ref, xhigh_ref, olow_ref, ohigh_ref, oxlow_ref, oxhigh_ref,
-                    first_ref, last_ref, ofirst_ref, olast_ref):
+                high_ref[pl.ds(256 + (x - 1) * 64 + s, 8, stride=8), :] = o
+
+
+def field_rows(low, high, xlow, xhigh, base):
+    return [ref.at[base + k] for ref in (xlow, low, high, xhigh) for k in range(2)]
+
+
+def offset_rows(low, high, xlow, xhigh):
+    return [ref.at[4 + k] for ref, ks in ((xlow, (0, 1, 2)), (low, (0, 1, 2)), (high, (2,)), (xhigh, (0, 1, 2))) for k in ks]
+
+
+def pack_first_body(low_ref, high_ref, xlow_ref, xhigh_ref, first_ref, last_ref):
+    four = (low_ref, high_ref, xlow_ref, xhigh_ref)
     for f in range(2):
-        for r, ref in enumerate((xlow_ref, low_ref, high_ref, xhigh_ref)):
-            for k in range(2):
-                first_ref[f, 2 * r + k] = ref[f, k, 0:2]
-                last_ref[f, 2 * r + k] = ref[f, k, 6:8]
-    rows = [oxlow_ref.at[0], oxlow_ref.at[1], oxlow_ref.at[2], olow_ref.at[0], olow_ref.at[1], olow_ref.at[2],
-            ohigh_ref.at[2], oxhigh_ref.at[0], oxhigh_ref.at[1], oxhigh_ref.at[2]]
-    for r, ref in enumerate(rows):
-        ofirst_ref[r] = ref[0:3]
-        olast_ref[r] = ref[5:8]
-
-
-def setup_body(me_ref, low_ref, high_ref, xlow_ref, xhigh_ref, ylow_ref, yhigh_ref, olow_ref, ohigh_ref,
-               oxlow_ref, oxhigh_ref, oylow_ref, oyhigh_ref, inverse_ref, scale_ref, offset_ref):
+        for x, ref in enumerate(field_rows(*four, 2 * f)):
+            at = 16 * f + 2 * x
+            first_ref[at : at + 2] = ref[0:2]
+            last_ref[at : at + 2] = ref[6:8]
+    for x, ref in enumerate(offset_rows(*four)):
+        at = 32 + 3 * x
+        first_ref[at : at + 3] = ref[0:3]
+        last_ref[at : at + 3] = ref[5:8]
+
+
+def setup_body(me_ref, low_ref, high_ref, xlow_ref, xhigh_ref, ylow_ref, yhigh_ref, inverse_ref, scale_ref, offset_ref):
     px, py, last_x, last_y = me_ref[0], me_ref[1], me_ref[2], me_ref[3]
     below = jnp.where(px > 0, 1.0, 0.0).astype(F32)
     above = jnp.where(px < last_x, 1.0, 0.0).astype(F32)
     left = jnp.where(py > 0, 1.0, 0.0).astype(F32)
     right = jnp.where(py < last_y, 1.0, 0.0).astype(F32)
-    for r, (ref, seen) in enumerate(((xlow_ref, below), (low_ref, None), (high_ref, None), (xhigh_ref, above))):
-        for k in range(2):
-            x = 2 * r + k
-            s_mid = 6.0 + ref[1, k]
-            s_left = 6.0 + ylow_ref[1, x]
-            s_right = 6.0 + yhigh_ref[1, x]
-            i_mid, i_left, i_right = 1.0 / s_mid, left / s_left, right / s_right
-            if seen is not None:
-                i_mid, i_left, i_right = i_mid * seen, i_left * seen, i_right * seen
-            inverse_ref[x, 0:2] = i_left
-            inverse_ref[x, 2:10] = i_mid
-            inverse_ref[x, 10:12] = i_right
-            if 1 <= x <= 6:
-                scale_ref[x - 1, 0:1] = s_left[1:2]
-                scale_ref[x - 1, 1:9] = s_mid
-                scale_ref[x - 1, 9:10] = s_right[0:1]
-    rows = [oxlow_ref.at[0], oxlow_ref.at[1], oxlow_ref.at[2], olow_ref.at[0], olow_ref.at[1], olow_ref.at[2],
-            ohigh_ref.at[2], oxhigh_ref.at[0], oxhigh_ref.at[1], oxhigh_ref.at[2]]
-    for r, ref in enumerate(rows):
-        offset_ref[r, 0:3] = oylow_ref[r]
-        offset_ref[r, 3:11] = ref[...]
-        offset_ref[r, 11:14] = oyhigh_ref[r]
+    four = (low_ref, high_ref, xlow_ref, xhigh_ref)
+    for x, ref in enumerate(field_rows(*four, 2)):
+        s_mid = 6.0 + ref[...]
+        s_left = 6.0 + ylow_ref[16 + 2 * x : 18 + 2 * x]
+        s_right = 6.0 + yhigh_ref[16 + 2 * x : 18 + 2 * x]
+        i_mid, i_left, i_right = 1.0 / s_mid, left / s_left, right / s_right
+        if x < 2 or x > 5:
+            seen = below if x < 2 else above
+            i_mid, i_left, i_right = i_mid * seen, i_left * seen, i_right * seen
+        inverse_ref[x, 0:2] = i_left
+        inverse_ref[x, 2:10] = i_mid
+        inverse_ref[x, 10:12] = i_right
+        if 1 <= x <= 6:
+            scale_ref[x - 1, 0:1] = s_left[1:2]
+            scale_ref[x - 1, 1:9] = s_mid
+            scale_ref[x - 1, 9:10] = s_right[0:1]
+    for x, ref in enumerate(offset_rows(*four)):
+        offset_ref[x, 0:3] = ylow_ref[32 + 3 * x : 35 + 3 * x]
+        offset_ref[x, 3:11] = ref[...]
+        offset_ref[x, 11:14] = yhigh_ref[32 + 3 * x : 35 + 3 * x]
 
 
 def pack_body(low_ref, high_ref, xlow_ref, xhigh_ref, first_ref, last_ref):
@@ -127,14 +131,17 @@
     if first:
         (low, high, xlow, xhigh, ylow, yhigh, inverse_ref, offset_ref, cdiag_ref, link_ref,
          smooth_ref, remain_ref, send_ref) = refs
-        low, high, xlow, xhigh, ylow, yhigh = (r.at[0] for r in (low, high, xlow, xhigh, ylow, yhigh))
     else:
         (low, high, xlow, xhigh, ylow, yhigh, inverse_ref, offset_ref, dots_ref,
          smooth_ref, remain_ref, send_ref) = refs
     mids = [ref.at[k] for ref in (xlow, low, high, xhigh) for k in range(2)]
 
     def vector(x):
-        return jnp.concatenate([ylow[x], mids[x][...], yhigh[x]], axis=0)
+        if first:
+            sides = ylow[2 * x : 2 * x + 2], yhigh[2 * x : 2 * x + 2]
+        else:
+            sides = ylow[x], yhigh[x]
+        return jnp.concatenate([sides[0], mids[x][...], sides[1]], axis=0)
 
     smooth = [OMEGA * vector(x) * inverse_ref[x] for x in range(8)]
     shrunk = []
@@ -178,45 +185,44 @@
     zero = jnp.zeros((1, 128), F32)
     rows = rows + ([zero] if first else [dots_ref[...]]) + [zero] * 3
     tile = jnp.concatenate(rows, axis=0)
-    for j in range(send_ref.shape[0]):
-        send_ref[j, 0:8] = tile
     if first:
+        send_ref[0:8] = tile
         more = [cdiag_ref[c // 2, c % 2 : c % 2 + 1, :] for c in range(4)]
         for f in range(3):
             more = more + [FACES[f] * link_ref[f, c // 2, c % 2 : c % 2 + 1, :] for c in range(4)]
-        tile = jnp.concatenate(more, axis=0)
+        send_ref[8:24] = jnp.concatenate(more, axis=0)
+    else:
         for j in range(send_ref.shape[0]):
-            send_ref[j, 8:24] = tile
-
-
-def window_body(first, me_ref, got_ref, send_ref):
+            send_ref[j] = tile
+
+
+def window_rows(pieces, start):
+    return [
+        [ref[start + 2 * big_x + big_y : start + 2 * big_x + big_y + 1, :] for ref in pieces for big_x in range(2)]
+        for big_y in range(2)
+    ]
+
+
+def window_first_body(*refs):
+    pieces, send_ref = refs[:5], refs[5]
+    zero = jnp.zeros((6, 128), F32)
+    early, late = window_rows(pieces, 0)
+    send_ref[0:32] = jnp.concatenate(early + [zero] + late + [zero], axis=0)
+    rows = []
+    for f in range(4):
+        early, late = window_rows(pieces, 8 + 4 * f)
+        rows = rows + early + late
+    send_ref[32:112] = jnp.concatenate(rows, axis=0)
+
+
+def window_body(me_ref, got_ref, send_ref):
     px, last_x = me_ref[0], me_ref[2]
-    count = got_ref.shape[0]
-    total = got_ref[0, 4:5, :]
-    for j in range(1, count):
-        total = total + got_ref[j, 4:5, :]
-    zero = jnp.zeros((1, 128), F32)
-    at = [jnp.clip(px + d, 0, last_x) for d in range(-2, 3)]
-    rows = []
-    for big_y in range(2):
-        for d in range(5):
-            for big_x in range(2):
-                rows.append(got_ref[at[d], 2 * big_x + big_y : 2 * big_x + big_y + 1, :])
-        rows = rows + [total] + [zero] * 5
-    tile = jnp.concatenate(rows, axis=0)
+    total = total_of(got_ref, 4)
+    zero = jnp.zeros((5, 128), F32)
+    early, late = window_rows([got_ref.at[jnp.clip(px + d, 0, last_x)] for d in range(-2, 3)], 0)
+    tile = jnp.concatenate(early + [total, zero] + late + [total, zero], axis=0)
     for j in range(send_ref.shape[0]):
-        send_ref[j, 0:32] = tile
-    if first:
-        rows = []
-        for f in range(4):
-            for big_y in range(2):
-                for d in range(5):
-                    for big_x in range(2):
-                        r = 8 + 4 * f + 2 * big_x + big_y
-                        rows.append(got_ref[at[d], r : r + 1, :])
-        tile = jnp.concatenate(rows, axis=0)
-        for j in range(send_ref.shape[0]):
-            send_ref[j, 32:112] = tile
+        send_ref[j] = tile
 
 
 SPOTS = ((-2, 1), (-1, 0), (-1, 1), (0, 0), (0, 1), (1, 0), (1, 1), (2, 0))
@@ -230,7 +236,8 @@
     return pltpu.roll(value, 127 if ahead else 1, 1)
 
 
-def coarse_setup_body(me_ref, got_ref, coef_ref):
+def coarse_setup_body(me_ref, *refs):
+    pieces, coef_ref = refs[:5], refs[5]
     px, py, last_x, last_y = me_ref[0], me_ref[1], me_ref[2], me_ref[3]
     row = lax.broadcasted_iota(jnp.int32, (16, 128), 0)
     lane = lax.broadcasted_iota(jnp.int32, (16, 128), 1)
@@ -240,9 +247,8 @@
 
     def take(y, f):
         d, big_y = SPOTS[y]
-        at = jnp.clip(py + d, 0, last_y)
         start = 32 + 20 * f + 10 * big_y
-        return jnp.concatenate([got_ref[at, start : start + 10, :], pad], axis=0)
+        return jnp.concatenate([pieces[d + 2][start : start + 10, :], pad], axis=0)
 
     links = [[take(y, f) for y in range(8)] for f in range(1, 4)]
     for y in range(8):
@@ -271,12 +277,10 @@
     return out
 
 
-def correct_rows(me_ref, got_ref, coef_ref, smooth_ref, remain_ref, inverse_ref, scale_ref, offset_ref):
-    py, last_y = me_ref[1], me_ref[3]
-    start = []
-    for y, (d, big_y) in enumerate(SPOTS):
-        at = jnp.clip(py + d, 0, last_y)
-        start.append(got_ref[at, 16 * big_y : 16 * big_y + 16, :] * coef_ref[0, y])
+def correct_rows(pieces, coef_ref, smooth_ref, remain_ref, inverse_ref, scale_ref, offset_ref):
+    start = [
+        pieces[d + 2][16 * big_y : 16 * big_y + 16, :] * coef_ref[0, y] for y, (d, big_y) in enumerate(SPOTS)
+    ]
 
     def sweep(now, y):
         here = now[y]
@@ -332,14 +336,15 @@
     (low_ref if x < 2 else high_ref)[x % 2] = value
 
 
-def begin_body(me_ref, got_ref, coef_ref, smooth_ref, remain_ref, inverse_ref, scale_ref, offset_ref,
-               low_ref, high_ref, z_ref, wlow_ref, whigh_ref, dots_ref):
+def begin_body(*refs):
+    pieces, refs = refs[:5], refs[5:]
+    fixed, (low_ref, high_ref, z_ref, wlow_ref, whigh_ref, dots_ref) = refs[:6], refs[6:]
     gamma = jnp.zeros((8, 128), F32)
     delta = jnp.zeros((8, 128), F32)
-    for x, z, w in correct_rows(me_ref, got_ref, coef_ref, smooth_ref, remain_ref, inverse_ref, scale_ref, offset_ref):
+    for x, z, w in correct_rows(pieces, *fixed):
         z_ref[x] = z
         put(wlow_ref, whigh_ref, x, w)
-        r = (low_ref if x < 2 else high_ref)[0, x % 2]
+        r = (low_ref if x < 2 else high_ref)[x % 2]
         gamma = gamma + jnp.sum(r * z, axis=0)
         delta = delta + jnp.sum(w * z, axis=0)
     dots_ref[...] = dots_of((gamma, delta))
@@ -383,12 +388,15 @@
     beta3 = None if first else jnp.broadcast_to(beta, (8, 128))[None]
     gamma_sum = jnp.zeros((8, 128), F32)
     delta_sum = jnp.zeros((8, 128), F32)
-    for x, m, n in correct_rows(me_ref, got_ref, coef_ref, smooth_ref, remain_ref, inverse_ref, scale_ref, offset_ref):
+    py, last_y = me_ref[1], me_ref[3]
+    pieces = [got_ref.at[jnp.clip(py + d, 0, last_y)] for d in range(-2, 3)]
+    fixed = (coef_ref, smooth_ref, remain_ref, inverse_ref, scale_ref, offset_ref)
+    for x, m, n in correct_rows(pieces, *fixed):
         z = z_ref[x]
         w = (wlow_ref if x < 2 else whigh_ref)[x % 2]
         if first:
             p, s, q, t = z, w, m, n
-            r = (low_ref if x < 2 else high_ref)[0, x % 2]
+            r = (low_ref if x < 2 else high_ref)[x % 2]
             xo_ref[x] = alpha3 * p
         else:
             p, s, q, t = z + beta3 * p_ref[x], w + beta3 * s_ref[x], m + beta3 * q_ref[x], n + beta3 * t_ref[x]
@@ -448,44 +456,40 @@
     count_x, count_y = lax.axis_size("px"), lax.axis_size("py")
     me = jnp.stack([lax.axis_index("px"), lax.axis_index("py"), count_x - 1, count_y - 1]).astype(jnp.int32)
 
-    def both_ways(low, high, axis):
+    def both_ways(low, high, axis, far=1):
         count = lax.axis_size(axis)
-        up = [(i, (i + 1) % count) for i in range(count)]
+        up = [(i, (i + far) % count) for i in range(count)]
         down = [(b, a) for a, b in up]
         return lax.ppermute(high, axis, up), lax.ppermute(low, axis, down)
 
+    def around(value, axis):
+        one_low, one_high = both_ways(value, value, axis)
+        two_low, two_high = both_ways(value, value, axis, 2)
+        return two_low, one_low, value, one_high, two_high
+
     def gather(value, axis):
         return lax.all_to_all(value, axis, 0, 0)
 
     two, field = (2, 8, 8, 128), (4, 8, 8, 128)
-    low, high, olow, ohigh = call(
-        enter_body, [(256, 128)] * 2 + [(192, 128)] * 2, right_side, diagonal, aggregate_id, scalars=0
-    )
-    low, high = low.reshape((2,) + two), high.reshape((2,) + two)
-    olow, ohigh = olow.reshape(3, 8, 8, 128), ohigh.reshape(3, 8, 8, 128)
+    low, high = call(enter_body, [(448, 128)] * 2, right_side, diagonal, aggregate_id, scalars=0)
+    low, high = low.reshape(7, 8, 8, 128), high.reshape(7, 8, 8, 128)
     xlow, xhigh = both_ways(low, high, "px")
-    oxlow, oxhigh = both_ways(olow, ohigh, "px")
-    first, last, ofirst, olast = call(
-        pack_first_body, [(2, 8, 2, 8, 128)] * 2 + [(10, 3, 8, 128)] * 2,
-        low, high, xlow, xhigh, olow, ohigh, oxlow, oxhigh, scalars=0,
-    )
+    first, last = call(pack_first_body, [(62, 8, 128)] * 2, low, high, xlow, xhigh, scalars=0)
     ylow, yhigh = both_ways(first, last, "py")
-    oylow, oyhigh = both_ways(ofirst, olast, "py")
     inverse, scale, offset = call(
-        setup_body, [(8, 12, 8, 128), (6, 10, 8, 128), (10, 14, 8, 128)],
-        me, low, high, xlow, xhigh, ylow, yhigh, olow, ohigh, oxlow, oxhigh, oylow, oyhigh,
+        setup_body, [(8, 12, 8, 128), (6, 10, 8, 128), (10, 14, 8, 128)], me, low, high, xlow, xhigh, ylow, yhigh
     )
     mid = (6, 10, 8, 128)
     smooth, remain, send = call(
-        bodied(restrict_body, True), [mid, mid, (count_x, 24, 128)],
+        bodied(restrict_body, True), [mid, mid, (24, 128)],
         low, high, xlow, xhigh, ylow, yhigh, inverse, offset, coarse_diag, coarse_link, scalars=0,
     )
-    send, = call(bodied(window_body, True), [(count_y, 112, 128)], me, gather(send, "px"))
-    got = gather(send, "py")
-    coef, = call(coarse_setup_body, [(7, 8, 16, 128)], me, got)
+    send, = call(window_first_body, [(112, 128)], *around(send, "px"), scalars=0)
+    pieces = around(send, "py")
+    coef, = call(coarse_setup_body, [(7, 8, 16, 128)], me, *pieces)
     fixed = (inverse, scale, offset)
     z, wlow, whigh, dots = call(
-        begin_body, [field, two, two, (1, 128)], me, got, coef, smooth, remain, *fixed, low, high
+        begin_body, [field, two, two, (1, 128)], *pieces, coef, smooth, remain, *fixed, low, high, scalars=0
     )
     state = None
     for iteration in range(ITERS - 1):
@@ -496,7 +500,7 @@
             bodied(restrict_body, False), [mid, mid, (count_x, 8, 128)],
             wlow, whigh, xlow, xhigh, ylow, yhigh, inverse, offset, dots, scalars=0,
         )
-        send, = call(bodied(window_body, False), [(count_y, 32, 128)], me, gather(send, "px"))
+        send, = call(window_body, [(count_y, 32, 128)], me, gather(send, "px"))
         got = gather(send, "py")
         more = (low, high) if state is None else state
         z, wlow, whigh, x, r, p, s, q, t, dots, keep = call(

time: 219 us -> 198 us (0.904)
  blocking collectives: 149 us -> 106 us
  waiting for transfers between devices: 30.9 us -> 43.8 us
  starting transfers between devices: 19.9 us -> 29.8 us
    all_to_all x10 -> x8, blocking collectives: 149 us -> 106 us  [gather(): return lax.all_to_all(value, axis, 0, 0)]
    ppermute x20 -> x24, waiting for transfers between devices: 30.9 us -> 43.8 us  [both_ways(): return (lax.ppermute(high, axis, up), lax.ppermute(low, axis, down))]
    ppermute x20 -> x24, starting transfers between devices: 19.9 us -> 29.8 us  [both_ways(): return (lax.ppermute(high, axis, up), lax.ppermute(low, axis, down))]
  transfers between devices with their start and end apart: 20 -> 24, of which waited for: 15 -> 22; matrix products, arithmetic and copies ran while one was open for 0% -> 0% of each run, Pallas kernels for 0% -> 0%
where the time goes in v2:
time: 198 us; the launch traced here: 196 us
  blocking collectives  106 us (54%)
  waiting for transfers between devices  43.8 us (22%)
  starting transfers between devices  29.8 us (15%)
  Pallas kernels  12.2 us (6%)
  local copies, waits for them, and re-layouts  3.38 us (2%)
    all_to_all x8, blocking collectives, gather(): return lax.all_to_all(value, axis, 0, 0)  106 us
    ppermute x24, waiting for transfers between devices, both_ways(): return (lax.ppermute(high, axis, up), lax.ppermute(low, axis, down))  43.8 us
    ppermute x24, starting transfers between devices, both_ways(): return (lax.ppermute(high, axis, up), lax.ppermute(low, axis, down))  29.8 us
    pallas_call x22, Pallas kernels, call(): pl.pallas_call(body, out_shape=[jax.ShapeDtypeStruct(shape, F32) for shap...  12.2 us
  transfers between devices with their start and end apart: 24, of which 22 were waited for; matrix products, arithmetic and copies ran while one was open for 0% of the time, Pallas kernels for 0%

profile of v2, /device:TPU:8, one launch (start us, length us, event | category | flops | bytes accessed | tf_op | source)
XLA Modules:
  0.0 196.3 jit_solution(8158196805076912399)
XLA Ops:
  0.6 0.9 copy-done
  1.5 0.9 copy-done.1
  2.4 0.9 copy-done.2
  3.4 5.3 %collective-permute-start.1 = (f32[7,8,8,128]{3,2,1,0:T(8,128)S(1)}, f32[7,8,8,128]{3,2,1,0:T(8,128)S(1)}, u32[]{:S(2)}, u32[]{:S(2)}) collective-permute-start(f32[7,8,8,128]{3,2,1,0:T(8,128)S(1)} %bitcast.4), channel_id=1, source_target_pairs={{16,0},{32,16},{48,32},{64,48},{80,64},{96,80},{112,96},{128,112},... | collective-permute-start | bytes 688136 | tf_op jit(solution)/shard_map/ppermute | solution.py:463
  8.8 3.7 %collective-permute-done.xlow_ref.refs_2_ = f32[7,8,8,128]{3,2,1,0:T(8,128)S(1)} collective-permute-done((f32[7,8,8,128]{3,2,1,0:T(8,128)S(1)}, f32[7,8,8,128]{3,2,1,0:T(8,128)S(1)}, u32[]{:S(2)}, u32[]{:S(2)}) %collective-permute-start) | collective-permute-done | bytes 229408 | tf_op jit(solution)/shard_map/ppermute | solution.py:463
  12.5 1.7 collective-permute-start.2
  14.7 4.7 %collective-permute-done.2.ylow_ref.refs_4_ = f32[62,8,128]{2,1,0:T(8,128)S(1)} collective-permute-done((f32[62,8,128]{2,1,0:T(8,128)S(1)}, f32[62,8,128]{2,1,0:T(8,128)S(1)}, u32[]{:S(2)}, u32[]{:S(2)}) %collective-permute-start.2) | collective-permute-done | bytes 253984 | tf_op jit(solution)/shard_map/ppermute | solution.py:463
  19.4 1.3 collective-permute-done.3.yhigh_ref.refs_5_
  20.7 0.6 shard_map.70
  21.3 0.6 copy-done.4
  22.5 4.7 %collective-permute-start.7 = (f32[24,128]{1,0:T(8,128)S(1)}, f32[24,128]{1,0:T(8,128)S(1)}, u32[]{:S(2)}, u32[]{:S(2)}) collective-permute-start(f32[24,128]{1,0:T(8,128)S(1)} %get-tuple-element.68.refs_2_), channel_id=1, source_target_pairs={{32,0},{48,16},{64,32},{80,48},{96,64},{112,80},{128,96},{144,112}... | collective-permute-start | bytes 36872 | tf_op jit(solution)/shard_map/ppermute | solution.py:463
  27.7 0.8 collective-permute-start.4
  29.0 2.9 %collective-permute-done.5.refs_1_ = f32[24,128]{1,0:T(8,128)S(1)} collective-permute-done((f32[24,128]{1,0:T(8,128)S(1)}, f32[24,128]{1,0:T(8,128)S(1)}, u32[]{:S(2)}, u32[]{:S(2)}) %collective-permute-start.5) | collective-permute-done | bytes 12320 | tf_op jit(solution)/shard_map/ppermute | solution.py:463
  31.9 0.7 collective-permute-done.4.refs_0_
  32.7 6.6 %collective-permute-start.11 = (f32[112,128]{1,0:T(8,128)S(1)}, f32[112,128]{1,0:T(8,128)S(1)}, u32[]{:S(2)}, u32[]{:S(2)}) collective-permute-start(f32[112,128]{1,0:T(8,128)S(1)} %shard_map.72.refs_2_), channel_id=1, source_target_pairs={{2,0},{3,1},{4,2},{5,3},{6,4},{7,5},{8,6},{9,7},{10,8},{11,9},{12,... | collective-permute-start | bytes 172040 | tf_op jit(solution)/shard_map/ppermute | solution.py:463
  39.2 2.0 %collective-permute-start.9 = (f32[112,128]{1,0:T(8,128)S(1)}, f32[112,128]{1,0:T(8,128)S(1)}, u32[]{:S(2)}, u32[]{:S(2)}) collective-permute-start(f32[112,128]{1,0:T(8,128)S(1)} %shard_map.72.refs_2_), channel_id=1, source_target_pairs={{0,1},{1,2},{2,3},{3,4},{4,5},{5,6},{6,7},{7,8},{8,9},{9,10},{10,1... | collective-permute-start | bytes 172040 | tf_op jit(solution)/shard_map/ppermute | solution.py:463
  41.3 2.1 %collective-permute-done.10.refs_3_ = f32[112,128]{1,0:T(8,128)S(1)} collective-permute-done((f32[112,128]{1,0:T(8,128)S(1)}, f32[112,128]{1,0:T(8,128)S(1)}, u32[]{:S(2)}, u32[]{:S(2)}) %collective-permute-start.10) | collective-permute-done | bytes 57376 | tf_op jit(solution)/shard_map/ppermute | solution.py:463
  43.6 5.4 %collective-permute-done.8.refs_0_ = f32[112,128]{1,0:T(8,128)S(1)} collective-permute-done((f32[112,128]{1,0:T(8,128)S(1)}, f32[112,128]{1,0:T(8,128)S(1)}, u32[]{:S(2)}, u32[]{:S(2)}) %collective-permute-start.8) | collective-permute-done | bytes 57376 | tf_op jit(solution)/shard_map/ppermute | solution.py:463
  49.0 0.6 shard_map.73.refs_5_.refs_2_
  49.7 0.9 shard_map.74
  51.1 1.4 collective-permute-done.13.xhigh_ref.refs_3_
  52.5 3.0 %collective-permute-done.12.xlow_ref.refs_2_ = f32[2,8,8,128]{3,2,1,0:T(8,128)S(1)} collective-permute-done((f32[2,8,8,128]{3,2,1,0:T(8,128)S(1)}, f32[2,8,8,128]{3,2,1,0:T(8,128)S(1)}, u32[]{:S(2)}, u32[]{:S(2)}) %collective-permute-start.12) | collective-permute-done | bytes 65568 | tf_op jit(solution)/shard_map/ppermute | solution.py:463
  55.6 2.0 %collective-permute-start.15 = (f32[8,2,8,128]{3,2,1,0:T(8,128)S(1)}, f32[8,2,8,128]{3,2,1,0:T(8,128)S(1)}, u32[]{:S(2)}, u32[]{:S(2)}) collective-permute-start(f32[8,2,8,128]{3,2,1,0:T(8,128)S(1)} %get-tuple-element.75), channel_id=1, source_target_pairs={{1,0},{2,1},{3,2},{4,3},{5,4},{6,5},{7,6},{8,7},{9,8},{10,9},{11,1... | collective-permute-start | bytes 196616 | tf_op jit(solution)/shard_map/ppermute | solution.py:463
  57.7 2.2 %collective-permute-done.14.refs_4_ = f32[8,2,8,128]{3,2,1,0:T(8,128)S(1)} collective-permute-done((f32[8,2,8,128]{3,2,1,0:T(8,128)S(1)}, f32[8,2,8,128]{3,2,1,0:T(8,128)S(1)}, u32[]{:S(2)}, u32[]{:S(2)}) %collective-permute-start.14) | collective-permute-done | bytes 65568 | tf_op jit(solution)/shard_map/ppermute | solution.py:463
  60.5 10.7 %all_to_all.40.got_ref = f32[16,8,128]{2,1,0:T(8,128)S(1)} all-to-all(f32[16,8,128]{2,1,0:T(8,128)S(1)} %get-tuple-element.77), channel_id=1, replica_groups=mesh['px'=16,'py'=16] {'px'}, dimensions={0} | all-to-all | bytes 131072 | tf_op jit(solution)/shard_map/all_to_all | solution.py:471
  71.8 17.3 %all_to_all.41.refs_1_ = f32[16,32,128]{2,1,0:T(8,128)S(1)} all-to-all(f32[16,32,128]{2,1,0:T(8,128)S(1)} %shard_map.77), channel_id=1, replica_groups=mesh['px'=16,'py'=16] {'py'}, dimensions={0} | all-to-all | bytes 524288 | tf_op jit(solution)/shard_map/all_to_all | solution.py:471
  89.1 1.5 shard_map.78
  91.1 1.4 collective-permute-done.17.xhigh_ref.refs_3_
  92.5 3.0 %collective-permute-done.16.xlow_ref.refs_2_ = f32[2,8,8,128]{3,2,1,0:T(8,128)S(1)} collective-permute-done((f32[2,8,8,128]{3,2,1,0:T(8,128)S(1)}, f32[2,8,8,128]{3,2,1,0:T(8,128)S(1)}, u32[]{:S(2)}, u32[]{:S(2)}) %collective-permute-start.16) | collective-permute-done | bytes 65568 | tf_op jit(solution)/shard_map/ppermute | solution.py:463
  95.5 1.1 collective-permute-start.18
  96.6 1.0 collective-permute-start.19
  97.6 2.2 %collective-permute-done.18.refs_4_ = f32[8,2,8,128]{3,2,1,0:T(8,128)S(1)} collective-permute-done((f32[8,2,8,128]{3,2,1,0:T(8,128)S(1)}, f32[8,2,8,128]{3,2,1,0:T(8,128)S(1)}, u32[]{:S(2)}, u32[]{:S(2)}) %collective-permute-start.18) | collective-permute-done | bytes 65568 | tf_op jit(solution)/shard_map/ppermute | solution.py:463
  99.9 1.0 collective-permute-done.19.refs_5_
  101.4 10.6 %all_to_all.42.got_ref = f32[16,8,128]{2,1,0:T(8,128)S(1)} all-to-all(f32[16,8,128]{2,1,0:T(8,128)S(1)} %get-tuple-element.86), channel_id=1, replica_groups=mesh['px'=16,'py'=16] {'px'}, dimensions={0} | all-to-all | bytes 131072 | tf_op jit(solution)/shard_map/all_to_all | solution.py:471
  112.6 17.7 %all_to_all.43.refs_1_ = f32[16,32,128]{2,1,0:T(8,128)S(1)} all-to-all(f32[16,32,128]{2,1,0:T(8,128)S(1)} %shard_map.81), channel_id=1, replica_groups=mesh['px'=16,'py'=16] {'py'}, dimensions={0} | all-to-all | bytes 524288 | tf_op jit(solution)/shard_map/all_to_all | solution.py:471
  130.3 1.5 shard_map.82
  132.3 1.4 collective-permute-done.21.xhigh_ref.refs_3_
  133.7 3.0 %collective-permute-done.20.xlow_ref.refs_2_ = f32[2,8,8,128]{3,2,1,0:T(8,128)S(1)} collective-permute-done((f32[2,8,8,128]{3,2,1,0:T(8,128)S(1)}, f32[2,8,8,128]{3,2,1,0:T(8,128)S(1)}, u32[]{:S(2)}, u32[]{:S(2)}) %collective-permute-start.20) | collective-permute-done | bytes 65568 | tf_op jit(solution)/shard_map/ppermute | solution.py:463
  136.8 1.1 collective-permute-start.22
  137.9 1.0 collective-permute-start.23
  138.9 2.2 %collective-permute-done.22.refs_4_ = f32[8,2,8,128]{3,2,1,0:T(8,128)S(1)} collective-permute-done((f32[8,2,8,128]{3,2,1,0:T(8,128)S(1)}, f32[8,2,8,128]{3,2,1,0:T(8,128)S(1)}, u32[]{:S(2)}, u32[]{:S(2)}) %collective-permute-start.22) | collective-permute-done | bytes 65568 | tf_op jit(solution)/shard_map/ppermute | solution.py:463
  141.1 1.0 collective-permute-done.23.refs_5_
  142.7 10.6 %all_to_all.44.got_ref = f32[16,8,128]{2,1,0:T(8,128)S(1)} all-to-all(f32[16,8,128]{2,1,0:T(8,128)S(1)} %get-tuple-element.102), channel_id=1, replica_groups=mesh['px'=16,'py'=16] {'px'}, dimensions={0} | all-to-all | bytes 131072 | tf_op jit(solution)/shard_map/all_to_all | solution.py:471
  153.9 17.7 %all_to_all.45.refs_1_ = f32[16,32,128]{2,1,0:T(8,128)S(1)} all-to-all(f32[16,32,128]{2,1,0:T(8,128)S(1)} %shard_map.85), channel_id=1, replica_groups=mesh['px'=16,'py'=16] {'py'}, dimensions={0} | all-to-all | bytes 524288 | tf_op jit(solution)/shard_map/all_to_all | solution.py:471
  171.6 2.1 %shard_map.86 = (f32[4,8,8,128]{3,2,1,0:T(8,128)S(1)}, f32[2,8,8,128]{3,2,1,0:T(8,128)S(1)}, f32[2,8,8,128]{3,2,1,0:T(8,128)S(1)}, f32[4,8,8,128]{3,2,1,0:T(8,12...) custom-call(s32[4]{0:T(128)S(1)} %pad_add_fusion.me_ref.refs_0_, ...), custom_call_target="tpu_custom_call" | custom-call | flops 2000000 | bytes 1000000 | tf_op jit(solution)/shard_map/pallas_call | solution.py:19
  173.6 10.4 %all_to_all.46.got_ref = f32[16,8,128]{2,1,0:T(8,128)S(1)} all-to-all(f32[16,8,128]{2,1,0:T(8,128)S(1)} %shard_map.87), channel_id=1, replica_groups=mesh['px'=16,'py'=16] {'px'}, dimensions={0} | all-to-all | bytes 131072 | tf_op jit(solution)/shard_map/all_to_all | solution.py:471
  184.0 11.3 %all_to_all.47.got_ref = f32[16,8,128]{2,1,0:T(8,128)S(1)} all-to-all(f32[16,8,128]{2,1,0:T(8,128)S(1)} %shard_map.88), channel_id=1, replica_groups=mesh['px'=16,'py'=16] {'py'}, dimensions={0} | all-to-all | bytes 131072 | tf_op jit(solution)/shard_map/all_to_all | solution.py:471
  195.3 1.0 shard_map.89
  (42 shorter events, 7.5 us)
Async XLA Ops:
  0.6 0.9 copy-start
  1.5 0.9 copy-start.1
  2.4 0.9 copy-start.2
  3.4 9.0 %collective-permute-start = (f32[7,8,8,128]{3,2,1,0:T(8,128)S(1)}, f32[7,8,8,128]{3,2,1,0:T(8,128)S(1)}, u32[]{:S(2)}, u32[]{:S(2)}) collective-permute-start(f32[7,8,8,128]{3,2,1,0:T(8,128)S(1)} %bitcast.10), channel_id=1, source_target_pairs={{0,16},{16,32},{32,48},{48,64},{64,80},{80,96},{96,112},{112,128},... | collective-permute-start | bytes 688136 | tf_op jit(solution)/shard_map/ppermute | solution.py:463
  3.4 9.0 %collective-permute-start.1 = (f32[7,8,8,128]{3,2,1,0:T(8,128)S(1)}, f32[7,8,8,128]{3,2,1,0:T(8,128)S(1)}, u32[]{:S(2)}, u32[]{:S(2)}) collective-permute-start(f32[7,8,8,128]{3,2,1,0:T(8,128)S(1)} %bitcast.4), channel_id=1, source_target_pairs={{16,0},{32,16},{48,32},{64,48},{80,64},{96,80},{112,96},{128,112},... | collective-permute-start | bytes 688136 | tf_op jit(solution)/shard_map/ppermute | solution.py:463
  12.5 6.9 %collective-permute-start.2 = (f32[62,8,128]{2,1,0:T(8,128)S(1)}, f32[62,8,128]{2,1,0:T(8,128)S(1)}, u32[]{:S(2)}, u32[]{:S(2)}) collective-permute-start(f32[62,8,128]{2,1,0:T(8,128)S(1)} %get-tuple-element.64), channel_id=1, source_target_pairs={{0,1},{1,2},{2,3},{3,4},{4,5},{5,6},{6,7},{7,8},{8,9},{9,10},{10,1... | collective-permute-start | bytes 761864 | tf_op jit(solution)/shard_map/ppermute | solution.py:463
  14.1 6.5 %collective-permute-start.3 = (f32[62,8,128]{2,1,0:T(8,128)S(1)}, f32[62,8,128]{2,1,0:T(8,128)S(1)}, u32[]{:S(2)}, u32[]{:S(2)}) collective-permute-start(f32[62,8,128]{2,1,0:T(8,128)S(1)} %get-tuple-element.65), channel_id=1, source_target_pairs={{1,0},{2,1},{3,2},{4,3},{5,4},{6,5},{7,6},{8,7},{9,8},{10,9},{11,1... | collective-permute-start | bytes 761864 | tf_op jit(solution)/shard_map/ppermute | solution.py:463
  20.7 0.7 copy-start.3
  21.3 0.7 copy-start.4
  22.5 6.1 %collective-permute-start.7 = (f32[24,128]{1,0:T(8,128)S(1)}, f32[24,128]{1,0:T(8,128)S(1)}, u32[]{:S(2)}, u32[]{:S(2)}) collective-permute-start(f32[24,128]{1,0:T(8,128)S(1)} %get-tuple-element.68.refs_2_), channel_id=1, source_target_pairs={{32,0},{48,16},{64,32},{80,48},{96,64},{112,80},{128,96},{144,112}... | collective-permute-start | bytes 36872 | tf_op jit(solution)/shard_map/ppermute | solution.py:463
  27.2 1.8 collective-permute-start.6
  27.6 4.3 %collective-permute-start.5 = (f32[24,128]{1,0:T(8,128)S(1)}, f32[24,128]{1,0:T(8,128)S(1)}, u32[]{:S(2)}, u32[]{:S(2)}) collective-permute-start(f32[24,128]{1,0:T(8,128)S(1)} %get-tuple-element.68.refs_2_), channel_id=1, source_target_pairs={{0,16},{16,32},{32,48},{48,64},{64,80},{80,96},{96,112},{112,128},... | collective-permute-start | bytes 36872 | tf_op jit(solution)/shard_map/ppermute | solution.py:463
  27.7 5.0 %collective-permute-start.4 = (f32[24,128]{1,0:T(8,128)S(1)}, f32[24,128]{1,0:T(8,128)S(1)}, u32[]{:S(2)}, u32[]{:S(2)}) collective-permute-start(f32[24,128]{1,0:T(8,128)S(1)} %get-tuple-element.68.refs_2_), channel_id=1, source_target_pairs={{0,32},{16,48},{32,64},{48,80},{64,96},{80,112},{96,128},{112,144}... | collective-permute-start | bytes 36872 | tf_op jit(solution)/shard_map/ppermute | solution.py:463
  32.7 8.6 %collective-permute-start.11 = (f32[112,128]{1,0:T(8,128)S(1)}, f32[112,128]{1,0:T(8,128)S(1)}, u32[]{:S(2)}, u32[]{:S(2)}) collective-permute-start(f32[112,128]{1,0:T(8,128)S(1)} %shard_map.72.refs_2_), channel_id=1, source_target_pairs={{2,0},{3,1},{4,2},{5,3},{6,4},{7,5},{8,6},{9,7},{10,8},{11,9},{12,... | collective-permute-start | bytes 172040 | tf_op jit(solution)/shard_map/ppermute | solution.py:463
  39.2 4.2 %collective-permute-start.10 = (f32[112,128]{1,0:T(8,128)S(1)}, f32[112,128]{1,0:T(8,128)S(1)}, u32[]{:S(2)}, u32[]{:S(2)}) collective-permute-start(f32[112,128]{1,0:T(8,128)S(1)} %shard_map.72.refs_2_), channel_id=1, source_target_pairs={{1,0},{2,1},{3,2},{4,3},{5,4},{6,5},{7,6},{8,7},{9,8},{10,9},{11,1... | collective-permute-start | bytes 172040 | tf_op jit(solution)/shard_map/ppermute | solution.py:463
  39.2 4.4 %collective-permute-start.9 = (f32[112,128]{1,0:T(8,128)S(1)}, f32[112,128]{1,0:T(8,128)S(1)}, u32[]{:S(2)}, u32[]{:S(2)}) collective-permute-start(f32[112,128]{1,0:T(8,128)S(1)} %shard_map.72.refs_2_), channel_id=1, source_target_pairs={{0,1},{1,2},{2,3},{3,4},{4,5},{5,6},{6,7},{7,8},{8,9},{9,10},{10,1... | collective-permute-start | bytes 172040 | tf_op jit(solution)/shard_map/ppermute | solution.py:463
  41.3 7.8 %collective-permute-start.8 = (f32[112,128]{1,0:T(8,128)S(1)}, f32[112,128]{1,0:T(8,128)S(1)}, u32[]{:S(2)}, u32[]{:S(2)}) collective-permute-start(f32[112,128]{1,0:T(8,128)S(1)} %shard_map.72.refs_2_), channel_id=1, source_target_pairs={{0,2},{1,3},{2,4},{3,5},{4,6},{5,7},{6,8},{7,9},{8,10},{9,11},{10,... | collective-permute-start | bytes 172040 | tf_op jit(solution)/shard_map/ppermute | solution.py:463
  50.6 1.9 collective-permute-start.13
  50.6 4.9 %collective-permute-start.12 = (f32[2,8,8,128]{3,2,1,0:T(8,128)S(1)}, f32[2,8,8,128]{3,2,1,0:T(8,128)S(1)}, u32[]{:S(2)}, u32[]{:S(2)}) collective-permute-start(f32[2,8,8,128]{3,2,1,0:T(8,128)S(1)} %get-tuple-element.73.high_ref.refs_1_.refs_10_), channel_id=1, source_target_pairs={{0,16},{16,32},{32,48},{48,64},{64,80},{80,96},{96,112},{112,128},... | collective-permute-start | bytes 196616 | tf_op jit(solution)/shard_map/ppermute | solution.py:463
  55.6 4.3 %collective-permute-start.14 = (f32[8,2,8,128]{3,2,1,0:T(8,128)S(1)}, f32[8,2,8,128]{3,2,1,0:T(8,128)S(1)}, u32[]{:S(2)}, u32[]{:S(2)}) collective-permute-start(f32[8,2,8,128]{3,2,1,0:T(8,128)S(1)} %get-tuple-element.74), channel_id=1, source_target_pairs={{0,1},{1,2},{2,3},{3,4},{4,5},{5,6},{6,7},{7,8},{8,9},{9,10},{10,1... | collective-permute-start | bytes 196616 | tf_op jit(solution)/shard_map/ppermute | solution.py:463
  55.6 4.3 %collective-permute-start.15 = (f32[8,2,8,128]{3,2,1,0:T(8,128)S(1)}, f32[8,2,8,128]{3,2,1,0:T(8,128)S(1)}, u32[]{:S(2)}, u32[]{:S(2)}) collective-permute-start(f32[8,2,8,128]{3,2,1,0:T(8,128)S(1)} %get-tuple-element.75), channel_id=1, source_target_pairs={{1,0},{2,1},{3,2},{4,3},{5,4},{6,5},{7,6},{8,7},{9,8},{10,9},{11,1... | collective-permute-start | bytes 196616 | tf_op jit(solution)/shard_map/ppermute | solution.py:463
  90.6 1.9 collective-permute-start.17
  90.6 4.9 %collective-permute-start.16 = (f32[2,8,8,128]{3,2,1,0:T(8,128)S(1)}, f32[2,8,8,128]{3,2,1,0:T(8,128)S(1)}, u32[]{:S(2)}, u32[]{:S(2)}) collective-permute-start(f32[2,8,8,128]{3,2,1,0:T(8,128)S(1)} %get-tuple-element.82.high_ref.refs_1_.refs_10_), channel_id=1, source_target_pairs={{0,16},{16,32},{32,48},{48,64},{64,80},{80,96},{96,112},{112,128},... | collective-permute-start | bytes 196616 | tf_op jit(solution)/shard_map/ppermute | solution.py:463
  95.5 4.3 %collective-permute-start.18 = (f32[8,2,8,128]{3,2,1,0:T(8,128)S(1)}, f32[8,2,8,128]{3,2,1,0:T(8,128)S(1)}, u32[]{:S(2)}, u32[]{:S(2)}) collective-permute-start(f32[8,2,8,128]{3,2,1,0:T(8,128)S(1)} %get-tuple-element.83), channel_id=1, source_target_pairs={{0,1},{1,2},{2,3},{3,4},{4,5},{5,6},{6,7},{7,8},{8,9},{9,10},{10,1... | collective-permute-start | bytes 196616 | tf_op jit(solution)/shard_map/ppermute | solution.py:463
  96.6 4.3 %collective-permute-start.19 = (f32[8,2,8,128]{3,2,1,0:T(8,128)S(1)}, f32[8,2,8,128]{3,2,1,0:T(8,128)S(1)}, u32[]{:S(2)}, u32[]{:S(2)}) collective-permute-start(f32[8,2,8,128]{3,2,1,0:T(8,128)S(1)} %get-tuple-element.84), channel_id=1, source_target_pairs={{1,0},{2,1},{3,2},{4,3},{5,4},{6,5},{7,6},{8,7},{9,8},{10,9},{11,1... | collective-permute-start | bytes 196616 | tf_op jit(solution)/shard_map/ppermute | solution.py:463
  131.8 1.9 collective-permute-start.21
  131.8 4.9 %collective-permute-start.20 = (f32[2,8,8,128]{3,2,1,0:T(8,128)S(1)}, f32[2,8,8,128]{3,2,1,0:T(8,128)S(1)}, u32[]{:S(2)}, u32[]{:S(2)}) collective-permute-start(f32[2,8,8,128]{3,2,1,0:T(8,128)S(1)} %get-tuple-element.98.high_ref.refs_1_.refs_10_), channel_id=1, source_target_pairs={{0,16},{16,32},{32,48},{48,64},{64,80},{80,96},{96,112},{112,128},... | collective-permute-start | bytes 196616 | tf_op jit(solution)/shard_map/ppermute | solution.py:463
  136.8 4.3 %collective-permute-start.22 = (f32[8,2,8,128]{3,2,1,0:T(8,128)S(1)}, f32[8,2,8,128]{3,2,1,0:T(8,128)S(1)}, u32[]{:S(2)}, u32[]{:S(2)}) collective-permute-start(f32[8,2,8,128]{3,2,1,0:T(8,128)S(1)} %get-tuple-element.99), channel_id=1, source_target_pairs={{0,1},{1,2},{2,3},{3,4},{4,5},{5,6},{6,7},{7,8},{8,9},{9,10},{10,1... | collective-permute-start | bytes 196616 | tf_op jit(solution)/shard_map/ppermute | solution.py:463
  137.9 4.3 %collective-permute-start.23 = (f32[8,2,8,128]{3,2,1,0:T(8,128)S(1)}, f32[8,2,8,128]{3,2,1,0:T(8,128)S(1)}, u32[]{:S(2)}, u32[]{:S(2)}) collective-permute-start(f32[8,2,8,128]{3,2,1,0:T(8,128)S(1)} %get-tuple-element.100), channel_id=1, source_target_pairs={{1,0},{2,1},{3,2},{4,3},{5,4},{6,5},{7,6},{8,7},{9,8},{10,9},{11,1... | collective-permute-start | bytes 196616 | tf_op jit(solution)/shard_map/ppermute | solution.py:463

commit v3 on v2

--- a/solution.py
+++ b/solution.py
@@ -5,7 +5,6 @@
 from jax.experimental.pallas import tpu as pltpu
 from jax.sharding import PartitionSpec as P
 
-ITERS = 4
 OMEGA = 2.0 / 3.0
 REST = 1.0 - OMEGA
 FACES = (32.0, 16.0, 8.0)
@@ -127,13 +126,10 @@
             last_ref[2 * r + k] = ref[k, 6:8]
 
 
-def restrict_body(first, *refs):
-    if first:
-        (low, high, xlow, xhigh, ylow, yhigh, inverse_ref, offset_ref, cdiag_ref, link_ref,
-         smooth_ref, remain_ref, send_ref) = refs
-    else:
-        (low, high, xlow, xhigh, ylow, yhigh, inverse_ref, offset_ref, dots_ref,
-         smooth_ref, remain_ref, send_ref) = refs
+def restrict_body(mode, *refs):
+    low, high, xlow, xhigh, ylow, yhigh, inverse_ref, offset_ref = refs[:8]
+    smooth_ref, remain_ref, send_ref = refs[-3:]
+    first = mode == 0
     mids = [ref.at[k] for ref in (xlow, low, high, xhigh) for k in range(2)]
 
     def vector(x):
@@ -183,14 +179,17 @@
         for c in range(4)
     ]
     zero = jnp.zeros((1, 128), F32)
-    rows = rows + ([zero] if first else [dots_ref[...]]) + [zero] * 3
+    rows = rows + ([refs[8][...]] if mode == 2 else [zero]) + [zero] * 3
     tile = jnp.concatenate(rows, axis=0)
-    if first:
+    if mode == 0:
+        cdiag_ref, link_ref = refs[8:10]
         send_ref[0:8] = tile
         more = [cdiag_ref[c // 2, c % 2 : c % 2 + 1, :] for c in range(4)]
         for f in range(3):
             more = more + [FACES[f] * link_ref[f, c // 2, c % 2 : c % 2 + 1, :] for c in range(4)]
         send_ref[8:24] = jnp.concatenate(more, axis=0)
+    elif mode == 1:
+        send_ref[...] = tile
     else:
         for j in range(send_ref.shape[0]):
             send_ref[j] = tile
@@ -203,24 +202,25 @@
     ]
 
 
-def window_first_body(*refs):
+def window_near_body(*refs):
     pieces, send_ref = refs[:5], refs[5]
     zero = jnp.zeros((6, 128), F32)
     early, late = window_rows(pieces, 0)
     send_ref[0:32] = jnp.concatenate(early + [zero] + late + [zero], axis=0)
-    rows = []
-    for f in range(4):
-        early, late = window_rows(pieces, 8 + 4 * f)
-        rows = rows + early + late
-    send_ref[32:112] = jnp.concatenate(rows, axis=0)
+    if send_ref.shape[0] > 32:
+        rows = []
+        for f in range(4):
+            early, late = window_rows(pieces, 8 + 4 * f)
+            rows = rows + early + late
+        send_ref[32:112] = jnp.concatenate(rows, axis=0)
 
 
 def window_body(me_ref, got_ref, send_ref):
     px, last_x = me_ref[0], me_ref[2]
-    total = total_of(got_ref, 4)
-    zero = jnp.zeros((5, 128), F32)
+    total, rest = total_of(got_ref, 4, None)
+    zero = jnp.zeros((4, 128), F32)
     early, late = window_rows([got_ref.at[jnp.clip(px + d, 0, last_x)] for d in range(-2, 3)], 0)
-    tile = jnp.concatenate(early + [total, zero] + late + [total, zero], axis=0)
+    tile = jnp.concatenate(early + [total, rest, zero] + late + [total, rest, zero], axis=0)
     for j in range(send_ref.shape[0]):
         send_ref[j] = tile
 
@@ -336,108 +336,189 @@
     (low_ref if x < 2 else high_ref)[x % 2] = value
 
 
+def half(low_ref, high_ref, x):
+    return (low_ref if x < 2 else high_ref)[x % 2]
+
+
+def products(left, right):
+    return [jnp.sum(a * b, axis=0) for a in left for b in right]
+
+
 def begin_body(*refs):
-    pieces, refs = refs[:5], refs[5:]
-    fixed, (low_ref, high_ref, z_ref, wlow_ref, whigh_ref, dots_ref) = refs[:6], refs[6:]
-    gamma = jnp.zeros((8, 128), F32)
-    delta = jnp.zeros((8, 128), F32)
+    pieces, fixed, (z_ref, wlow_ref, whigh_ref) = refs[:5], refs[5:11], refs[11:]
     for x, z, w in correct_rows(pieces, *fixed):
         z_ref[x] = z
         put(wlow_ref, whigh_ref, x, w)
-        r = (low_ref if x < 2 else high_ref)[x % 2]
-        gamma = gamma + jnp.sum(r * z, axis=0)
-        delta = delta + jnp.sum(w * z, axis=0)
-    dots_ref[...] = dots_of((gamma, delta))
-
-
-def scalars_of(total, old):
-    gamma, delta = total[:, 0:1], total[:, 1:2]
-    if old is None:
-        return gamma, gamma / delta, None
-    gamma_old, alpha_old = old[:, 0:1], old[:, 1:2]
-    beta = gamma / gamma_old
-    return gamma, gamma / (delta - beta * gamma / alpha_old), beta
-
-
-def as_row(gamma, alpha):
-    lane = lax.broadcasted_iota(jnp.int32, (1, 128), 1)
-    return jnp.where(lane == 0, gamma, jnp.where(lane == 1, alpha, 0.0))
-
-
-def total_of(got_ref, row):
+
+
+def second_body(*refs):
+    pieces, fixed, refs = refs[:5], refs[5:11], refs[11:]
+    low_ref, high_ref, z_ref, wlow_ref, whigh_ref, m_ref, nlow_ref, nhigh_ref, dots_ref = refs
+    sums = [jnp.zeros((8, 128), F32)] * 6
+    for x, m, n in correct_rows(pieces, *fixed):
+        m_ref[x] = m
+        put(nlow_ref, nhigh_ref, x, n)
+        here = products((half(low_ref, high_ref, x), half(wlow_ref, whigh_ref, x), n), (z_ref[x], m))
+        sums = [a + b for a, b in zip(sums, here)]
+    dots_ref[...] = dots_of(sums)
+
+
+def fourth_body(*refs):
+    pieces, fixed, refs = refs[:5], refs[5:11], refs[11:]
+    z_ref, wlow_ref, whigh_ref, r_ref, s_ref, q_ref, t_ref, m_ref, n_ref, dots_ref = refs
+    sums = [jnp.zeros((8, 128), F32)] * 15
+    for x, m, n in correct_rows(pieces, *fixed):
+        m_ref[x] = m
+        n_ref[x] = n
+        here = products((r_ref[x], half(wlow_ref, whigh_ref, x), s_ref[x], n, t_ref[x]), (z_ref[x], m, q_ref[x]))
+        sums = [a + b for a, b in zip(sums, here)]
+    dots_ref[...] = dots_of(sums)
+
+
+def two_sum(a, b):
+    total = a + b
+    part = total - a
+    return total, (a - (total - part)) + (b - part)
+
+
+def split(a):
+    wide = a * 4097.0
+    high = wide - (wide - a)
+    return high, a - high
+
+
+def two_product(a, b):
+    product = a * b
+    a_high, a_low = split(a)
+    b_high, b_low = split(b)
+    return product, a_low * b_low - (((product - a_high * b_high) - a_low * b_high) - a_high * b_low)
+
+
+def pair_add(a, b):
+    total, rest = two_sum(a[0], b[0])
+    return two_sum(total, rest + (a[1] + b[1]))
+
+
+def pair_scale(a, factor):
+    product, rest = two_product(a[0], factor)
+    return two_sum(product, rest + a[1] * factor)
+
+
+def pair_times(a, b):
+    product, rest = two_product(a[0], b[0])
+    return two_sum(product, rest + (a[0] * b[1] + a[1] * b[0]))
+
+
+def total_of(got_ref, row, rest_row):
     total = got_ref[0, row : row + 1, :]
+    rest = jnp.zeros((1, 128), F32) if rest_row is None else got_ref[0, rest_row : rest_row + 1, :]
     for j in range(1, got_ref.shape[0]):
-        total = total + got_ref[j, row : row + 1, :]
-    return total
-
-
-def step_body(first, me_ref, got_ref, coef_ref, smooth_ref, remain_ref, inverse_ref, scale_ref, offset_ref,
-              z_ref, wlow_ref, whigh_ref, *refs):
-    if first:
-        low_ref, high_ref = refs[:2]
-        refs = refs[2:]
-        old = None
-    else:
-        x_ref, r_ref, p_ref, s_ref, q_ref, t_ref, old_ref = refs[:7]
-        refs = refs[7:]
-        old = old_ref[...]
-    zo_ref, wolow_ref, wohigh_ref, xo_ref, ro_ref, po_ref, so_ref, qo_ref, to_ref, dots_ref, keep_ref = refs
-    gamma, alpha, beta = scalars_of(total_of(got_ref, 10), old)
-    keep_ref[...] = as_row(gamma, alpha)
-    alpha3 = jnp.broadcast_to(alpha, (8, 128))[None]
-    beta3 = None if first else jnp.broadcast_to(beta, (8, 128))[None]
-    gamma_sum = jnp.zeros((8, 128), F32)
-    delta_sum = jnp.zeros((8, 128), F32)
+        total, lost = two_sum(total, got_ref[j, row : row + 1, :])
+        rest = rest + lost
+        if rest_row is not None:
+            rest = rest + got_ref[j, rest_row : rest_row + 1, :]
+    return total, rest
+
+
+def pairs_of(got_ref, row, rest_row, count):
+    total, rest = total_of(got_ref, row, rest_row)
+    total, rest = two_sum(total, rest)
+    return [
+        (jnp.broadcast_to(total[:, k : k + 1], (1, 128)), jnp.broadcast_to(rest[:, k : k + 1], (1, 128)))
+        for k in range(count)
+    ]
+
+
+def form(table, left, weights):
+    out = None
+    for i, row in enumerate(left):
+        for j, entry in enumerate(table[row]):
+            factor = None
+            for w in (weights[i], weights[j]):
+                if w is not None:
+                    factor = w if factor is None else pair_times(factor, w)
+            term = entry if factor is None else pair_times(entry, factor)
+            out = term if out is None else pair_add(out, term)
+    return out[0] + out[1]
+
+
+def tiled(row):
+    return jnp.broadcast_to(row, (8, 128))[None]
+
+
+def negated(pair):
+    return -pair[0], -pair[1]
+
+
+def merge_body(me_ref, got_ref, *refs):
     py, last_y = me_ref[1], me_ref[3]
     pieces = [got_ref.at[jnp.clip(py + d, 0, last_y)] for d in range(-2, 3)]
-    fixed = (coef_ref, smooth_ref, remain_ref, inverse_ref, scale_ref, offset_ref)
-    for x, m, n in correct_rows(pieces, *fixed):
-        z = z_ref[x]
-        w = (wlow_ref if x < 2 else whigh_ref)[x % 2]
-        if first:
-            p, s, q, t = z, w, m, n
-            r = (low_ref if x < 2 else high_ref)[x % 2]
-            xo_ref[x] = alpha3 * p
-        else:
-            p, s, q, t = z + beta3 * p_ref[x], w + beta3 * s_ref[x], m + beta3 * q_ref[x], n + beta3 * t_ref[x]
-            r = r_ref[x]
-            xo_ref[x] = x_ref[x] + alpha3 * p
-        r = r - alpha3 * s
-        z = z - alpha3 * q
-        w = w - alpha3 * t
+    fixed, refs = refs[:6], refs[6:]
+    low_ref, high_ref, z_ref, wlow_ref, whigh_ref, m_ref, nlow_ref, nhigh_ref = refs[:8]
+    zo_ref, wolow_ref, wohigh_ref, xo_ref, ro_ref, po_ref, so_ref, qo_ref, to_ref, keep_ref = refs[8:]
+    sums = pairs_of(got_ref, 10, 11, 6)
+    table = [sums[0:2], sums[2:4], sums[4:6]]
+    gamma0 = table[0][0][0]
+    alpha0 = gamma0 / table[1][0][0]
+    weights = (None, negated((alpha0, jnp.zeros_like(alpha0))))
+    gamma1 = form(table, (0, 1), weights)
+    delta1 = form(table, (1, 2), weights)
+    beta1 = gamma1 / gamma0
+    alpha1 = gamma1 / (delta1 - beta1 * gamma1 / alpha0)
+    lane = lax.broadcasted_iota(jnp.int32, (1, 128), 1)
+    keep_ref[...] = jnp.where(lane == 0, gamma1, jnp.where(lane == 1, alpha1, 0.0))
+    alpha0, alpha1, beta1 = tiled(alpha0), tiled(alpha1), tiled(beta1)
+    for x, k, l in correct_rows(pieces, *fixed):
+        z0, w0 = z_ref[x], half(wlow_ref, whigh_ref, x)
+        m0, n0 = m_ref[x], half(nlow_ref, nhigh_ref, x)
+        z1, w1 = z0 - alpha0 * m0, w0 - alpha0 * n0
+        p, s = z1 + beta1 * z0, w1 + beta1 * w0
+        q = (m0 - alpha0 * k) + beta1 * m0
+        t = (n0 - alpha0 * l) + beta1 * n0
+        xo_ref[x] = alpha0 * z0 + alpha1 * p
+        ro_ref[x] = (half(low_ref, high_ref, x) - alpha0 * w0) - alpha1 * s
+        zo_ref[x] = z1 - alpha1 * q
+        put(wolow_ref, wohigh_ref, x, w1 - alpha1 * t)
         po_ref[x], so_ref[x], qo_ref[x], to_ref[x] = p, s, q, t
-        ro_ref[x], zo_ref[x] = r, z
-        put(wolow_ref, wohigh_ref, x, w)
-        gamma_sum = gamma_sum + jnp.sum(r * z, axis=0)
-        delta_sum = delta_sum + jnp.sum(w * z, axis=0)
-    dots_ref[...] = dots_of((gamma_sum, delta_sum))
 
 
 def spread_dots_body(dots_ref, send_ref):
-    tile = jnp.broadcast_to(dots_ref[...], (8, 128))
+    tile = jnp.concatenate([dots_ref[...], jnp.zeros((7, 128), F32)], axis=0)
     for j in range(send_ref.shape[0]):
         send_ref[j] = tile
 
 
 def sum_dots_body(got_ref, send_ref):
-    total = got_ref[0]
-    for j in range(1, got_ref.shape[0]):
-        total = total + got_ref[j]
+    total, rest = total_of(got_ref, 0, None)
+    tile = jnp.concatenate([total, rest, jnp.zeros((6, 128), F32)], axis=0)
     for j in range(send_ref.shape[0]):
-        send_ref[j] = total
-
-
-def finish_body(got_ref, z_ref, wlow_ref, whigh_ref, x_ref, r_ref, p_ref, s_ref, old_ref, xo_ref, ro_ref,
-                xs_ref, rs_ref):
-    gamma, alpha, beta = scalars_of(total_of(got_ref, 0), old_ref[...])
-    alpha3 = jnp.broadcast_to(alpha, (8, 128))[None]
-    beta3 = jnp.broadcast_to(beta, (8, 128))[None]
+        send_ref[j] = tile
+
+
+def finish_body(got_ref, z_ref, wlow_ref, whigh_ref, m_ref, n_ref, x_ref, r_ref, p_ref, s_ref, q_ref, t_ref, keep_ref,
+                xo_ref, ro_ref, xs_ref, rs_ref):
+    sums = pairs_of(got_ref, 0, 1, 15)
+    table = [sums[3 * k : 3 * k + 3] for k in range(5)]
+    keep = keep_ref[...]
+    gamma1 = jnp.broadcast_to(keep[:, 0:1], (1, 128))
+    alpha1 = jnp.broadcast_to(keep[:, 1:2], (1, 128))
+    gamma2 = table[0][0][0]
+    beta2 = gamma2 / gamma1
+    alpha2 = gamma2 / (table[1][0][0] - beta2 * gamma2 / alpha1)
+    weights = (None, (-alpha2, jnp.zeros_like(alpha2)), two_product(-alpha2, beta2))
+    gamma3 = form(table, (0, 1, 2), weights)
+    delta3 = form(table, (1, 3, 4), weights)
+    beta3 = gamma3 / gamma2
+    alpha3 = gamma3 / (delta3 - beta3 * gamma3 / alpha2)
+    alpha2, beta2, alpha3, beta3 = tiled(alpha2), tiled(beta2), tiled(alpha3), tiled(beta3)
     for x in range(4):
-        w = (wlow_ref if x < 2 else whigh_ref)[x % 2]
-        p = z_ref[x] + beta3 * p_ref[x]
-        s = w + beta3 * s_ref[x]
-        xs_ref[pl.ds(64 * x, 64), :] = (x_ref[x] + alpha3 * p).reshape(64, 128)
-        rs_ref[pl.ds(64 * x, 64), :] = (r_ref[x] - alpha3 * s).reshape(64, 128)
+        z, w, q1, t1 = z_ref[x], half(wlow_ref, whigh_ref, x), q_ref[x], t_ref[x]
+        p2, s2 = z + beta2 * p_ref[x], w + beta2 * s_ref[x]
+        q2, t2 = m_ref[x] + beta2 * q1, n_ref[x] + beta2 * t1
+        p3 = (z - alpha2 * q2) + beta3 * p2
+        s3 = (w - alpha2 * t2) + beta3 * s2
+        xs_ref[pl.ds(64 * x, 64), :] = ((x_ref[x] + alpha2 * p2) + alpha3 * p3).reshape(64, 128)
+        rs_ref[pl.ds(64 * x, 64), :] = ((r_ref[x] - alpha2 * s2) - alpha3 * s3).reshape(64, 128)
     for x in range(4):
         for s in range(8):
             part = slice(s * 128, (s + 1) * 128)
@@ -479,40 +560,51 @@
     inverse, scale, offset = call(
         setup_body, [(8, 12, 8, 128), (6, 10, 8, 128), (10, 14, 8, 128)], me, low, high, xlow, xhigh, ylow, yhigh
     )
-    mid = (6, 10, 8, 128)
+    mid, dots = (6, 10, 8, 128), (1, 128)
     smooth, remain, send = call(
-        bodied(restrict_body, True), [mid, mid, (24, 128)],
+        bodied(restrict_body, 0), [mid, mid, (24, 128)],
         low, high, xlow, xhigh, ylow, yhigh, inverse, offset, coarse_diag, coarse_link, scalars=0,
     )
-    send, = call(window_first_body, [(112, 128)], *around(send, "px"), scalars=0)
+    send, = call(window_near_body, [(112, 128)], *around(send, "px"), scalars=0)
     pieces = around(send, "py")
     coef, = call(coarse_setup_body, [(7, 8, 16, 128)], me, *pieces)
     fixed = (inverse, scale, offset)
-    z, wlow, whigh, dots = call(
-        begin_body, [field, two, two, (1, 128)], *pieces, coef, smooth, remain, *fixed, low, high, scalars=0
+    z, wlow, whigh = call(begin_body, [field, two, two], *pieces, coef, smooth, remain, *fixed, scalars=0)
+
+    def restricted(mode, low, high, outs, *more):
+        xlow, xhigh = both_ways(low, high, "px")
+        first, last = call(pack_body, [(8, 2, 8, 128)] * 2, low, high, xlow, xhigh, scalars=0)
+        ylow, yhigh = both_ways(first, last, "py")
+        return call(
+            bodied(restrict_body, mode), [mid, mid, outs],
+            low, high, xlow, xhigh, ylow, yhigh, inverse, offset, *more, scalars=0,
+        )
+
+    def near_window(send):
+        send, = call(window_near_body, [(32, 128)], *around(send, "px"), scalars=0)
+        return around(send, "py")
+
+    smooth, remain, send = restricted(1, wlow, whigh, (8, 128))
+    m, nlow, nhigh, sums = call(
+        second_body, [field, two, two, dots],
+        *near_window(send), coef, smooth, remain, *fixed, low, high, z, wlow, whigh, scalars=0,
     )
-    state = None
-    for iteration in range(ITERS - 1):
-        xlow, xhigh = both_ways(wlow, whigh, "px")
-        first, last = call(pack_body, [(8, 2, 8, 128)] * 2, wlow, whigh, xlow, xhigh, scalars=0)
-        ylow, yhigh = both_ways(first, last, "py")
-        smooth, remain, send = call(
-            bodied(restrict_body, False), [mid, mid, (count_x, 8, 128)],
-            wlow, whigh, xlow, xhigh, ylow, yhigh, inverse, offset, dots, scalars=0,
-        )
-        send, = call(window_body, [(count_y, 32, 128)], me, gather(send, "px"))
-        got = gather(send, "py")
-        more = (low, high) if state is None else state
-        z, wlow, whigh, x, r, p, s, q, t, dots, keep = call(
-            bodied(step_body, state is None), [field, two, two] + [field] * 6 + [(1, 128)] * 2,
-            me, got, coef, smooth, remain, *fixed, z, wlow, whigh, *more,
-        )
-        state = (x, r, p, s, q, t, keep)
-    send, = call(spread_dots_body, [(count_x, 8, 128)], dots, scalars=0)
+    smooth, remain, send = restricted(2, nlow, nhigh, (count_x, 8, 128), sums)
+    send, = call(window_body, [(count_y, 32, 128)], me, gather(send, "px"))
+    z, wlow, whigh, x, r, p, s, q, t, keep = call(
+        merge_body, [field, two, two] + [field] * 6 + [dots],
+        me, gather(send, "py"), coef, smooth, remain, *fixed, low, high, z, wlow, whigh, m, nlow, nhigh,
+    )
+    smooth, remain, send = restricted(1, wlow, whigh, (8, 128))
+    m, n, sums = call(
+        fourth_body, [field, field, dots],
+        *near_window(send), coef, smooth, remain, *fixed, z, wlow, whigh, r, s, q, t, scalars=0,
+    )
+    send, = call(spread_dots_body, [(count_x, 8, 128)], sums, scalars=0)
     send, = call(sum_dots_body, [(count_y, 8, 128)], gather(send, "px"), scalars=0)
-    got = gather(send, "py")
     return tuple(call(
-        finish_body, [right_side.shape] * 2, got, z, wlow, whigh, x, r, p, s, keep,
+        finish_body, [right_side.shape] * 2,
+        gather(send, "py"), z, wlow, whigh, m, n, x, r, p, s, q, t, keep,
         scalars=0, scratch=[pltpu.VMEM((256, 128), F32)] * 2,
     ))
 

time: 198 us -> 182 us (0.919)
  blocking collectives: 106 us -> 48.9 us
  starting transfers between devices: 29.8 us -> 54.7 us
  waiting for transfers between devices: 43.8 us -> 63.1 us
  Pallas kernels: 12.2 us -> 9.48 us
    all_to_all x8 -> x4, blocking collectives: 106 us -> 48.9 us  [gather(): return lax.all_to_all(value, axis, 0, 0)]
    ppermute x24 -> x40, starting transfers between devices: 29.8 us -> 54.7 us  [both_ways(): return (lax.ppermute(high, axis, up), lax.ppermute(low, axis, down))]
    ppermute x24 -> x40, waiting for transfers between devices: 43.8 us -> 63.1 us  [both_ways(): return (lax.ppermute(high, axis, up), lax.ppermute(low, axis, down))]
    pallas_call x22, Pallas kernels: 12.2 us -> 9.48 us  [call(): pl.pallas_call(body, out_shape=[jax.ShapeDtypeStruct(shape, F32) for shap...]
  transfers between devices with their start and end apart: 24 -> 40, of which waited for: 22 -> 32; matrix products, arithmetic and copies ran while one was open for 0% -> 0% of each run, Pallas kernels for 0% -> 0%
where the time goes in v3:
time: 182 us; the launch traced here: 181 us
  waiting for transfers between devices  63.1 us (35%)
  starting transfers between devices  54.7 us (30%)
  blocking collectives  48.9 us (27%)
  Pallas kernels  9.48 us (5%)
  local copies, waits for them, and re-layouts  3.38 us (2%)
    ppermute x40, waiting for transfers between devices, both_ways(): return (lax.ppermute(high, axis, up), lax.ppermute(low, axis, down))  63.1 us
    ppermute x40, starting transfers between devices, both_ways(): return (lax.ppermute(high, axis, up), lax.ppermute(low, axis, down))  54.7 us
    all_to_all x4, blocking collectives, gather(): return lax.all_to_all(value, axis, 0, 0)  48.9 us
    pallas_call x22, Pallas kernels, call(): pl.pallas_call(body, out_shape=[jax.ShapeDtypeStruct(shape, F32) for shap...  9.48 us
  transfers between devices with their start and end apart: 40, of which 32 were waited for; matrix products, arithmetic and copies ran while one was open for 0% of the time, Pallas kernels for 0%

profile of v3, /device:TPU:8, one launch (start us, length us, event | category | flops | bytes accessed | tf_op | source)
XLA Modules:
  0.0 180.6 jit_solution(12030212532820074781)
XLA Ops:
  1.5 0.9 copy-done.1
  3.4 5.3 %collective-permute-start.1 = (f32[7,8,8,128]{3,2,1,0:T(8,128)S(1)}, f32[7,8,8,128]{3,2,1,0:T(8,128)S(1)}, u32[]{:S(2)}, u32[]{:S(2)}) collective-permute-start(f32[7,8,8,128]{3,2,1,0:T(8,128)S(1)} %bitcast.4), channel_id=1, source_target_pairs={{16,0},{32,16},{48,32},{64,48},{80,64},{96,80},{112,96},{128,112},... | collective-permute-start | bytes 688136 | tf_op jit(solution)/shard_map/ppermute | solution.py:544
  8.8 3.7 %collective-permute-done.xlow_ref.refs_2_ = f32[7,8,8,128]{3,2,1,0:T(8,128)S(1)} collective-permute-done((f32[7,8,8,128]{3,2,1,0:T(8,128)S(1)}, f32[7,8,8,128]{3,2,1,0:T(8,128)S(1)}, u32[]{:S(2)}, u32[]{:S(2)}) %collective-permute-start) | collective-permute-done | bytes 229408 | tf_op jit(solution)/shard_map/ppermute | solution.py:544
  12.5 1.7 collective-permute-start.2
  14.7 4.7 %collective-permute-done.2.ylow_ref.refs_4_ = f32[62,8,128]{2,1,0:T(8,128)S(1)} collective-permute-done((f32[62,8,128]{2,1,0:T(8,128)S(1)}, f32[62,8,128]{2,1,0:T(8,128)S(1)}, u32[]{:S(2)}, u32[]{:S(2)}) %collective-permute-start.2) | collective-permute-done | bytes 253984 | tf_op jit(solution)/shard_map/ppermute | solution.py:544
  19.4 1.3 collective-permute-done.3.yhigh_ref.refs_5_
  22.5 4.7 %collective-permute-start.7 = (f32[24,128]{1,0:T(8,128)S(1)}, f32[24,128]{1,0:T(8,128)S(1)}, u32[]{:S(2)}, u32[]{:S(2)}) collective-permute-start(f32[24,128]{1,0:T(8,128)S(1)} %get-tuple-element.53.refs_2_), channel_id=1, source_target_pairs={{32,0},{48,16},{64,32},{80,48},{96,64},{112,80},{128,96},{144,112}... | collective-permute-start | bytes 36872 | tf_op jit(solution)/shard_map/ppermute | solution.py:544
  29.0 2.9 %collective-permute-done.5.refs_1_ = f32[24,128]{1,0:T(8,128)S(1)} collective-permute-done((f32[24,128]{1,0:T(8,128)S(1)}, f32[24,128]{1,0:T(8,128)S(1)}, u32[]{:S(2)}, u32[]{:S(2)}) %collective-permute-start.5) | collective-permute-done | bytes 12320 | tf_op jit(solution)/shard_map/ppermute | solution.py:544
  32.7 6.6 %collective-permute-start.11 = (f32[112,128]{1,0:T(8,128)S(1)}, f32[112,128]{1,0:T(8,128)S(1)}, u32[]{:S(2)}, u32[]{:S(2)}) collective-permute-start(f32[112,128]{1,0:T(8,128)S(1)} %shard_map.72.refs_2_), channel_id=1, source_target_pairs={{2,0},{3,1},{4,2},{5,3},{6,4},{7,5},{8,6},{9,7},{10,8},{11,9},{12,... | collective-permute-start | bytes 172040 | tf_op jit(solution)/shard_map/ppermute | solution.py:544
  39.3 2.0 %collective-permute-start.9 = (f32[112,128]{1,0:T(8,128)S(1)}, f32[112,128]{1,0:T(8,128)S(1)}, u32[]{:S(2)}, u32[]{:S(2)}) collective-permute-start(f32[112,128]{1,0:T(8,128)S(1)} %shard_map.72.refs_2_), channel_id=1, source_target_pairs={{0,1},{1,2},{2,3},{3,4},{4,5},{5,6},{6,7},{7,8},{8,9},{9,10},{10,1... | collective-permute-start | bytes 172040 | tf_op jit(solution)/shard_map/ppermute | solution.py:544
  41.3 2.1 %collective-permute-done.10.refs_3_ = f32[112,128]{1,0:T(8,128)S(1)} collective-permute-done((f32[112,128]{1,0:T(8,128)S(1)}, f32[112,128]{1,0:T(8,128)S(1)}, u32[]{:S(2)}, u32[]{:S(2)}) %collective-permute-start.10) | collective-permute-done | bytes 57376 | tf_op jit(solution)/shard_map/ppermute | solution.py:544
  43.6 5.4 %collective-permute-done.8.refs_0_ = f32[112,128]{1,0:T(8,128)S(1)} collective-permute-done((f32[112,128]{1,0:T(8,128)S(1)}, f32[112,128]{1,0:T(8,128)S(1)}, u32[]{:S(2)}, u32[]{:S(2)}) %collective-permute-start.8) | collective-permute-done | bytes 57376 | tf_op jit(solution)/shard_map/ppermute | solution.py:544
  51.1 1.4 collective-permute-done.13.xhigh_ref.refs_3_
  52.5 3.0 %collective-permute-done.12.xlow_ref.refs_2_ = f32[2,8,8,128]{3,2,1,0:T(8,128)S(1)} collective-permute-done((f32[2,8,8,128]{3,2,1,0:T(8,128)S(1)}, f32[2,8,8,128]{3,2,1,0:T(8,128)S(1)}, u32[]{:S(2)}, u32[]{:S(2)}) %collective-permute-start.12) | collective-permute-done | bytes 65568 | tf_op jit(solution)/shard_map/ppermute | solution.py:544
  55.6 2.0 %collective-permute-start.15 = (f32[8,2,8,128]{3,2,1,0:T(8,128)S(1)}, f32[8,2,8,128]{3,2,1,0:T(8,128)S(1)}, u32[]{:S(2)}, u32[]{:S(2)}) collective-permute-start(f32[8,2,8,128]{3,2,1,0:T(8,128)S(1)} %get-tuple-element.60), channel_id=1, source_target_pairs={{1,0},{2,1},{3,2},{4,3},{5,4},{6,5},{7,6},{8,7},{9,8},{10,9},{11,1... | collective-permute-start | bytes 196616 | tf_op jit(solution)/shard_map/ppermute | solution.py:544
  57.6 2.2 %collective-permute-done.14.refs_4_ = f32[8,2,8,128]{3,2,1,0:T(8,128)S(1)} collective-permute-done((f32[8,2,8,128]{3,2,1,0:T(8,128)S(1)}, f32[8,2,8,128]{3,2,1,0:T(8,128)S(1)}, u32[]{:S(2)}, u32[]{:S(2)}) %collective-permute-start.14) | collective-permute-done | bytes 65568 | tf_op jit(solution)/shard_map/ppermute | solution.py:544
  61.1 2.0 %collective-permute-start.16 = (f32[8,128]{1,0:T(8,128)S(1)}, f32[8,128]{1,0:T(8,128)S(1)}, u32[]{:S(2)}, u32[]{:S(2)}) collective-permute-start(f32[8,128]{1,0:T(8,128)S(1)} %get-tuple-element.61.refs_2_), channel_id=1, source_target_pairs={{0,32},{16,48},{32,64},{48,80},{64,96},{80,112},{96,128},{112,144}... | collective-permute-start | bytes 12296 | tf_op jit(solution)/shard_map/ppermute | solution.py:544
  63.1 1.1 collective-permute-done.19.refs_4_
  64.9 1.1 collective-permute-done.16.refs_0_
  65.9 7.5 %collective-permute-start.23 = (f32[32,128]{1,0:T(8,128)S(1)}, f32[32,128]{1,0:T(8,128)S(1)}, u32[]{:S(2)}, u32[]{:S(2)}) collective-permute-start(f32[32,128]{1,0:T(8,128)S(1)} %shard_map.77.refs_2_), channel_id=1, source_target_pairs={{2,0},{3,1},{4,2},{5,3},{6,4},{7,5},{8,6},{9,7},{10,8},{11,9},{12,... | collective-permute-start | bytes 49160 | tf_op jit(solution)/shard_map/ppermute | solution.py:544
  73.4 2.0 %collective-permute-start.21 = (f32[32,128]{1,0:T(8,128)S(1)}, f32[32,128]{1,0:T(8,128)S(1)}, u32[]{:S(2)}, u32[]{:S(2)}) collective-permute-start(f32[32,128]{1,0:T(8,128)S(1)} %shard_map.77.refs_2_), channel_id=1, source_target_pairs={{0,1},{1,2},{2,3},{3,4},{4,5},{5,6},{6,7},{7,8},{8,9},{9,10},{10,1... | collective-permute-start | bytes 49160 | tf_op jit(solution)/shard_map/ppermute | solution.py:544
  75.5 1.7 collective-permute-done.22.refs_3_
  77.2 5.6 %collective-permute-done.20.refs_0_ = f32[32,128]{1,0:T(8,128)S(1)} collective-permute-done((f32[32,128]{1,0:T(8,128)S(1)}, f32[32,128]{1,0:T(8,128)S(1)}, u32[]{:S(2)}, u32[]{:S(2)}) %collective-permute-start.20) | collective-permute-done | bytes 16416 | tf_op jit(solution)/shard_map/ppermute | solution.py:544
  82.8 1.0 shard_map.78
  84.3 1.4 collective-permute-done.25.xhigh_ref.refs_3_
  85.7 3.0 %collective-permute-done.24.xlow_ref.refs_2_ = f32[2,8,8,128]{3,2,1,0:T(8,128)S(1)} collective-permute-done((f32[2,8,8,128]{3,2,1,0:T(8,128)S(1)}, f32[2,8,8,128]{3,2,1,0:T(8,128)S(1)}, u32[]{:S(2)}, u32[]{:S(2)}) %collective-permute-start.24) | collective-permute-done | bytes 65568 | tf_op jit(solution)/shard_map/ppermute | solution.py:544
  88.8 2.0 %collective-permute-start.27 = (f32[8,2,8,128]{3,2,1,0:T(8,128)S(1)}, f32[8,2,8,128]{3,2,1,0:T(8,128)S(1)}, u32[]{:S(2)}, u32[]{:S(2)}) collective-permute-start(f32[8,2,8,128]{3,2,1,0:T(8,128)S(1)} %get-tuple-element.68), channel_id=1, source_target_pairs={{1,0},{2,1},{3,2},{4,3},{5,4},{6,5},{7,6},{8,7},{9,8},{10,9},{11,1... | collective-permute-start | bytes 196616 | tf_op jit(solution)/shard_map/ppermute | solution.py:544
  90.8 2.2 %collective-permute-done.26.refs_4_ = f32[8,2,8,128]{3,2,1,0:T(8,128)S(1)} collective-permute-done((f32[8,2,8,128]{3,2,1,0:T(8,128)S(1)}, f32[8,2,8,128]{3,2,1,0:T(8,128)S(1)}, u32[]{:S(2)}, u32[]{:S(2)}) %collective-permute-start.26) | collective-permute-done | bytes 65568 | tf_op jit(solution)/shard_map/ppermute | solution.py:544
  93.7 10.8 %all_to_all.20.got_ref = f32[16,8,128]{2,1,0:T(8,128)S(1)} all-to-all(f32[16,8,128]{2,1,0:T(8,128)S(1)} %get-tuple-element.70), channel_id=1, replica_groups=mesh['px'=16,'py'=16] {'px'}, dimensions={0} | all-to-all | bytes 131072 | tf_op jit(solution)/shard_map/all_to_all | solution.py:552
  105.1 17.2 %all_to_all.21.got_ref = f32[16,32,128]{2,1,0:T(8,128)S(1)} all-to-all(f32[16,32,128]{2,1,0:T(8,128)S(1)} %shard_map.81), channel_id=1, replica_groups=mesh['px'=16,'py'=16] {'py'}, dimensions={0} | all-to-all | bytes 524288 | tf_op jit(solution)/shard_map/all_to_all | solution.py:552
  122.3 1.4 shard_map.82
  124.2 1.4 collective-permute-done.29.xhigh_ref.refs_3_
  125.6 3.0 %collective-permute-done.28.xlow_ref.refs_2_ = f32[2,8,8,128]{3,2,1,0:T(8,128)S(1)} collective-permute-done((f32[2,8,8,128]{3,2,1,0:T(8,128)S(1)}, f32[2,8,8,128]{3,2,1,0:T(8,128)S(1)}, u32[]{:S(2)}, u32[]{:S(2)}) %collective-permute-start.28) | collective-permute-done | bytes 65568 | tf_op jit(solution)/shard_map/ppermute | solution.py:544
  128.7 1.1 collective-permute-start.30
  129.8 1.0 collective-permute-start.31
  130.8 2.2 %collective-permute-done.30.refs_4_ = f32[8,2,8,128]{3,2,1,0:T(8,128)S(1)} collective-permute-done((f32[8,2,8,128]{3,2,1,0:T(8,128)S(1)}, f32[8,2,8,128]{3,2,1,0:T(8,128)S(1)}, u32[]{:S(2)}, u32[]{:S(2)}) %collective-permute-start.30) | collective-permute-done | bytes 65568 | tf_op jit(solution)/shard_map/ppermute | solution.py:544
  133.0 1.0 collective-permute-done.31.refs_5_
  135.2 2.0 %collective-permute-start.32 = (f32[8,128]{1,0:T(8,128)S(1)}, f32[8,128]{1,0:T(8,128)S(1)}, u32[]{:S(2)}, u32[]{:S(2)}) collective-permute-start(f32[8,128]{1,0:T(8,128)S(1)} %get-tuple-element.78.refs_2_), channel_id=1, source_target_pairs={{0,32},{16,48},{32,64},{48,80},{64,96},{80,112},{96,128},{112,144}... | collective-permute-start | bytes 12296 | tf_op jit(solution)/shard_map/ppermute | solution.py:544
  137.2 1.1 collective-permute-done.35.refs_4_
  138.9 1.1 collective-permute-done.32.refs_0_
  140.0 8.2 %collective-permute-start.39 = (f32[32,128]{1,0:T(8,128)S(1)}, f32[32,128]{1,0:T(8,128)S(1)}, u32[]{:S(2)}, u32[]{:S(2)}) collective-permute-start(f32[32,128]{1,0:T(8,128)S(1)} %shard_map.85.refs_2_), channel_id=1, source_target_pairs={{2,0},{3,1},{4,2},{5,3},{6,4},{7,5},{8,6},{9,7},{10,8},{11,9},{12,... | collective-permute-start | bytes 49160 | tf_op jit(solution)/shard_map/ppermute | solution.py:544
  148.2 2.0 %collective-permute-start.37 = (f32[32,128]{1,0:T(8,128)S(1)}, f32[32,128]{1,0:T(8,128)S(1)}, u32[]{:S(2)}, u32[]{:S(2)}) collective-permute-start(f32[32,128]{1,0:T(8,128)S(1)} %shard_map.85.refs_2_), channel_id=1, source_target_pairs={{0,1},{1,2},{2,3},{3,4},{4,5},{5,6},{6,7},{7,8},{8,9},{9,10},{10,1... | collective-permute-start | bytes 49160 | tf_op jit(solution)/shard_map/ppermute | solution.py:544
  150.2 1.7 collective-permute-done.38.refs_3_
  151.9 5.6 %collective-permute-done.36.refs_0_ = f32[32,128]{1,0:T(8,128)S(1)} collective-permute-done((f32[32,128]{1,0:T(8,128)S(1)}, f32[32,128]{1,0:T(8,128)S(1)}, u32[]{:S(2)}, u32[]{:S(2)}) %collective-permute-start.36) | collective-permute-done | bytes 16416 | tf_op jit(solution)/shard_map/ppermute | solution.py:544
  157.6 1.1 shard_map.86
  158.7 11.0 %all_to_all.22.got_ref = f32[16,8,128]{2,1,0:T(8,128)S(1)} all-to-all(f32[16,8,128]{2,1,0:T(8,128)S(1)} %shard_map.87), channel_id=1, replica_groups=mesh['px'=16,'py'=16] {'px'}, dimensions={0} | all-to-all | bytes 131072 | tf_op jit(solution)/shard_map/all_to_all | solution.py:552
  169.7 9.9 %all_to_all.23.got_ref = f32[16,8,128]{2,1,0:T(8,128)S(1)} all-to-all(f32[16,8,128]{2,1,0:T(8,128)S(1)} %shard_map.88), channel_id=1, replica_groups=mesh['px'=16,'py'=16] {'py'}, dimensions={0} | all-to-all | bytes 131072 | tf_op jit(solution)/shard_map/all_to_all | solution.py:552
  179.6 1.0 shard_map.89
  (70 shorter events, 15.3 us)
Async XLA Ops:
  0.6 0.9 copy-start
  1.5 0.9 copy-start.1
  2.4 0.9 copy-start.2
  3.4 9.0 %collective-permute-start = (f32[7,8,8,128]{3,2,1,0:T(8,128)S(1)}, f32[7,8,8,128]{3,2,1,0:T(8,128)S(1)}, u32[]{:S(2)}, u32[]{:S(2)}) collective-permute-start(f32[7,8,8,128]{3,2,1,0:T(8,128)S(1)} %bitcast.10), channel_id=1, source_target_pairs={{0,16},{16,32},{32,48},{48,64},{64,80},{80,96},{96,112},{112,128},... | collective-permute-start | bytes 688136 | tf_op jit(solution)/shard_map/ppermute | solution.py:544
  3.4 9.0 %collective-permute-start.1 = (f32[7,8,8,128]{3,2,1,0:T(8,128)S(1)}, f32[7,8,8,128]{3,2,1,0:T(8,128)S(1)}, u32[]{:S(2)}, u32[]{:S(2)}) collective-permute-start(f32[7,8,8,128]{3,2,1,0:T(8,128)S(1)} %bitcast.4), channel_id=1, source_target_pairs={{16,0},{32,16},{48,32},{64,48},{80,64},{96,80},{112,96},{128,112},... | collective-permute-start | bytes 688136 | tf_op jit(solution)/shard_map/ppermute | solution.py:544
  12.5 6.9 %collective-permute-start.2 = (f32[62,8,128]{2,1,0:T(8,128)S(1)}, f32[62,8,128]{2,1,0:T(8,128)S(1)}, u32[]{:S(2)}, u32[]{:S(2)}) collective-permute-start(f32[62,8,128]{2,1,0:T(8,128)S(1)} %get-tuple-element.49), channel_id=1, source_target_pairs={{0,1},{1,2},{2,3},{3,4},{4,5},{5,6},{6,7},{7,8},{8,9},{9,10},{10,1... | collective-permute-start | bytes 761864 | tf_op jit(solution)/shard_map/ppermute | solution.py:544
  14.1 6.5 %collective-permute-start.3 = (f32[62,8,128]{2,1,0:T(8,128)S(1)}, f32[62,8,128]{2,1,0:T(8,128)S(1)}, u32[]{:S(2)}, u32[]{:S(2)}) collective-permute-start(f32[62,8,128]{2,1,0:T(8,128)S(1)} %get-tuple-element.50), channel_id=1, source_target_pairs={{1,0},{2,1},{3,2},{4,3},{5,4},{6,5},{7,6},{8,7},{9,8},{10,9},{11,1... | collective-permute-start | bytes 761864 | tf_op jit(solution)/shard_map/ppermute | solution.py:544
  20.7 0.7 copy-start.3
  21.3 0.7 copy-start.4
  22.5 6.1 %collective-permute-start.7 = (f32[24,128]{1,0:T(8,128)S(1)}, f32[24,128]{1,0:T(8,128)S(1)}, u32[]{:S(2)}, u32[]{:S(2)}) collective-permute-start(f32[24,128]{1,0:T(8,128)S(1)} %get-tuple-element.53.refs_2_), channel_id=1, source_target_pairs={{32,0},{48,16},{64,32},{80,48},{96,64},{112,80},{128,96},{144,112}... | collective-permute-start | bytes 36872 | tf_op jit(solution)/shard_map/ppermute | solution.py:544
  27.2 1.8 collective-permute-start.6
  27.6 4.3 %collective-permute-start.5 = (f32[24,128]{1,0:T(8,128)S(1)}, f32[24,128]{1,0:T(8,128)S(1)}, u32[]{:S(2)}, u32[]{:S(2)}) collective-permute-start(f32[24,128]{1,0:T(8,128)S(1)} %get-tuple-element.53.refs_2_), channel_id=1, source_target_pairs={{0,16},{16,32},{32,48},{48,64},{64,80},{80,96},{96,112},{112,128},... | collective-permute-start | bytes 36872 | tf_op jit(solution)/shard_map/ppermute | solution.py:544
  27.7 5.0 %collective-permute-start.4 = (f32[24,128]{1,0:T(8,128)S(1)}, f32[24,128]{1,0:T(8,128)S(1)}, u32[]{:S(2)}, u32[]{:S(2)}) collective-permute-start(f32[24,128]{1,0:T(8,128)S(1)} %get-tuple-element.53.refs_2_), channel_id=1, source_target_pairs={{0,32},{16,48},{32,64},{48,80},{64,96},{80,112},{96,128},{112,144}... | collective-permute-start | bytes 36872 | tf_op jit(solution)/shard_map/ppermute | solution.py:544
  32.7 8.6 %collective-permute-start.11 = (f32[112,128]{1,0:T(8,128)S(1)}, f32[112,128]{1,0:T(8,128)S(1)}, u32[]{:S(2)}, u32[]{:S(2)}) collective-permute-start(f32[112,128]{1,0:T(8,128)S(1)} %shard_map.72.refs_2_), channel_id=1, source_target_pairs={{2,0},{3,1},{4,2},{5,3},{6,4},{7,5},{8,6},{9,7},{10,8},{11,9},{12,... | collective-permute-start | bytes 172040 | tf_op jit(solution)/shard_map/ppermute | solution.py:544
  39.3 4.2 %collective-permute-start.10 = (f32[112,128]{1,0:T(8,128)S(1)}, f32[112,128]{1,0:T(8,128)S(1)}, u32[]{:S(2)}, u32[]{:S(2)}) collective-permute-start(f32[112,128]{1,0:T(8,128)S(1)} %shard_map.72.refs_2_), channel_id=1, source_target_pairs={{1,0},{2,1},{3,2},{4,3},{5,4},{6,5},{7,6},{8,7},{9,8},{10,9},{11,1... | collective-permute-start | bytes 172040 | tf_op jit(solution)/shard_map/ppermute | solution.py:544
  39.3 4.4 %collective-permute-start.9 = (f32[112,128]{1,0:T(8,128)S(1)}, f32[112,128]{1,0:T(8,128)S(1)}, u32[]{:S(2)}, u32[]{:S(2)}) collective-permute-start(f32[112,128]{1,0:T(8,128)S(1)} %shard_map.72.refs_2_), channel_id=1, source_target_pairs={{0,1},{1,2},{2,3},{3,4},{4,5},{5,6},{6,7},{7,8},{8,9},{9,10},{10,1... | collective-permute-start | bytes 172040 | tf_op jit(solution)/shard_map/ppermute | solution.py:544
  41.3 7.8 %collective-permute-start.8 = (f32[112,128]{1,0:T(8,128)S(1)}, f32[112,128]{1,0:T(8,128)S(1)}, u32[]{:S(2)}, u32[]{:S(2)}) collective-permute-start(f32[112,128]{1,0:T(8,128)S(1)} %shard_map.72.refs_2_), channel_id=1, source_target_pairs={{0,2},{1,3},{2,4},{3,5},{4,6},{5,7},{6,8},{7,9},{8,10},{9,11},{10,... | collective-permute-start | bytes 172040 | tf_op jit(solution)/shard_map/ppermute | solution.py:544
  50.6 1.9 %collective-permute-start.13 = (f32[2,8,8,128]{3,2,1,0:T(8,128)S(1)}, f32[2,8,8,128]{3,2,1,0:T(8,128)S(1)}, u32[]{:S(2)}, u32[]{:S(2)}) collective-permute-start(f32[2,8,8,128]{3,2,1,0:T(8,128)S(1)} %get-tuple-element.57.low_ref.refs_0_.refs_14_.refs_9_), channel_id=1, source_target_pairs={{16,0},{32,16},{48,32},{64,48},{80,64},{96,80},{112,96},{128,112},... | collective-permute-start | bytes 196616 | tf_op jit(solution)/shard_map/ppermute | solution.py:544
  50.6 4.9 %collective-permute-start.12 = (f32[2,8,8,128]{3,2,1,0:T(8,128)S(1)}, f32[2,8,8,128]{3,2,1,0:T(8,128)S(1)}, u32[]{:S(2)}, u32[]{:S(2)}) collective-permute-start(f32[2,8,8,128]{3,2,1,0:T(8,128)S(1)} %get-tuple-element.58.high_ref.refs_1_.refs_15_.refs_10_), channel_id=1, source_target_pairs={{0,16},{16,32},{32,48},{48,64},{64,80},{80,96},{96,112},{112,128},... | collective-permute-start | bytes 196616 | tf_op jit(solution)/shard_map/ppermute | solution.py:544
  55.5 4.3 %collective-permute-start.14 = (f32[8,2,8,128]{3,2,1,0:T(8,128)S(1)}, f32[8,2,8,128]{3,2,1,0:T(8,128)S(1)}, u32[]{:S(2)}, u32[]{:S(2)}) collective-permute-start(f32[8,2,8,128]{3,2,1,0:T(8,128)S(1)} %get-tuple-element.59), channel_id=1, source_target_pairs={{0,1},{1,2},{2,3},{3,4},{4,5},{5,6},{6,7},{7,8},{8,9},{9,10},{10,1... | collective-permute-start | bytes 196616 | tf_op jit(solution)/shard_map/ppermute | solution.py:544
  55.6 4.3 %collective-permute-start.15 = (f32[8,2,8,128]{3,2,1,0:T(8,128)S(1)}, f32[8,2,8,128]{3,2,1,0:T(8,128)S(1)}, u32[]{:S(2)}, u32[]{:S(2)}) collective-permute-start(f32[8,2,8,128]{3,2,1,0:T(8,128)S(1)} %get-tuple-element.60), channel_id=1, source_target_pairs={{1,0},{2,1},{3,2},{4,3},{5,4},{6,5},{7,6},{8,7},{9,8},{10,9},{11,1... | collective-permute-start | bytes 196616 | tf_op jit(solution)/shard_map/ppermute | solution.py:544
  60.5 3.7 %collective-permute-start.19 = (f32[8,128]{1,0:T(8,128)S(1)}, f32[8,128]{1,0:T(8,128)S(1)}, u32[]{:S(2)}, u32[]{:S(2)}) collective-permute-start(f32[8,128]{1,0:T(8,128)S(1)} %get-tuple-element.61.refs_2_), channel_id=1, source_target_pairs={{32,0},{48,16},{64,32},{80,48},{96,64},{112,80},{128,96},{144,112}... | collective-permute-start | bytes 12296 | tf_op jit(solution)/shard_map/ppermute | solution.py:544
  60.6 3.6 %collective-permute-start.18 = (f32[8,128]{1,0:T(8,128)S(1)}, f32[8,128]{1,0:T(8,128)S(1)}, u32[]{:S(2)}, u32[]{:S(2)}) collective-permute-start(f32[8,128]{1,0:T(8,128)S(1)} %get-tuple-element.61.refs_2_), channel_id=1, source_target_pairs={{16,0},{32,16},{48,32},{64,48},{80,64},{96,80},{112,96},{128,112},... | collective-permute-start | bytes 12296 | tf_op jit(solution)/shard_map/ppermute | solution.py:544
  60.6 4.3 %collective-permute-start.17 = (f32[8,128]{1,0:T(8,128)S(1)}, f32[8,128]{1,0:T(8,128)S(1)}, u32[]{:S(2)}, u32[]{:S(2)}) collective-permute-start(f32[8,128]{1,0:T(8,128)S(1)} %get-tuple-element.61.refs_2_), channel_id=1, source_target_pairs={{0,16},{16,32},{32,48},{48,64},{64,80},{80,96},{96,112},{112,128},... | collective-permute-start | bytes 12296 | tf_op jit(solution)/shard_map/ppermute | solution.py:544
  61.1 4.8 %collective-permute-start.16 = (f32[8,128]{1,0:T(8,128)S(1)}, f32[8,128]{1,0:T(8,128)S(1)}, u32[]{:S(2)}, u32[]{:S(2)}) collective-permute-start(f32[8,128]{1,0:T(8,128)S(1)} %get-tuple-element.61.refs_2_), channel_id=1, source_target_pairs={{0,32},{16,48},{32,64},{48,80},{64,96},{80,112},{96,128},{112,144}... | collective-permute-start | bytes 12296 | tf_op jit(solution)/shard_map/ppermute | solution.py:544
  65.9 9.5 %collective-permute-start.23 = (f32[32,128]{1,0:T(8,128)S(1)}, f32[32,128]{1,0:T(8,128)S(1)}, u32[]{:S(2)}, u32[]{:S(2)}) collective-permute-start(f32[32,128]{1,0:T(8,128)S(1)} %shard_map.77.refs_2_), channel_id=1, source_target_pairs={{2,0},{3,1},{4,2},{5,3},{6,4},{7,5},{8,6},{9,7},{10,8},{11,9},{12,... | collective-permute-start | bytes 49160 | tf_op jit(solution)/shard_map/ppermute | solution.py:544
  73.4 3.7 %collective-permute-start.22 = (f32[32,128]{1,0:T(8,128)S(1)}, f32[32,128]{1,0:T(8,128)S(1)}, u32[]{:S(2)}, u32[]{:S(2)}) collective-permute-start(f32[32,128]{1,0:T(8,128)S(1)} %shard_map.77.refs_2_), channel_id=1, source_target_pairs={{1,0},{2,1},{3,2},{4,3},{5,4},{6,5},{7,6},{8,7},{9,8},{10,9},{11,1... | collective-permute-start | bytes 49160 | tf_op jit(solution)/shard_map/ppermute | solution.py:544
  73.4 3.7 %collective-permute-start.21 = (f32[32,128]{1,0:T(8,128)S(1)}, f32[32,128]{1,0:T(8,128)S(1)}, u32[]{:S(2)}, u32[]{:S(2)}) collective-permute-start(f32[32,128]{1,0:T(8,128)S(1)} %shard_map.77.refs_2_), channel_id=1, source_target_pairs={{0,1},{1,2},{2,3},{3,4},{4,5},{5,6},{6,7},{7,8},{8,9},{9,10},{10,1... | collective-permute-start | bytes 49160 | tf_op jit(solution)/shard_map/ppermute | solution.py:544
  75.5 7.4 %collective-permute-start.20 = (f32[32,128]{1,0:T(8,128)S(1)}, f32[32,128]{1,0:T(8,128)S(1)}, u32[]{:S(2)}, u32[]{:S(2)}) collective-permute-start(f32[32,128]{1,0:T(8,128)S(1)} %shard_map.77.refs_2_), channel_id=1, source_target_pairs={{0,2},{1,3},{2,4},{3,5},{4,6},{5,7},{6,8},{7,9},{8,10},{9,11},{10,... | collective-permute-start | bytes 49160 | tf_op jit(solution)/shard_map/ppermute | solution.py:544
  83.8 1.9 %collective-permute-start.25 = (f32[2,8,8,128]{3,2,1,0:T(8,128)S(1)}, f32[2,8,8,128]{3,2,1,0:T(8,128)S(1)}, u32[]{:S(2)}, u32[]{:S(2)}) collective-permute-start(f32[2,8,8,128]{3,2,1,0:T(8,128)S(1)} %get-tuple-element.65.low_ref.refs_0_.refs_12_), channel_id=1, source_target_pairs={{16,0},{32,16},{48,32},{64,48},{80,64},{96,80},{112,96},{128,112},... | collective-permute-start | bytes 196616 | tf_op jit(solution)/shard_map/ppermute | solution.py:544
  83.8 4.9 %collective-permute-start.24 = (f32[2,8,8,128]{3,2,1,0:T(8,128)S(1)}, f32[2,8,8,128]{3,2,1,0:T(8,128)S(1)}, u32[]{:S(2)}, u32[]{:S(2)}) collective-permute-start(f32[2,8,8,128]{3,2,1,0:T(8,128)S(1)} %get-tuple-element.66.high_ref.refs_1_.refs_13_), channel_id=1, source_target_pairs={{0,16},{16,32},{32,48},{48,64},{64,80},{80,96},{96,112},{112,128},... | collective-permute-start | bytes 196616 | tf_op jit(solution)/shard_map/ppermute | solution.py:544
  88.7 4.3 %collective-permute-start.26 = (f32[8,2,8,128]{3,2,1,0:T(8,128)S(1)}, f32[8,2,8,128]{3,2,1,0:T(8,128)S(1)}, u32[]{:S(2)}, u32[]{:S(2)}) collective-permute-start(f32[8,2,8,128]{3,2,1,0:T(8,128)S(1)} %get-tuple-element.67), channel_id=1, source_target_pairs={{0,1},{1,2},{2,3},{3,4},{4,5},{5,6},{6,7},{7,8},{8,9},{9,10},{10,1... | collective-permute-start | bytes 196616 | tf_op jit(solution)/shard_map/ppermute | solution.py:544
  88.8 4.3 %collective-permute-start.27 = (f32[8,2,8,128]{3,2,1,0:T(8,128)S(1)}, f32[8,2,8,128]{3,2,1,0:T(8,128)S(1)}, u32[]{:S(2)}, u32[]{:S(2)}) collective-permute-start(f32[8,2,8,128]{3,2,1,0:T(8,128)S(1)} %get-tuple-element.68), channel_id=1, source_target_pairs={{1,0},{2,1},{3,2},{4,3},{5,4},{6,5},{7,6},{8,7},{9,8},{10,9},{11,1... | collective-permute-start | bytes 196616 | tf_op jit(solution)/shard_map/ppermute | solution.py:544
  123.7 1.9 %collective-permute-start.29 = (f32[2,8,8,128]{3,2,1,0:T(8,128)S(1)}, f32[2,8,8,128]{3,2,1,0:T(8,128)S(1)}, u32[]{:S(2)}, u32[]{:S(2)}) collective-permute-start(f32[2,8,8,128]{3,2,1,0:T(8,128)S(1)} %get-tuple-element.74.low_ref.refs_0_.refs_12_.wlow_ref), channel_id=1, source_target_pairs={{16,0},{32,16},{48,32},{64,48},{80,64},{96,80},{112,96},{128,112},... | collective-permute-start | bytes 196616 | tf_op jit(solution)/shard_map/ppermute | solution.py:544
  123.7 4.9 %collective-permute-start.28 = (f32[2,8,8,128]{3,2,1,0:T(8,128)S(1)}, f32[2,8,8,128]{3,2,1,0:T(8,128)S(1)}, u32[]{:S(2)}, u32[]{:S(2)}) collective-permute-start(f32[2,8,8,128]{3,2,1,0:T(8,128)S(1)} %get-tuple-element.75.high_ref.refs_1_.refs_13_.whigh_ref), channel_id=1, source_target_pairs={{0,16},{16,32},{32,48},{48,64},{64,80},{80,96},{96,112},{112,128},... | collective-permute-start | bytes 196616 | tf_op jit(solution)/shard_map/ppermute | solution.py:544
  128.7 4.3 %collective-permute-start.30 = (f32[8,2,8,128]{3,2,1,0:T(8,128)S(1)}, f32[8,2,8,128]{3,2,1,0:T(8,128)S(1)}, u32[]{:S(2)}, u32[]{:S(2)}) collective-permute-start(f32[8,2,8,128]{3,2,1,0:T(8,128)S(1)} %get-tuple-element.76), channel_id=1, source_target_pairs={{0,1},{1,2},{2,3},{3,4},{4,5},{5,6},{6,7},{7,8},{8,9},{9,10},{10,1... | collective-permute-start | bytes 196616 | tf_op jit(solution)/shard_map/ppermute | solution.py:544
  129.8 4.3 %collective-permute-start.31 = (f32[8,2,8,128]{3,2,1,0:T(8,128)S(1)}, f32[8,2,8,128]{3,2,1,0:T(8,128)S(1)}, u32[]{:S(2)}, u32[]{:S(2)}) collective-permute-start(f32[8,2,8,128]{3,2,1,0:T(8,128)S(1)} %get-tuple-element.77), channel_id=1, source_target_pairs={{1,0},{2,1},{3,2},{4,3},{5,4},{6,5},{7,6},{8,7},{9,8},{10,9},{11,1... | collective-permute-start | bytes 196616 | tf_op jit(solution)/shard_map/ppermute | solution.py:544
  134.6 3.7 %collective-permute-start.35 = (f32[8,128]{1,0:T(8,128)S(1)}, f32[8,128]{1,0:T(8,128)S(1)}, u32[]{:S(2)}, u32[]{:S(2)}) collective-permute-start(f32[8,128]{1,0:T(8,128)S(1)} %get-tuple-element.78.refs_2_), channel_id=1, source_target_pairs={{32,0},{48,16},{64,32},{80,48},{96,64},{112,80},{128,96},{144,112}... | collective-permute-start | bytes 12296 | tf_op jit(solution)/shard_map/ppermute | solution.py:544
  134.7 3.6 %collective-permute-start.34 = (f32[8,128]{1,0:T(8,128)S(1)}, f32[8,128]{1,0:T(8,128)S(1)}, u32[]{:S(2)}, u32[]{:S(2)}) collective-permute-start(f32[8,128]{1,0:T(8,128)S(1)} %get-tuple-element.78.refs_2_), channel_id=1, source_target_pairs={{16,0},{32,16},{48,32},{64,48},{80,64},{96,80},{112,96},{128,112},... | collective-permute-start | bytes 12296 | tf_op jit(solution)/shard_map/ppermute | solution.py:544
  134.7 4.3 %collective-permute-start.33 = (f32[8,128]{1,0:T(8,128)S(1)}, f32[8,128]{1,0:T(8,128)S(1)}, u32[]{:S(2)}, u32[]{:S(2)}) collective-permute-start(f32[8,128]{1,0:T(8,128)S(1)} %get-tuple-element.78.refs_2_), channel_id=1, source_target_pairs={{0,16},{16,32},{32,48},{48,64},{64,80},{80,96},{96,112},{112,128},... | collective-permute-start | bytes 12296 | tf_op jit(solution)/shard_map/ppermute | solution.py:544
  135.2 4.8 %collective-permute-start.32 = (f32[8,128]{1,0:T(8,128)S(1)}, f32[8,128]{1,0:T(8,128)S(1)}, u32[]{:S(2)}, u32[]{:S(2)}) collective-permute-start(f32[8,128]{1,0:T(8,128)S(1)} %get-tuple-element.78.refs_2_), channel_id=1, source_target_pairs={{0,32},{16,48},{32,64},{48,80},{64,96},{80,112},{96,128},{112,144}... | collective-permute-start | bytes 12296 | tf_op jit(solution)/shard_map/ppermute | solution.py:544
  140.0 10.2 %collective-permute-start.39 = (f32[32,128]{1,0:T(8,128)S(1)}, f32[32,128]{1,0:T(8,128)S(1)}, u32[]{:S(2)}, u32[]{:S(2)}) collective-permute-start(f32[32,128]{1,0:T(8,128)S(1)} %shard_map.85.refs_2_), channel_id=1, source_target_pairs={{2,0},{3,1},{4,2},{5,3},{6,4},{7,5},{8,6},{9,7},{10,8},{11,9},{12,... | collective-permute-start | bytes 49160 | tf_op jit(solution)/shard_map/ppermute | solution.py:544
  148.2 3.7 %collective-permute-start.38 = (f32[32,128]{1,0:T(8,128)S(1)}, f32[32,128]{1,0:T(8,128)S(1)}, u32[]{:S(2)}, u32[]{:S(2)}) collective-permute-start(f32[32,128]{1,0:T(8,128)S(1)} %shard_map.85.refs_2_), channel_id=1, source_target_pairs={{1,0},{2,1},{3,2},{4,3},{5,4},{6,5},{7,6},{8,7},{9,8},{10,9},{11,1... | collective-permute-start | bytes 49160 | tf_op jit(solution)/shard_map/ppermute | solution.py:544
  148.2 3.7 %collective-permute-start.37 = (f32[32,128]{1,0:T(8,128)S(1)}, f32[32,128]{1,0:T(8,128)S(1)}, u32[]{:S(2)}, u32[]{:S(2)}) collective-permute-start(f32[32,128]{1,0:T(8,128)S(1)} %shard_map.85.refs_2_), channel_id=1, source_target_pairs={{0,1},{1,2},{2,3},{3,4},{4,5},{5,6},{6,7},{7,8},{8,9},{9,10},{10,1... | collective-permute-start | bytes 49160 | tf_op jit(solution)/shard_map/ppermute | solution.py:544
  150.2 7.4 %collective-permute-start.36 = (f32[32,128]{1,0:T(8,128)S(1)}, f32[32,128]{1,0:T(8,128)S(1)}, u32[]{:S(2)}, u32[]{:S(2)}) collective-permute-start(f32[32,128]{1,0:T(8,128)S(1)} %shard_map.85.refs_2_), channel_id=1, source_target_pairs={{0,2},{1,3},{2,4},{3,5},{4,6},{5,7},{6,8},{7,9},{8,10},{9,11},{10,... | collective-permute-start | bytes 49160 | tf_op jit(solution)/shard_map/ppermute | solution.py:544
